TPU v7x, 32 devices: a whole 2x2x4 slice. The times are simulated.
32 devices in a mesh: section: 4 (over y, x), dp: 8 (over z, core).
Axes of the slice: x: 2, y: 2, z: 4, core: 2. Of those that a mesh axis runs over, the one named last changes fastest.
Arguments:
- momentum: float32 [4, 4, 3584, 288], P('section', None, 'dp'), may hold values from -6 to 6
- gradient: bfloat16 [4, 4, 3584, 288], P('section', None, 'dp'), may hold values from -1300 to 1300
- assignment: int32 [4, 4], P('section'), may hold values from 0 to 7, as said below
Outputs:
- new_momentum: float32 [4, 4, 3584, 288], P('section', None, 'dp')
- update: bfloat16 [4, 4, 3584, 288], P('section', None, 'dp')
- slot_rms: float32 [4, 16], P('section', 'dp')
Inputs may be any that keep to these rules, and one draw needn't show every extreme that they name: `assignment`: within one section no owner holds more than 2 matrices, and some owner holds exactly 2.
All inputs are finite; a program needn't handle non-finite values.
Results may differ from a plain program's by a relative error of at most 0.015.
The roundings to bfloat16 on the way count: a program that leaves them out, or rounds other values in their place, can miss the bound.
Values may be sent and summed in bfloat16 or wider, within the bound.
No kernel may reach another device: no remote copies, remote signals or barrier semaphores. Data moves between devices by JAX's collectives and lax.ppermute only.
A program may use at most 64 MiB of HBM per device.

v0:
```python
import math

import jax
import jax.numpy as jnp
from jax import lax
from jax.sharding import PartitionSpec as P

D_IN = 3584
KV = 288
MAXOWN = 2
NS_STEPS = 5


momentum_decay = 0.95
clip_rms = 0.5
newton_coeffs = (3.4445, -4.775, 2.0315)


def newton(matrices):
    values = matrices.astype(jnp.float32)
    squares = jnp.sum(values * values, axis=(1, 2))
    current = (values / (jnp.sqrt(squares)[:, None, None] + 1e-07)).astype(jnp.bfloat16)
    for iteration in range(NS_STEPS):
        gram_mat = jnp.einsum(
            "kri,krj->kij", current, current, preferred_element_type=jnp.float32
        ).astype(jnp.bfloat16)
        square_mat = jnp.einsum(
            "kij,kjl->kil", gram_mat, gram_mat, preferred_element_type=jnp.float32
        )
        mixing = (
            newton_coeffs[1] * gram_mat.astype(jnp.float32) + newton_coeffs[2] * square_mat
        ).astype(jnp.bfloat16)
        following = newton_coeffs[0] * current.astype(jnp.float32) + jnp.einsum(
            "kri,kij->krj", current, mixing, preferred_element_type=jnp.float32
        )
        if iteration == NS_STEPS - 1:
            following = following * math.sqrt(D_IN)
        current = following.astype(jnp.bfloat16)
    return current


def solve_slots(gathered):
    return newton(gathered[0])[None]


def body(momentum, gradient, assignment):
    layers = momentum.shape[1]
    shard_rows = momentum.shape[2]
    kv_width = momentum.shape[3]
    owners = lax.axis_size("dp")
    grads = gradient.astype(jnp.float32)
    entries = lax.axis_size("section") * owners * layers * shard_rows * kv_width
    total_sq = lax.psum(jnp.sum(grads * grads), ("section", "dp"))
    factor = clip_rms / jnp.sqrt(total_sq / entries + 1e-06)
    fresh = momentum_decay * momentum + factor * grads
    nesterov = (factor * grads + momentum_decay * fresh).astype(jnp.bfloat16)[0]
    owner_of = assignment[0]
    positions = jnp.arange(layers, dtype=jnp.int32)
    shared = owner_of[:, None] == owner_of[None, :]
    earlier = positions[None, :] < positions[:, None]
    slot_index = jnp.sum((shared & earlier).astype(jnp.int32), axis=1)
    target = owner_of * MAXOWN + slot_index
    placing = (jnp.arange(owners * MAXOWN, dtype=jnp.int32)[:, None] == target[None, :]).astype(
        jnp.bfloat16
    )
    spread = (jnp.arange(owners, dtype=jnp.int32)[:, None] == 2 * positions[None, :]).astype(
        jnp.bfloat16
    )
    outgoing = jnp.einsum(
        "tl,lrc->trc", spread, nesterov, preferred_element_type=jnp.float32
    ).astype(jnp.bfloat16)
    outgoing = outgoing.reshape(owners, 1, shard_rows, kv_width)
    worked = solve_slots(lax.all_to_all(outgoing, "dp", split_axis=0, concat_axis=2, tiled=True))
    worked32 = worked.astype(jnp.float32)
    own_sum = jnp.sum(worked32 * worked32) / (D_IN * KV)
    my_row = lax.dynamic_slice_in_dim(spread, lax.axis_index("dp"), 1, 0)[0].astype(jnp.float32)
    layer_vec = lax.psum(my_row * own_sum, "dp")
    slot_sums = jnp.dot(placing.astype(jnp.float32), layer_vec, precision=lax.Precision.HIGHEST)
    mine = lax.dynamic_slice_in_dim(slot_sums, lax.axis_index("dp") * MAXOWN, MAXOWN)[None]
    returned = lax.all_to_all(worked, "dp", split_axis=2, concat_axis=0, tiled=True)
    returned = returned.reshape(owners, shard_rows, kv_width)
    update = jnp.einsum("tl,trc->lrc", spread, returned, preferred_element_type=jnp.float32).astype(
        jnp.bfloat16
    )
    return (fresh, update[None], mine)


def solution(mesh):
    in_specs = (P("section", None, "dp", None), P("section", None, "dp", None), P("section", None))
    out_specs = (P("section", None, "dp", None), P("section", None, "dp", None), P("section", "dp"))
    return jax.shard_map(body, mesh=mesh, in_specs=in_specs, out_specs=out_specs, check_vma=False)
```

profile of v0, /device:TPU:1, one launch (start us, length us, event | category | flops | bytes accessed | tf_op | source)
XLA Modules:
  0.0 268.9 jit_solution(12937370110417175016)
XLA Ops:
  0.6 2.5 fusion.11
  3.1 40.9 %psum.14 = f32[]{:T(128)} all-reduce(f32[]{:T(128)} %fusion.11), channel_id=1, replica_groups=mesh['section'=4,'dp'=8] {'section','dp'}, use_global_device_ids=true, to_apply=%region_1.0 | all-reduce | flops 1 | bytes 8 | tf_op jit(solution)/shard_map/psum | solution.py:53
  44.7 4.0 %fusion.31 = (bf16[4,448,288]{1,2,0:T(8,128)(2,1)S(1)}, f32[1,4,448,288]{2,3,1,0:T(8,128)}) fusion(bf16[1,4,448,288]{2,3,1,0:T(8,128)(2,1)} %param.4, f32[]{:T(128)S(6)} %div.33, f32[1,4,448,288]{2,3,1,0:T(8,128)} %param.3), kind=kLoop, calls=%fused_computation.48 | loop fusion | flops 3612672 | bytes 6193156 | tf_op jit(solution)/shard_map/squeeze | solution.py:56
  48.7 0.9 convert_bitcast_fusion
  49.5 0.8 copy.31
  50.4 58.3 %all_to_all.8 = bf16[8,1,448,288]{2,3,1,0:T(8,128)(2,1)S(1)} all-to-all(bf16[8,1,448,288]{2,3,1,0:T(8,128)(2,1)S(1)} %copy.31), channel_id=1, replica_groups=mesh['section'=4,'dp'=8] {'dp'}, dimensions={0} | all-to-all | bytes 4128768 | tf_op jit(solution)/shard_map/all_to_all | solution.py:73
  108.7 1.8 fusion.6
  111.2 0.4 fusion.7
  111.6 1.4 fusion.23
  113.0 1.3 copy.33
  114.3 3.6 %convert_element_type.180 = bf16[3584,288]{0,1:T(8,128)(2,1)} reshape(bf16[8,1,448,288]{2,0,3,1:T(8,128)(2,1)S(1)} %copy.33) | data formatting | bytes 4128768 | tf_op jit(solution)/shard_map/convert_element_type | solution.py:22
  117.9 3.8 %fusion.2 = bf16[3584,288]{0,1:T(8,128)(2,1)S(1)} fusion(bf16[3584,288]{0,1:T(8,128)(2,1)} %convert_element_type.180, bf16[288,288]{1,0:T(8,128)(2,1)S(1)} %fusion.23), kind=kOutput, calls=%fused_computation.9 | convolution fusion | flops 646861824 | bytes 4294656 | tf_op jit(solution)/shard_map/kri,kij->krj/dot_general | solution.py:33
  121.7 1.2 convolution_convert_fusion.4
  123.0 2.9 %fusion.3 = bf16[3584,288]{0,1:T(8,128)(2,1)} fusion(bf16[3584,288]{0,1:T(8,128)(2,1)S(1)} %fusion.2, bf16[288,288]{1,0:T(8,128)(2,1)S(1)} %convolution_convert_fusion.4), kind=kOutput, calls=%fused_computation.10 | convolution fusion | flops 646861824 | bytes 4294656 | tf_op jit(solution)/shard_map/kri,kij->krj/dot_general | solution.py:33
  125.9 0.0 copy-start.2
  125.9 3.6 %convolution_convert_fusion.3 = bf16[288,288]{1,0:T(8,128)(2,1)S(1)} fusion(bf16[3584,288]{0,1:T(8,128)(2,1)} %fusion.3), kind=kOutput, calls=%fused_computation.46 | convolution fusion | flops 594625536 | bytes 2230272 | tf_op jit(solution)/shard_map/kri,krj->kij/dot_general | solution.py:24
  129.5 0.0 copy-done.2
  129.5 2.9 %fusion.4 = bf16[3584,288]{0,1:T(8,128)(2,1)} fusion(bf16[3584,288]{0,1:T(8,128)(2,1)S(1)} %copy-done.2, bf16[288,288]{1,0:T(8,128)(2,1)S(1)} %convolution_convert_fusion.3), kind=kOutput, calls=%fused_computation.11 | convolution fusion | flops 646861824 | bytes 4294656 | tf_op jit(solution)/shard_map/kri,kij->krj/dot_general | solution.py:33
  132.4 3.4 %convolution_convert_fusion.2 = bf16[288,288]{1,0:T(8,128)(2,1)S(1)} fusion(bf16[3584,288]{0,1:T(8,128)(2,1)} %fusion.4), kind=kOutput, calls=%fused_computation.45 | convolution fusion | flops 594625536 | bytes 2230272 | tf_op jit(solution)/shard_map/kri,krj->kij/dot_general | solution.py:24
  135.8 3.8 %fusion.5 = bf16[3584,288]{0,1:T(8,128)(2,1)S(1)} fusion(bf16[3584,288]{0,1:T(8,128)(2,1)} %fusion.4, bf16[288,288]{1,0:T(8,128)(2,1)S(1)} %convolution_convert_fusion.2), kind=kOutput, calls=%fused_computation.12 | convolution fusion | flops 646861824 | bytes 4294656 | tf_op jit(solution)/shard_map/kri,kij->krj/dot_general | solution.py:33
  139.6 0.0 copy-start.1
  139.6 1.3 copy-done.1
  141.0 1.2 convolution_convert_fusion.1
  142.2 5.1 %multiply_reduce_fusion = (f32[]{:T(128)}, bf16[3584,288]{0,1:T(8,128)(2,1)S(1)}) fusion(bf16[3584,288]{0,1:T(8,128)(2,1)} %copy-done.1, bf16[288,288]{1,0:T(8,128)(2,1)S(1)} %convolution_convert_fusion.1), kind=kOutput, calls=%fused_computation.15 | convolution fusion | flops 650990592 | bytes 4294660 | tf_op jit(solution)/shard_map/kri,kij->krj/dot_general | solution.py:33
  147.3 10.6 %copy.34 = bf16[1,1,3584,288]{3,1,0,2:T(2,128)(2,1)} copy(bf16[1,1,3584,288]{2,3,1,0:T(8,128)(2,1)S(1)} %bitcast.78) | data formatting | bytes 4128768 | tf_op jit(solution)/shard_map/broadcast_in_dim | solution.py:43
  157.9 0.5 broadcast.119
  158.4 23.2 %reduce.5 = bf16[3584,288]{1,0:T(8,128)(2,1)S(1)} reduce(bf16[3584,1,1,288]{3,2,1,0:T(2,128)(2,1)} %bitcast.76, bf16[]{:T(256)} %broadcast.119), dimensions={1,2}, to_apply=%bitcast.50.reduce_sub_computation | reduce | bytes 4128770
  181.6 5.5 %reshape.208 = bf16[8,2,64512]{2,1,0:T(2,128)(2,1)} reshape(bf16[3584,288]{1,0:T(8,128)(2,1)S(1)} %reduce.5) | data formatting | bytes 4128768
  187.0 0.0 copy-start
  187.0 4.7 %all-to-all-start.1 = ((bf16[8,2,64512]{2,1,0:T(2,128)(2,1)}), bf16[8,2,64512]{2,1,0:T(2,128)(2,1)S(1)}, u32[]{:S(2)}, u32[]{:S(2)}) async-start(bf16[8,2,64512]{2,1,0:T(2,128)(2,1)} %reshape.208), calls=%async_computation.1 | async-start | bytes 4128768 | tf_op jit(solution)/shard_map/all_to_all | solution.py:80
  191.7 0.0 copy-done
  191.7 0.2 convert_reduce_fusion
  192.6 50.5 %psum.15 = f32[4]{0:T(128)S(1)} all-reduce(f32[4]{0:T(128)S(1)} %multiply_bitcast_fusion), channel_id=1, replica_groups=mesh['section'=4,'dp'=8] {'dp'}, use_global_device_ids=true, to_apply=%region_5.0 | all-reduce | flops 4 | bytes 32 | tf_op jit(solution)/shard_map/psum | solution.py:77
  243.0 0.1 convolution_bitcast_fusion
  243.2 0.6 dynamic-slice_bitcast_fusion
  243.8 0.0 all-to-all-done.1
  243.8 6.5 %reshape.209 = bf16[3584,1,1,288]{3,2,1,0:T(2,128)(2,1)} reshape(bf16[8,2,64512]{2,1,0:T(2,128)(2,1)S(1)} %all-to-all-done.1) | data formatting | bytes 4128768
  250.2 12.1 %copy.35 = bf16[1,1,3584,288]{2,3,1,0:T(8,128)(2,1)} copy(bf16[1,1,3584,288]{3,1,0,2:T(2,128)(2,1)} %bitcast.77) | data formatting | bytes 4128768 | tf_op jit(solution)/shard_map/all_to_all | solution.py:80
  262.4 4.2 %reshape.202 = bf16[8,448,288]{1,0,2:T(8,128)(2,1)S(1)} reshape(bf16[1,1,3584,288]{2,3,1,0:T(8,128)(2,1)} %copy.35) | data formatting | bytes 4128768 | tf_op jit(solution)/shard_map/reshape | solution.py:81
  266.6 1.1 fusion.14
  267.7 1.2 copy.37
  (4 shorter events, 0.0 us)
Async XLA Ops:
  125.9 3.6 %copy-start.2 = (bf16[3584,288]{0,1:T(8,128)(2,1)S(1)}, bf16[3584,288]{0,1:T(8,128)(2,1)}, u32[]{:S(2)}) copy-start(bf16[3584,288]{0,1:T(8,128)(2,1)} %fusion.3) | copy-start | bytes 6193156
  139.6 1.3 copy-start.1
  187.0 4.7 %copy-start = (s32[1,4]{1,0:T(1,128)S(1)}, s32[1,4]{1,0:T(1,128)}, u32[]{:S(2)}) copy-start(s32[1,4]{1,0:T(1,128)} %param.5) | copy-start | bytes 52
  187.0 56.7 %all-to-all-start.1 = ((bf16[8,2,64512]{2,1,0:T(2,128)(2,1)}), bf16[8,2,64512]{2,1,0:T(2,128)(2,1)S(1)}, u32[]{:S(2)}, u32[]{:S(2)}) async-start(bf16[8,2,64512]{2,1,0:T(2,128)(2,1)} %reshape.208), calls=%async_computation.1 | async-start | bytes 4128768 | tf_op jit(solution)/shard_map/all_to_all | solution.py:80
where the time goes:
time: 271 us; the launch traced here: 269 us
  blocking collectives  150 us (55%)
  local copies, waits for them, and re-layouts  48.2 us (18%)
  other arithmetic  32.1 us (12%)
  matrix products  31.5 us (12%)
  starting transfers between devices  4.67 us (2%)
  between operations  2.8 us (1%)
    all_to_all x1, blocking collectives, body(): lax.all_to_all(outgoing, 'dp', split_axis=0, concat_axis=2, tiled=True)  58.3 us
    psum x1, blocking collectives, body(): layer_vec = lax.psum(my_row * own_sum, 'dp')  50.5 us
    psum x1, blocking collectives, body(): total_sq = lax.psum(jnp.sum(grads * grads), ('section', 'dp'))  40.9 us
    unnamed x1, other arithmetic  23.2 us
    dot_general x5, matrix products, newton(): jnp.einsum('kri,kij->krj', current, mixing, preferred_element_type=jnp.fl...  18.5 us
    unnamed x10, local copies, waits for them, and re-layouts  15 us
    all_to_all x1, local copies, waits for them, and re-layouts, body(): lax.all_to_all(worked, 'dp', split_axis=2, concat_axis=0, tiled=True)  12.1 us
    dot_general x5, matrix products, newton(): jnp.einsum('kri,krj->kij', current, current, preferred_element_type=jnp.f...  10.9 us
  transfers between devices with their start and end apart: 1, of which 0 were waited for; matrix products, arithmetic and copies ran while one was open for 0% of the time, Pallas kernels for 0%

commit v1 on v0

v1 whole, which is shorter than its diff:
```python
import functools
import math

import jax
import jax.numpy as jnp
from jax import lax
from jax.experimental import pallas as pl
from jax.experimental.pallas import tpu as pltpu
from jax.sharding import PartitionSpec as P

MAXOWN = 2
NS_STEPS = 5
LANES = 128

momentum_decay = 0.95
clip_rms = 0.5
newton_coeffs = (3.4445, -4.775, 2.0315)

F32 = jnp.float32
BF16 = jnp.bfloat16


def whole(shape):
    return pl.BlockSpec(shape, lambda *_: (0,) * len(shape))


def total_of(values):
    return jnp.sum(jnp.sum(values, axis=0, keepdims=True), axis=1, keepdims=True)


def sums_kernel(grad_ref, mom_ref, out_ref):
    layer = pl.program_id(0)

    @pl.when(layer == 0)
    def _():
        out_ref[...] = jnp.zeros_like(out_ref)

    grads = grad_ref[0].astype(F32)
    moms = mom_ref[0]
    gg, gm, mm = total_of(grads * grads), total_of(grads * moms), total_of(moms * moms)
    lane = lax.broadcasted_iota(jnp.int32, (1, out_ref.shape[1]), 1)
    first = 1 + 3 * layer
    row = jnp.where((lane == 0) | (lane == first), gg, 0.0)
    row = row + jnp.where(lane == first + 1, gm, 0.0) + jnp.where(lane == first + 2, mm, 0.0)
    out_ref[...] += jnp.broadcast_to(row, out_ref.shape)


def block_rows(width):
    tail = width - 2 * LANES
    return 3 * LANES + 3 * tail


def start_kernel(
    entries, owners, scal_ref, sums_ref, grad_ref, mom_ref, start_ref, keep_ref, send_ref, fac_ref, pack
):
    layer = pl.program_id(0)
    core, section = scal_ref[1], scal_ref[2]
    sums = sums_ref[...]
    lane = lax.broadcasted_iota(jnp.int32, sums.shape, 1)
    row = lax.broadcasted_iota(jnp.int32, sums.shape, 0)
    mine = (row >= section * owners) & (row < (section + 1) * owners)
    total = total_of(jnp.where(lane == 0, sums, 0.0))
    first = 1 + 3 * layer
    gg = total_of(jnp.where(mine & (lane == first), sums, 0.0))
    gm = total_of(jnp.where(mine & (lane == first + 1), sums, 0.0))
    mm = total_of(jnp.where(mine & (lane == first + 2), sums, 0.0))
    factor = clip_rms / jnp.sqrt(total / entries + 1e-06)
    fac_ref[...] = jnp.broadcast_to(factor, fac_ref.shape)
    on_grad = factor * (1.0 + momentum_decay)
    on_mom = momentum_decay * momentum_decay
    guess = on_grad * on_grad * gg + 2.0 * (on_grad * on_mom) * gm + (on_mom * on_mom) * mm
    guess = jnp.maximum(guess, 0.0)
    scale = 1.0 / (jnp.sqrt(guess) + 1e-07)
    scaled = factor * grad_ref[0].astype(F32)
    fresh = momentum_decay * mom_ref[0] + scaled
    nesterov = (scaled + momentum_decay * fresh).astype(BF16).astype(F32)
    squares = total_of(nesterov * nesterov)
    start = (nesterov * scale).astype(BF16)
    start_ref[0] = start
    gram = lax.dot_general(start, start, (((1,), (1,)), ((), ())), preferred_element_type=F32)
    width = start.shape[0]
    tail = width - 2 * LANES
    a, b = LANES, 2 * LANES
    pack[0:a, :] = gram[0:a, 0:a]
    pack[a:b, :] = gram[0:a, a:b]
    pack[b : b + a, :] = gram[a:b, a:b]
    at = b + a
    pack[at : at + tail, :] = gram[b:, 0:a]
    pack[at + tail : at + 2 * tail, :] = gram[b:, a:b]
    spot = lax.broadcasted_iota(jnp.int32, (tail, LANES), 1)
    extra = jnp.where(spot == 64, squares, 0.0) + jnp.where(spot == 65, guess, 0.0)
    pack[at + 2 * tail :, :] = extra
    pack[at + 2 * tail :, 0:tail] = gram[b:, b:]
    half = pack.shape[0] // 2
    keep_ref[0] = pack[pl.ds(pl.multiple_of(core * half, 8), half), :]
    send_ref[0] = pack[pl.ds(pl.multiple_of((1 - core) * half, 8), half), :]


def split(value):
    high = value.astype(BF16)
    return high, (value - high.astype(F32)).astype(BF16)


def dot(left, right):
    return jnp.dot(left, right, preferred_element_type=F32)


def newton_kernel(owners, width, scal_ref, own_ref, other_ref, both_ref, mine_ref, pack):
    core = scal_ref[1]
    half = own_ref.shape[0]
    pack[pl.ds(pl.multiple_of(core * half, 8), half), :] = own_ref[...]
    pack[pl.ds(pl.multiple_of((1 - core) * half, 8), half), :] = other_ref[...]
    tail = width - 2 * LANES
    a, b = LANES, 2 * LANES
    at = b + a
    t00, t01, t11 = pack[0:a, :], pack[a:b, :], pack[b:at, :]
    t20, t21 = pack[at : at + tail, :], pack[at + tail : at + 2 * tail, :]
    last = pack[at + 2 * tail :, :]
    t22 = last[:, 0:tail]
    squares = last[0:1, 64:65]
    guess = last[0:1, 65:66] * (1.0 / owners)
    ratio = (jnp.sqrt(guess) + 1e-07) / (jnp.sqrt(squares) + 1e-07)
    gram = jnp.concatenate(
        [
            jnp.concatenate([t00, t01, t20.T], axis=1),
            jnp.concatenate([t01.T, t11, t21.T], axis=1),
            jnp.concatenate([t20, t21, t22], axis=1),
        ],
        axis=0,
    )
    gram = gram * (ratio * ratio)
    ca, cb, cc = newton_coeffs
    rows = lax.broadcasted_iota(jnp.int32, (width, width), 0)
    cols = lax.broadcasted_iota(jnp.int32, (width, width), 1)
    prod = None
    mean_sq = None
    for step in range(NS_STEPS):
        rounded = gram.astype(BF16)
        mix = (cb * rounded.astype(F32) + cc * dot(rounded, rounded)).astype(BF16)
        mix32 = mix.astype(F32)
        gram_hi, gram_lo = split(gram)
        if prod is None:
            prod = ratio * (jnp.where(rows == cols, ca, 0.0) + mix32)
            turned = ca * gram + dot(gram_hi, mix) + dot(gram_lo, mix)
        else:
            prod_hi, prod_lo = split(prod)
            turned = ca * gram + dot(gram_hi, mix) + dot(gram_lo, mix)
            prod = ca * prod + dot(prod_hi, mix) + dot(prod_lo, mix)
        if step < NS_STEPS - 1:
            turned_hi, turned_lo = split(turned)
            gram = ca * turned + dot(mix, turned_hi) + dot(mix, turned_lo)
        else:
            diagonal = jnp.where(rows == cols, turned, 0.0)
            mean_sq = total_of(ca * diagonal + mix32 * turned) * (1.0 / width)
    prod_hi, prod_lo = split(prod)
    mean_hi, mean_lo = split(jnp.broadcast_to(mean_sq, (width, LANES)))
    both_ref[0, :, 0:width] = prod_hi
    both_ref[1, :, 0:width] = prod_lo
    free = both_ref.shape[2] - width
    both_ref[0, :, width:] = mean_hi[:, 0:free]
    both_ref[1, :, width:] = mean_lo[:, 0:free]
    mine_ref[...] = both_ref[core]


def update_kernel(scale, width, chips, scal_ref, owner_ref, start_ref, high_ref, low_ref, out_ref, slot_ref):
    step = pl.program_id(0)
    layer = lax.rem(scal_ref[0] + step, chips)
    me = scal_ref[3]
    high, low = high_ref[0][:, 0:width], low_ref[0][:, 0:width]
    turn = (((0,), (0,)), ((), ()))
    start = start_ref[0]
    value = lax.dot_general(high, start, turn, preferred_element_type=F32)
    value = value + lax.dot_general(low, start, turn, preferred_element_type=F32)
    out_ref[0] = (value * scale).astype(BF16)
    mean_sq = high_ref[0][0:16, width:].astype(F32) + low_ref[0][0:16, width:].astype(F32)
    mean_sq = jnp.sum(jnp.where(
        (lax.broadcasted_iota(jnp.int32, mean_sq.shape, 0) == 0)
        & (lax.broadcasted_iota(jnp.int32, mean_sq.shape, 1) == 0), mean_sq, 0.0))

    @pl.when(step == 0)
    def _():
        for slot in range(MAXOWN):
            slot_ref[0, slot] = 0.0

    owner = owner_ref[0, layer]
    earlier = lax.fori_loop(
        0, layer, lambda i, n: n + jnp.where(owner_ref[0, i] == owner, 1, 0), jnp.int32(0)
    )
    for slot in range(MAXOWN):
        hit = (owner == me) & (earlier == slot)
        slot_ref[0, slot] = slot_ref[0, slot] + jnp.where(hit, mean_sq, 0.0)


def ring(size, by):
    return [(i, (i + 2 * by) % size) for i in range(size)]


def body(momentum, gradient, assignment):
    _, layers, rows, width = momentum.shape
    owners = lax.axis_size("dp")
    sections = lax.axis_size("section")
    chips = owners // 2
    assert chips == layers and width > 2 * LANES and width < 3 * LANES
    everyone = sections * owners
    entries = everyone * layers * rows * width
    mom = jnp.swapaxes(momentum[0], 1, 2)
    grad = jnp.swapaxes(gradient[0], 1, 2)
    place = lax.axis_index("dp")
    scal = jnp.stack([place // 2, place % 2, lax.axis_index("section"), place]).astype(jnp.int32)

    layer_spec = pl.BlockSpec((1, width, rows), lambda l, *_: (l, 0, 0))
    sum_width = -(-(1 + 3 * layers) // LANES) * LANES
    sums = pl.pallas_call(
        sums_kernel,
        grid=(layers,),
        in_specs=[layer_spec, layer_spec],
        out_specs=whole((everyone, sum_width)),
        out_shape=jax.ShapeDtypeStruct((everyone, sum_width), F32),
        name="sums",
    )(grad, mom)
    sums = lax.all_to_all(sums, ("section", "dp"), 0, 0, tiled=True)

    packed = block_rows(width)
    half = packed // 2
    rel_spec = pl.BlockSpec((1, half, LANES), lambda l, s: (lax.rem(l - s[0] + chips, chips), 0, 0))
    start, keep, send, factor = pl.pallas_call(
        functools.partial(start_kernel, entries, owners),
        grid_spec=pltpu.PrefetchScalarGridSpec(
            num_scalar_prefetch=1,
            grid=(layers,),
            in_specs=[whole((everyone, sum_width)), layer_spec, layer_spec],
            out_specs=[layer_spec, rel_spec, rel_spec, whole((8, LANES))],
            scratch_shapes=[pltpu.VMEM((packed, LANES), F32)],
        ),
        out_shape=[
            jax.ShapeDtypeStruct((layers, width, rows), BF16),
            jax.ShapeDtypeStruct((layers, half, LANES), F32),
            jax.ShapeDtypeStruct((layers, half, LANES), F32),
            jax.ShapeDtypeStruct((8, LANES), F32),
        ],
        name="start",
    )(scal, sums, grad, mom)
    fresh = momentum_decay * momentum + factor[0, 0] * gradient.astype(F32)

    swap = [(i, i ^ 1) for i in range(owners)]
    sums_up = keep + lax.ppermute(send, "dp", swap)
    far = chips // 2
    quarter = half // 2
    up, down = sums_up[far][:quarter], sums_up[far][quarter:]
    for step in range(1, far + 1):
        up = lax.ppermute(up, "dp", ring(owners, 1))
        down = lax.ppermute(down, "dp", ring(owners, -1))
        if step == 1 and far > 0:
            zero = jnp.zeros((quarter, LANES), F32)
            up = jnp.concatenate([up, zero], axis=0)
            down = jnp.concatenate([zero, down], axis=0)
        if step < far:
            up = up + sums_up[far - step]
            down = down + sums_up[chips - (far - step)]
    own = sums_up[0] + up + down
    other = lax.ppermute(own, "dp", swap)

    wide = 3 * LANES
    both, mine = pl.pallas_call(
        functools.partial(newton_kernel, owners, width),
        grid_spec=pltpu.PrefetchScalarGridSpec(
            num_scalar_prefetch=1,
            grid=(1,),
            in_specs=[whole((half, LANES)), whole((half, LANES))],
            out_specs=[whole((2, width, wide)), whole((width, wide))],
            scratch_shapes=[pltpu.VMEM((packed, LANES), F32)],
        ),
        out_shape=[
            jax.ShapeDtypeStruct((2, width, wide), BF16),
            jax.ShapeDtypeStruct((width, wide), BF16),
        ],
        name="newton",
    )(scal, own, other)

    cut = width // 2
    parts = {0: mine}
    from_down, from_up = mine, mine
    for step in range(1, far):
        from_down = lax.ppermute(from_down, "dp", ring(owners, 1))
        from_up = lax.ppermute(from_up, "dp", ring(owners, -1))
        parts[chips - step] = from_down
        parts[step] = from_up
    parts[far] = jnp.concatenate(
        [
            lax.ppermute(from_down[:cut], "dp", ring(owners, 1)),
            lax.ppermute(from_up[cut:], "dp", ring(owners, -1)),
        ],
        axis=0,
    )
    held = jnp.stack([parts[k] for k in range(1, chips)])
    swapped = lax.ppermute(held, "dp", swap)
    first = (scal[1] == 0)
    high = jnp.concatenate([both[0:1], jnp.where(first, held, swapped)], axis=0)
    low = jnp.concatenate([both[1:2], jnp.where(first, swapped, held)], axis=0)

    abs_spec = pl.BlockSpec((1, width, rows), lambda k, s, _: (lax.rem(k + s[0], chips), 0, 0))
    prod_spec = pl.BlockSpec((1, width, wide), lambda k, *_: (k, 0, 0))
    update, slots = pl.pallas_call(
        functools.partial(update_kernel, math.sqrt(owners * rows), width, chips),
        grid_spec=pltpu.PrefetchScalarGridSpec(
            num_scalar_prefetch=2,
            grid=(layers,),
            in_specs=[abs_spec, prod_spec, prod_spec],
            out_specs=[abs_spec, pl.BlockSpec((1, MAXOWN), lambda *_: (0, 0), memory_space=pltpu.SMEM)],
        ),
        out_shape=[
            jax.ShapeDtypeStruct((layers, width, rows), BF16),
            jax.ShapeDtypeStruct((1, MAXOWN), F32),
        ],
        name="update",
    )(scal, assignment, start, high, low)
    return (fresh, jnp.swapaxes(update, 1, 2)[None], slots)


def solution(mesh):
    in_specs = (P("section", None, "dp", None), P("section", None, "dp", None), P("section", None))
    out_specs = (P("section", None, "dp", None), P("section", None, "dp", None), P("section", "dp"))
    return jax.shard_map(body, mesh=mesh, in_specs=in_specs, out_specs=out_specs, check_vma=False)
```

time: 271 us -> 86.5 us (0.32)
  blocking collectives: 150 us -> 0 us
  local copies, waits for them, and re-layouts: 48.2 us -> 3.22 us
  matrix products: 31.5 us -> 0 us
  waiting for transfers between devices: 0.01 us -> 26.5 us
  other arithmetic: 32.1 us -> 8.21 us
  Pallas kernels: 0 us -> 23.4 us
  starting transfers between devices: 4.67 us -> 23.9 us
    psum x2 -> x0, blocking collectives: 91.3 us -> none  [the longest x1 50.5 us: body(): layer_vec = lax.psum(my_row * own_sum, 'dp')]
    all_to_all x1 -> x0, blocking collectives: 58.3 us -> none  [body(): lax.all_to_all(outgoing, 'dp', split_axis=0, concat_axis=2, tiled=True)]
    dot_general x13 -> x0, matrix products: 31.5 us -> none  [the longest x5 18.5 us: newton(): jnp.einsum('kri,kij->krj', current, mixing, preferred_element_type=jnp.fl...]
    pallas_call x0 -> x4, Pallas kernels: none -> 23.4 us  [the longest x1 8.42 us: body(): pl.pallas_call(functools.partial(newton_kernel, owners, width), grid_spec...]
    unnamed x1 -> x0, other arithmetic: 23.2 us -> none
    ppermute x0 -> x11, waiting for transfers between devices: none -> 20.4 us  [the longest x1 5.48 us: body(): from_down = lax.ppermute(from_down, 'dp', ring(owners, 1))]
    ppermute x0 -> x11, starting transfers between devices: none -> 16.8 us  [the longest x2 6.25 us: body(): down = lax.ppermute(down, 'dp', ring(owners, -1))]
    unnamed x10 -> x22, local copies, waits for them, and re-layouts: 15 us -> 1.95 us
  transfers between devices with their start and end apart: 1 -> 12, of which waited for: 0 -> 9; matrix products, arithmetic and copies ran while one was open for 0% -> 5% of each run, Pallas kernels for 0% -> 0%
where the time goes in v1:
time: 86.5 us; the launch traced here: 86 us
  waiting for transfers between devices  26.5 us (31%)
  starting transfers between devices  23.9 us (28%)
  Pallas kernels  23.4 us (27%)
  other arithmetic  8.21 us (9%)
  local copies, waits for them, and re-layouts  3.22 us (4%)
    pallas_call x1, Pallas kernels, body(): pl.pallas_call(functools.partial(newton_kernel, owners, width), grid_spec...  8.42 us
    all_to_all x1, starting transfers between devices, body(): sums = lax.all_to_all(sums, ('section', 'dp'), 0, 0, tiled=True)  7.08 us
    ppermute x2, starting transfers between devices, body(): down = lax.ppermute(down, 'dp', ring(owners, -1))  6.25 us
    all_to_all x1, waiting for transfers between devices, body(): sums = lax.all_to_all(sums, ('section', 'dp'), 0, 0, tiled=True)  6.1 us
    pallas_call x1, Pallas kernels, body(): pl.pallas_call(functools.partial(start_kernel, entries, owners), grid_spe...  5.84 us
    ppermute x1, waiting for transfers between devices, body(): from_down = lax.ppermute(from_down, 'dp', ring(owners, 1))  5.48 us
    pallas_call x1, Pallas kernels, body(): pl.pallas_call(functools.partial(update_kernel, math.sqrt(owners * rows),...  5.44 us
    ppermute x1, waiting for transfers between devices, body(): from_up = lax.ppermute(from_up, 'dp', ring(owners, -1))  4.44 us
  transfers between devices with their start and end apart: 12, of which 9 were waited for; matrix products, arithmetic and copies ran while one was open for 5% of the time, Pallas kernels for 0%

profile of v1, /device:TPU:1, one launch (start us, length us, event | category | flops | bytes accessed | tf_op | source)
XLA Modules:
  0.0 86.0 jit_solution(14706778953270271458)
XLA Ops:
  0.6 3.7 %sums.1 = f32[32,128]{1,0:T(8,128)} custom-call(bf16[4,288,448]{2,1,0:T(8,128)(2,1)} %bitcast.42, f32[4,288,448]{2,1,0:T(8,128)} %bitcast.40), custom_call_target="tpu_custom_call" | custom-call | tf_op jit(solution)/shard_map/sums/pallas_call | solution.py:213
  4.4 7.1 %all-to-all-start = ((f32[32,1,128]{2,1,0:T(1,128)}), f32[32,1,128]{2,1,0:T(1,128)S(1)}, u32[]{:S(2)}, u32[]{:S(2)}) async-start(f32[32,1,128]{2,1,0:T(1,128)} %bitcast.49), calls=%async_computation | async-start | bytes 32768 | tf_op jit(solution)/shard_map/all_to_all | solution.py:221
  11.5 0.6 pad_add_fusion.scal_ref
  12.1 6.1 %all-to-all-done = f32[32,1,128]{2,1,0:T(1,128)S(1)} async-done(((f32[32,1,128]{2,1,0:T(1,128)}), f32[32,1,128]{2,1,0:T(1,128)S(1)}, u32[]{:S(2)}, u32[]{:S(2)}) %all-to-all-start) | async-done | bytes 16416 | tf_op jit(solution)/shard_map/all_to_all | solution.py:221
  18.2 0.6 copy-done.10
  18.8 5.8 %start.1 = (bf16[4,288,448]{2,1,0:T(8,128)(2,1)}, f32[4,240,128]{2,1,0:T(8,128)}, f32[4,240,128]{2,1,0:T(8,128)}, f32[8,128]{1,0:T(8,128)}) custom-call(s32[4]{0:T(128)} %pad_add_fusion.scal_ref, f32[32,128]{1,0:T(8,128)} %bitcast.48, bf16[4,288,448]{2,1,0:T(8,128)(2,1)} %bitcast.43, f32[4,288,448]{2,1,0:T(8,128)} %bitcast.41), custom_call_target="tpu_custom_call" | custom-call | tf_op jit(solution)/shard_map/start/pallas_call | solution.py:226
  24.6 0.6 collective-permute-start
  25.3 1.7 %collective-permute-done = f32[4,240,128]{2,1,0:T(8,128)S(1)} collective-permute-done((f32[4,240,128]{2,1,0:T(8,128)}, f32[4,240,128]{2,1,0:T(8,128)S(1)}, u32[]{:S(2)}, u32[]{:S(2)}) %collective-permute-start) | collective-permute-done | bytes 491552 | tf_op jit(solution)/shard_map/ppermute | solution.py:246
  27.0 1.3 %add.29 = f32[4,240,128]{2,1,0:T(8,128)S(1)} add(f32[4,240,128]{2,1,0:T(8,128)} %get-tuple-element.13, f32[4,240,128]{2,1,0:T(8,128)S(1)} %collective-permute-done) | non-fusion elementwise | flops 122880 | bytes 1474560 | tf_op jit(solution)/shard_map/add | solution.py:246
  28.2 0.3 collective-permute-start.1
  28.5 3.0 %collective-permute-start.3 = (f32[120,128]{1,0:T(8,128)S(1)}, f32[120,128]{1,0:T(8,128)S(1)}, u32[]{:S(2)}, u32[]{:S(2)}) collective-permute-start(f32[120,128]{1,0:T(8,128)S(1)} %get-tuple-element.24), channel_id=1, source_target_pairs={{0,6},{1,7},{2,0},{3,1},{4,2},{5,3},{6,4},{7,5},{8,14},{9,15},{10,... | collective-permute-start | bytes 184328 | tf_op jit(solution)/shard_map/ppermute | solution.py:252
  31.5 1.7 %collective-permute-done.1 = f32[120,128]{1,0:T(8,128)S(1)} collective-permute-done((f32[120,128]{1,0:T(8,128)S(1)}, f32[120,128]{1,0:T(8,128)S(1)}, u32[]{:S(2)}, u32[]{:S(2)}) %collective-permute-start.1) | collective-permute-done | bytes 61472 | tf_op jit(solution)/shard_map/ppermute | solution.py:251
  33.3 0.0 collective-permute-done.3
  33.3 0.1 collective-permute-start.2
  33.4 3.3 %collective-permute-start.4 = (f32[240,128]{1,0:T(8,128)S(1)}, f32[240,128]{1,0:T(8,128)S(1)}, u32[]{:S(2)}, u32[]{:S(2)}) collective-permute-start(f32[240,128]{1,0:T(8,128)S(1)} %get-tuple-element.22), channel_id=1, source_target_pairs={{0,6},{1,7},{2,0},{3,1},{4,2},{5,3},{6,4},{7,5},{8,14},{9,15},{10,... | collective-permute-start | bytes 368648 | tf_op jit(solution)/shard_map/ppermute | solution.py:252
  36.6 2.4 %collective-permute-done.2 = f32[240,128]{1,0:T(8,128)S(1)} collective-permute-done((f32[240,128]{1,0:T(8,128)S(1)}, f32[240,128]{1,0:T(8,128)S(1)}, u32[]{:S(2)}, u32[]{:S(2)}) %collective-permute-start.2) | collective-permute-done | bytes 122912 | tf_op jit(solution)/shard_map/ppermute | solution.py:251
  39.0 0.0 collective-permute-done.4
  39.0 0.0 copy-start.8
  39.0 0.6 copy-done.8
  39.7 3.3 %collective-permute-start.5 = (f32[240,128]{1,0:T(8,128)S(1)}, f32[240,128]{1,0:T(8,128)}, u32[]{:S(2)}, u32[]{:S(2)}) collective-permute-start(f32[240,128]{1,0:T(8,128)S(1)} %fusion.3.own_ref), channel_id=1, source_target_pairs={{0,1},{1,0},{2,3},{3,2},{4,5},{5,4},{6,7},{7,6},{8,9},{9,8},{10,11... | collective-permute-start | bytes 368648 | tf_op jit(solution)/shard_map/ppermute | solution.py:261
  43.0 1.1 %collective-permute-done.5.other_ref = f32[240,128]{1,0:T(8,128)} collective-permute-done((f32[240,128]{1,0:T(8,128)S(1)}, f32[240,128]{1,0:T(8,128)}, u32[]{:S(2)}, u32[]{:S(2)}) %collective-permute-start.5) | collective-permute-done | bytes 122912 | tf_op jit(solution)/shard_map/ppermute | solution.py:261
  44.1 8.4 %newton.1 = (bf16[2,288,384]{2,1,0:T(8,128)(2,1)}, bf16[288,384]{1,0:T(8,128)(2,1)}) custom-call(s32[4]{0:T(128)} %pad_add_fusion.scal_ref, f32[240,128]{1,0:T(8,128)} %copy-done.8, f32[240,128]{1,0:T(8,128)} %collective-permute-done.5.other_ref), custom_call_target="tpu_custom_call" | custom-call | tf_op jit(solution)/shard_map/newton/pallas_call | solution.py:264
  52.5 1.5 %collective-permute-start.7 = (bf16[288,384]{1,0:T(8,128)(2,1)}, bf16[288,384]{1,0:T(8,128)(2,1)S(1)}, u32[]{:S(2)}, u32[]{:S(2)}) collective-permute-start(bf16[288,384]{1,0:T(8,128)(2,1)} %get-tuple-element.16), channel_id=1, source_target_pairs={{0,2},{1,3},{2,4},{3,5},{4,6},{5,7},{6,0},{7,1},{8,10},{9,11},{10,... | collective-permute-start | bytes 663560 | tf_op jit(solution)/shard_map/ppermute | solution.py:284
  54.0 1.9 %collective-permute-start.6 = (bf16[288,384]{1,0:T(8,128)(2,1)}, bf16[288,384]{1,0:T(8,128)(2,1)S(1)}, u32[]{:S(2)}, u32[]{:S(2)}) collective-permute-start(bf16[288,384]{1,0:T(8,128)(2,1)} %get-tuple-element.16), channel_id=1, source_target_pairs={{0,6},{1,7},{2,0},{3,1},{4,2},{5,3},{6,4},{7,5},{8,14},{9,15},{10,... | collective-permute-start | bytes 663560 | tf_op jit(solution)/shard_map/ppermute | solution.py:285
  55.9 5.5 %collective-permute-done.7 = bf16[288,384]{1,0:T(8,128)(2,1)S(1)} collective-permute-done((bf16[288,384]{1,0:T(8,128)(2,1)}, bf16[288,384]{1,0:T(8,128)(2,1)S(1)}, u32[]{:S(2)}, u32[]{:S(2)}) %collective-permute-start.7) | collective-permute-done | bytes 221216 | tf_op jit(solution)/shard_map/ppermute | solution.py:284
  61.4 0.1 collective-permute-start.8
  61.4 4.4 %collective-permute-done.6 = bf16[288,384]{1,0:T(8,128)(2,1)S(1)} collective-permute-done((bf16[288,384]{1,0:T(8,128)(2,1)}, bf16[288,384]{1,0:T(8,128)(2,1)S(1)}, u32[]{:S(2)}, u32[]{:S(2)}) %collective-permute-start.6) | collective-permute-done | bytes 221216 | tf_op jit(solution)/shard_map/ppermute | solution.py:285
  65.9 1.6 %collective-permute-start.9 = (bf16[144,384]{1,0:T(8,128)(2,1)S(1)}, bf16[144,384]{1,0:T(8,128)(2,1)S(1)}, u32[]{:S(2)}, u32[]{:S(2)}) collective-permute-start(bf16[144,384]{1,0:T(8,128)(2,1)S(1)} %slice.58), channel_id=1, source_target_pairs={{0,6},{1,7},{2,0},{3,1},{4,2},{5,3},{6,4},{7,5},{8,14},{9,15},{10,... | collective-permute-start | bytes 331784 | tf_op jit(solution)/shard_map/ppermute | solution.py:291
  67.5 0.3 collective-permute-done.8
  67.7 3.3 %collective-permute-done.9 = bf16[144,384]{1,0:T(8,128)(2,1)S(1)} collective-permute-done((bf16[144,384]{1,0:T(8,128)(2,1)S(1)}, bf16[144,384]{1,0:T(8,128)(2,1)S(1)}, u32[]{:S(2)}, u32[]{:S(2)}) %collective-permute-start.9) | collective-permute-done | bytes 110624 | tf_op jit(solution)/shard_map/ppermute | solution.py:291
  71.1 0.0 copy-start.2
  71.1 0.7 copy-done.2
  71.8 0.9 %pad_maximum_fusion.2 = bf16[3,288,384]{2,1,0:T(8,128)(2,1)} fusion(bf16[1,288,384]{2,1,0:T(8,128)(2,1)S(1)} %bitcast.44, bf16[1,288,384]{2,1,0:T(8,128)(2,1)S(1)} %maximum_bitcast_fusion, bf16[1,288,384]{2,1,0:T(8,128)(2,1)S(1)} %bitcast.46), kind=kLoop, calls=%fused_computation.3 | loop fusion | flops 663552 | bytes 1327104 | tf_op jit(solution)/shard_map/stack | solution.py:295
  72.7 0.0 copy-done.4
  72.7 0.0 copy-done.6
  72.7 1.2 %collective-permute-start.10 = (bf16[3,288,384]{2,1,0:T(8,128)(2,1)}, bf16[3,288,384]{2,1,0:T(8,128)(2,1)}, u32[]{:S(2)}, u32[]{:S(2)}) collective-permute-start(bf16[3,288,384]{2,1,0:T(8,128)(2,1)} %pad_maximum_fusion.2), channel_id=1, source_target_pairs={{0,1},{1,0},{2,3},{3,2},{4,5},{5,4},{6,7},{7,6},{8,9},{9,8},{10,11... | collective-permute-start | bytes 1990664 | tf_op jit(solution)/shard_map/ppermute | solution.py:296
  73.9 1.2 %slice.40 = f32[1,1]{1,0:T(1,128)} slice(f32[8,128]{1,0:T(8,128)} %get-tuple-element.11), slice={[0:1], [0:1]} | slice | bytes 8 | tf_op jit(solution)/shard_map/slice | solution.py:243
  75.1 0.0 copy-done
  75.1 0.0 copy-done.1
  75.1 0.0 copy-start.5
  75.2 0.0 copy-start.7
  75.2 2.6 %multiply_add_fusion = f32[1,4,448,288]{2,3,1,0:T(8,128)} fusion(bf16[1,4,448,288]{2,3,1,0:T(8,128)(2,1)S(1)} %copy-done.1, f32[1,4,448,288]{2,3,1,0:T(8,128)S(1)} %copy-done, f32[]{:T(128)} %bitcast.11), kind=kLoop, calls=%fused_computation | loop fusion | flops 2064384 | bytes 5160964 | tf_op jit(solution)/shard_map/add | solution.py:243
  77.8 0.0 copy-done.9
  77.9 0.0 collective-permute-done.10
  77.9 0.0 copy-done.3
  77.9 1.3 %broadcast_select_fusion = (bf16[3,288,384]{2,1,0:T(8,128)(2,1)S(1)}, bf16[3,288,384]{2,1,0:T(8,128)(2,1)S(1)}) fusion(bf16[3,288,384]{2,1,0:T(8,128)(2,1)} %collective-permute-done.10, pred[]{:T(512)S(6)} %eq.5, bf16[1,288,384]{2,1,0:T(8,128)(2,1)S(1)} %bitcast.45, bf16[1,288,384]{2,1,0:T(8,128)(2,1)S(1)} %copy-done.3, bf16[1,288,384]{2,1,0:T(8,128)(2,1)S(1)} %bitcast.47), kind=kLoop, calls=%fused_computation.4 | loop fusion | flops 1327104 | bytes 2654209 | tf_op jit(solution)/shard_map/jit(_where)/select_n | solution.py:299
  79.2 1.4 %pad_maximum_fusion = (bf16[4,288,384]{2,1,0:T(8,128)(2,1)}, bf16[4,288,384]{2,1,0:T(8,128)(2,1)}) fusion(bf16[3,288,384]{2,1,0:T(8,128)(2,1)S(1)} %get-tuple-element.20, bf16[1,288,384]{2,1,0:T(8,128)(2,1)S(1)} %get-tuple-element.26, bf16[3,288,384]{2,1,0:T(8,128)(2,1)S(1)} %get-tuple-element.19, bf16[1,288,384]{2,1,0:T(8,128)(2,1)S(1)} %get-tuple-element.25), kind=kLoop, calls=%fused_computation.1 | loop fusion | flops 884736 | bytes 3538944 | tf_op jit(solution)/shard_map/concatenate | solution.py:298
  80.6 5.4 %update.1 = (bf16[4,288,448]{2,1,0:T(8,128)(2,1)}, f32[1,2]{1,0:T(1,128)}) custom-call(s32[4]{0:T(128)} %pad_add_fusion.scal_ref, s32[1,4]{1,0:T(1,128)} %owner_ref.1, bf16[4,288,448]{2,1,0:T(8,128)(2,1)} %get-tuple-element.12.start_ref, bf16[4,288,384]{2,1,0:T(8,128)(2,1)} %get-tuple-element.27.high_ref, bf16[4,288,384]{2,1,0:T(8,128)(2,1)} %get-tuple-element.28.low_ref), custom_call_target="tpu_custom_call" | custom-call | tf_op jit(solution)/shard_map/update/pallas_call | solution.py:303
  (16 shorter events, 0.2 us)
Async XLA Ops:
  4.4 13.8 %all-to-all-start = ((f32[32,1,128]{2,1,0:T(1,128)}), f32[32,1,128]{2,1,0:T(1,128)S(1)}, u32[]{:S(2)}, u32[]{:S(2)}) async-start(f32[32,1,128]{2,1,0:T(1,128)} %bitcast.49), calls=%async_computation | async-start | bytes 32768 | tf_op jit(solution)/shard_map/all_to_all | solution.py:221
  18.2 0.6 copy-start.10
  24.6 2.3 %collective-permute-start = (f32[4,240,128]{2,1,0:T(8,128)}, f32[4,240,128]{2,1,0:T(8,128)S(1)}, u32[]{:S(2)}, u32[]{:S(2)}) collective-permute-start(f32[4,240,128]{2,1,0:T(8,128)} %get-tuple-element.14), channel_id=1, source_target_pairs={{0,1},{1,0},{2,3},{3,2},{4,5},{5,4},{6,7},{7,6},{8,9},{9,8},{10,11... | collective-permute-start | bytes 1474568 | tf_op jit(solution)/shard_map/ppermute | solution.py:246
  27.0 48.2 %copy-start = (f32[1,4,448,288]{2,3,1,0:T(8,128)S(1)}, f32[1,4,448,288]{2,3,1,0:T(8,128)}, u32[]{:S(2)}) copy-start(f32[1,4,448,288]{2,3,1,0:T(8,128)} %param.3) | copy-start | bytes 6193156
  27.0 48.2 %copy-start.1 = (bf16[1,4,448,288]{2,3,1,0:T(8,128)(2,1)S(1)}, bf16[1,4,448,288]{2,3,1,0:T(8,128)(2,1)}, u32[]{:S(2)}) copy-start(bf16[1,4,448,288]{2,3,1,0:T(8,128)(2,1)} %param.4) | copy-start | bytes 3096580
  28.2 5.0 %collective-permute-start.1 = (f32[120,128]{1,0:T(8,128)S(1)}, f32[120,128]{1,0:T(8,128)S(1)}, u32[]{:S(2)}, u32[]{:S(2)}) collective-permute-start(f32[120,128]{1,0:T(8,128)S(1)} %get-tuple-element.23), channel_id=1, source_target_pairs={{0,2},{1,3},{2,4},{3,5},{4,6},{5,7},{6,0},{7,1},{8,10},{9,11},{10,... | collective-permute-start | bytes 184328 | tf_op jit(solution)/shard_map/ppermute | solution.py:251
  28.5 4.7 %collective-permute-start.3 = (f32[120,128]{1,0:T(8,128)S(1)}, f32[120,128]{1,0:T(8,128)S(1)}, u32[]{:S(2)}, u32[]{:S(2)}) collective-permute-start(f32[120,128]{1,0:T(8,128)S(1)} %get-tuple-element.24), channel_id=1, source_target_pairs={{0,6},{1,7},{2,0},{3,1},{4,2},{5,3},{6,4},{7,5},{8,14},{9,15},{10,... | collective-permute-start | bytes 184328 | tf_op jit(solution)/shard_map/ppermute | solution.py:252
  33.3 5.7 %collective-permute-start.2 = (f32[240,128]{1,0:T(8,128)S(1)}, f32[240,128]{1,0:T(8,128)S(1)}, u32[]{:S(2)}, u32[]{:S(2)}) collective-permute-start(f32[240,128]{1,0:T(8,128)S(1)} %get-tuple-element.21), channel_id=1, source_target_pairs={{0,2},{1,3},{2,4},{3,5},{4,6},{5,7},{6,0},{7,1},{8,10},{9,11},{10,... | collective-permute-start | bytes 368648 | tf_op jit(solution)/shard_map/ppermute | solution.py:251
  33.4 5.6 %collective-permute-start.4 = (f32[240,128]{1,0:T(8,128)S(1)}, f32[240,128]{1,0:T(8,128)S(1)}, u32[]{:S(2)}, u32[]{:S(2)}) collective-permute-start(f32[240,128]{1,0:T(8,128)S(1)} %get-tuple-element.22), channel_id=1, source_target_pairs={{0,6},{1,7},{2,0},{3,1},{4,2},{5,3},{6,4},{7,5},{8,14},{9,15},{10,... | collective-permute-start | bytes 368648 | tf_op jit(solution)/shard_map/ppermute | solution.py:252
  39.0 0.7 copy-start.8
  39.7 4.5 %collective-permute-start.5 = (f32[240,128]{1,0:T(8,128)S(1)}, f32[240,128]{1,0:T(8,128)}, u32[]{:S(2)}, u32[]{:S(2)}) collective-permute-start(f32[240,128]{1,0:T(8,128)S(1)} %fusion.3.own_ref), channel_id=1, source_target_pairs={{0,1},{1,0},{2,3},{3,2},{4,5},{5,4},{6,7},{7,6},{8,9},{9,8},{10,11... | collective-permute-start | bytes 368648 | tf_op jit(solution)/shard_map/ppermute | solution.py:261
  52.5 8.8 %collective-permute-start.7 = (bf16[288,384]{1,0:T(8,128)(2,1)}, bf16[288,384]{1,0:T(8,128)(2,1)S(1)}, u32[]{:S(2)}, u32[]{:S(2)}) collective-permute-start(bf16[288,384]{1,0:T(8,128)(2,1)} %get-tuple-element.16), channel_id=1, source_target_pairs={{0,2},{1,3},{2,4},{3,5},{4,6},{5,7},{6,0},{7,1},{8,10},{9,11},{10,... | collective-permute-start | bytes 663560 | tf_op jit(solution)/shard_map/ppermute | solution.py:284
  54.0 11.9 %collective-permute-start.6 = (bf16[288,384]{1,0:T(8,128)(2,1)}, bf16[288,384]{1,0:T(8,128)(2,1)S(1)}, u32[]{:S(2)}, u32[]{:S(2)}) collective-permute-start(bf16[288,384]{1,0:T(8,128)(2,1)} %get-tuple-element.16), channel_id=1, source_target_pairs={{0,6},{1,7},{2,0},{3,1},{4,2},{5,3},{6,4},{7,5},{8,14},{9,15},{10,... | collective-permute-start | bytes 663560 | tf_op jit(solution)/shard_map/ppermute | solution.py:285
  61.4 11.4 %copy-start.4 = (bf16[288,384]{1,0:T(8,128)(2,1)}, bf16[288,384]{1,0:T(8,128)(2,1)S(1)}, u32[]{:S(2)}) copy-start(bf16[288,384]{1,0:T(8,128)(2,1)S(1)} %collective-permute-done.7) | copy-start | bytes 663556
  61.4 6.4 %collective-permute-start.8 = (bf16[144,384]{1,0:T(8,128)(2,1)S(1)}, bf16[144,384]{1,0:T(8,128)(2,1)S(1)}, u32[]{:S(2)}, u32[]{:S(2)}) collective-permute-start(bf16[144,384]{1,0:T(8,128)(2,1)S(1)} %slice.57), channel_id=1, source_target_pairs={{0,2},{1,3},{2,4},{3,5},{4,6},{5,7},{6,0},{7,1},{8,10},{9,11},{10,... | collective-permute-start | bytes 331784 | tf_op jit(solution)/shard_map/ppermute | solution.py:290
  65.9 6.9 %copy-start.6 = (bf16[288,384]{1,0:T(8,128)(2,1)}, bf16[288,384]{1,0:T(8,128)(2,1)S(1)}, u32[]{:S(2)}) copy-start(bf16[288,384]{1,0:T(8,128)(2,1)S(1)} %collective-permute-done.6) | copy-start | bytes 663556
  65.9 5.2 %collective-permute-start.9 = (bf16[144,384]{1,0:T(8,128)(2,1)S(1)}, bf16[144,384]{1,0:T(8,128)(2,1)S(1)}, u32[]{:S(2)}, u32[]{:S(2)}) collective-permute-start(bf16[144,384]{1,0:T(8,128)(2,1)S(1)} %slice.58), channel_id=1, source_target_pairs={{0,6},{1,7},{2,0},{3,1},{4,2},{5,3},{6,4},{7,5},{8,14},{9,15},{10,... | collective-permute-start | bytes 331784 | tf_op jit(solution)/shard_map/ppermute | solution.py:291
  71.1 0.7 copy-start.2
  72.7 5.1 %collective-permute-start.10 = (bf16[3,288,384]{2,1,0:T(8,128)(2,1)}, bf16[3,288,384]{2,1,0:T(8,128)(2,1)}, u32[]{:S(2)}, u32[]{:S(2)}) collective-permute-start(bf16[3,288,384]{2,1,0:T(8,128)(2,1)} %pad_maximum_fusion.2), channel_id=1, source_target_pairs={{0,1},{1,0},{2,3},{3,2},{4,5},{5,4},{6,7},{7,6},{8,9},{9,8},{10,11... | collective-permute-start | bytes 1990664 | tf_op jit(solution)/shard_map/ppermute | solution.py:296
  75.1 2.7 %copy-start.9 = (bf16[2,288,384]{2,1,0:T(8,128)(2,1)S(1)}, bf16[2,288,384]{2,1,0:T(8,128)(2,1)}, u32[]{:S(2)}) copy-start(bf16[2,288,384]{2,1,0:T(8,128)(2,1)} %get-tuple-element.15) | copy-start | bytes 1327108
  75.1 2.7 %copy-start.3 = (bf16[1,288,384]{2,1,0:T(8,128)(2,1)S(1)}, bf16[1,288,384]{2,1,0:T(8,128)(2,1)}, u32[]{:S(2)}) copy-start(bf16[1,288,384]{2,1,0:T(8,128)(2,1)} %copy-done.2) | copy-start | bytes 663556
  75.1 2.7 %copy-start.5 = (bf16[288,384]{1,0:T(8,128)(2,1)S(1)}, bf16[288,384]{1,0:T(8,128)(2,1)}, u32[]{:S(2)}) copy-start(bf16[288,384]{1,0:T(8,128)(2,1)} %copy-done.4) | copy-start | bytes 663556
  75.2 2.7 %copy-start.7 = (bf16[288,384]{1,0:T(8,128)(2,1)S(1)}, bf16[288,384]{1,0:T(8,128)(2,1)}, u32[]{:S(2)}) copy-start(bf16[288,384]{1,0:T(8,128)(2,1)} %copy-done.6) | copy-start | bytes 663556

commit v2 on v0

v2 whole, which is shorter than its diff:
```python
import functools
import math

import jax
import jax.numpy as jnp
from jax import lax
from jax.experimental import pallas as pl
from jax.experimental.pallas import tpu as pltpu
from jax.sharding import PartitionSpec as P


MAXOWN = 2
NS_STEPS = 5
LANES = 128

momentum_decay = 0.95
clip_rms = 0.5
newton_coeffs = (3.4445, -4.775, 2.0315)

F32 = jnp.float32
BF16 = jnp.bfloat16


VMEM_BYTES = 12 * 2**20


def params():
    return pltpu.CompilerParams(vmem_limit_bytes=VMEM_BYTES)


def cost(flops, bytes_accessed):
    return pl.CostEstimate(flops=flops, bytes_accessed=bytes_accessed, transcendentals=0)


def over(count, visit):
    if count <= 8:
        for i in range(count):
            visit(i)
    else:
        pl.loop(0, count)(visit)


def whole(shape):
    return pl.BlockSpec(shape, lambda *_: (0,) * len(shape))


def total_of(values):
    return jnp.sum(jnp.sum(values, axis=0, keepdims=True), axis=1, keepdims=True)


def sums_kernel(layers, grad_in, mom_in, out_ref, grad_ref, mom_ref, acc, sems):
    def copies(layer):
        return (
            pltpu.make_async_copy(grad_in.at[layer], grad_ref.at[layer], sems.at[layer, 0]),
            pltpu.make_async_copy(mom_in.at[layer], mom_ref.at[layer], sems.at[layer, 1]),
        )

    def begin(layer):
        for copy in copies(layer):
            copy.start()

    def visit(layer):
        for copy in copies(layer):
            copy.wait()
        grads = grad_ref[layer].astype(F32)
        moms = mom_ref[layer]
        for i, prod in enumerate((grads * grads, grads * moms, moms * moms)):
            acc[pl.ds(3 * layer + i, 1), :] = jnp.sum(prod, axis=0, keepdims=True)

    acc[...] = jnp.zeros_like(acc)
    over(layers, begin)
    over(layers, visit)
    column = jnp.sum(acc[...], axis=1, keepdims=True)
    shape = (acc.shape[0], out_ref.shape[1])
    hit = lax.broadcasted_iota(jnp.int32, shape, 0) == lax.broadcasted_iota(jnp.int32, shape, 1)
    line = jnp.sum(jnp.where(hit, column, 0.0), axis=0, keepdims=True)
    out_ref[...] = jnp.broadcast_to(line, out_ref.shape)


def pair_nt(left, right):
    return lax.dot_general(left, right, (((1,), (1,)), ((), ())), preferred_element_type=F32)


def start_kernel(
    layers, entries, owners, sums_ref, grad_ref, mom_ref, start_ref, keep_ref, send_ref, fac_ref, pack
):
    place = lax.axis_index("dp")
    chip, core, section = place >> 1, place & 1, lax.axis_index("section")
    lane = lax.broadcasted_iota(jnp.int32, (1, sums_ref.shape[1]), 1)
    every = jnp.sum(sums_ref[...], axis=0, keepdims=True)
    mine = sums_ref[pl.ds(pl.multiple_of(section * owners, 8), owners), :]
    mine = jnp.sum(mine, axis=0, keepdims=True)
    kind = lax.rem(lane, 3)
    total = jnp.sum(jnp.where(kind == 0, every, 0.0), axis=1, keepdims=True)
    factor = clip_rms / jnp.sqrt(total / entries + 1e-06)
    fac_ref[...] = jnp.broadcast_to(factor, fac_ref.shape)
    on_grad = factor * (1.0 + momentum_decay)
    on_mom = momentum_decay * momentum_decay
    cross = 2.0 * (on_grad * on_mom)
    known = mine * jnp.where(
        kind == 0, on_grad * on_grad, jnp.where(kind == 1, cross, on_mom * on_mom)
    )

    def visit(layer):
        here = (lane >= 3 * layer) & (lane < 3 * layer + 3)
        guess = jnp.maximum(jnp.sum(jnp.where(here, known, 0.0), axis=1, keepdims=True), 0.0)
        scale = 1.0 / (jnp.sqrt(guess) + 1e-07)
        scaled = factor * grad_ref[layer].astype(F32)
        fresh = momentum_decay * mom_ref[layer] + scaled
        nesterov = (scaled + momentum_decay * fresh).astype(BF16).astype(F32)
        squares = total_of(nesterov * nesterov)
        start = (nesterov * scale).astype(BF16)
        start_ref[layer] = start
        width = start.shape[0]
        tail = width - 2 * LANES
        a, b = LANES, 2 * LANES
        gram = pair_nt(start[0:b], start[0:b])
        edge = pair_nt(start[b:], start)
        hold = pack.at[lax.rem(layer, 2)]
        hold[0:a, :] = gram[0:a, 0:a]
        hold[a:b, :] = gram[0:a, a:b]
        hold[b : b + a, :] = gram[a:b, a:b]
        at = b + a
        hold[at : at + tail, :] = edge[:, 0:a]
        hold[at + tail : at + 2 * tail, :] = edge[:, a:b]
        spot = lax.broadcasted_iota(jnp.int32, (tail, LANES), 1)
        extra = jnp.where(spot == 64, squares, 0.0) + jnp.where(spot == 65, guess, 0.0)
        hold[at + 2 * tail :, :] = extra
        hold[at + 2 * tail :, 0:tail] = edge[:, b:]
        half = pack.shape[1] // 2
        keep_ref[layer ^ chip] = hold[pl.ds(pl.multiple_of(core * half, 8), half), :]
        send_ref[layer ^ chip] = hold[pl.ds(pl.multiple_of((1 - core) * half, 8), half), :]

    over(layers, visit)


def split(value):
    high = value.astype(BF16)
    return high, (value - high.astype(F32)).astype(BF16)


def dot(left, right):
    return jnp.dot(left, right, preferred_element_type=F32)


def wide_left(left, right):
    high, low = split(left)
    b = 2 * LANES
    ends = jnp.concatenate([high[:, b:], low[:, b:]], axis=1)
    rest = jnp.concatenate([right[b:], right[b:]], axis=0)
    return dot(high[:, :b], right[:b]) + dot(low[:, :b], right[:b]) + dot(ends, rest)


def wide_right(left, right):
    high, low = split(right)
    b = 2 * LANES
    ends = jnp.concatenate([left[:, b:], left[:, b:]], axis=1)
    rest = jnp.concatenate([high[b:], low[b:]], axis=0)
    return dot(left[:, :b], high[:b]) + dot(left[:, :b], low[:b]) + dot(ends, rest)


def newton_kernel(owners, width, scal_ref, own_ref, other_ref, mine_ref, theirs_ref, pack, full):
    core = scal_ref[1]
    half = own_ref.shape[0]
    pack[pl.ds(pl.multiple_of(core * half, 8), half), :] = own_ref[...]
    pack[pl.ds(pl.multiple_of((1 - core) * half, 8), half), :] = other_ref[...]
    tail = width - 2 * LANES
    a, b = LANES, 2 * LANES
    at = b + a
    t00, t01, t11 = pack[0:a, :], pack[a:b, :], pack[b:at, :]
    t20, t21 = pack[at : at + tail, :], pack[at + tail : at + 2 * tail, :]
    last = pack[at + 2 * tail :, :]
    t22 = last[:, 0:tail]
    squares = last[0:1, 64:65]
    guess = last[0:1, 65:66] * (1.0 / owners)
    ratio = (jnp.sqrt(guess) + 1e-07) / (jnp.sqrt(squares) + 1e-07)
    gram = jnp.concatenate(
        [
            jnp.concatenate([t00, t01, t20.T], axis=1),
            jnp.concatenate([t01.T, t11, t21.T], axis=1),
            jnp.concatenate([t20, t21, t22], axis=1),
        ],
        axis=0,
    )
    gram = gram * (ratio * ratio)
    ca, cb, cc = newton_coeffs
    rows = lax.broadcasted_iota(jnp.int32, (width, width), 0)
    cols = lax.broadcasted_iota(jnp.int32, (width, width), 1)
    prod = None
    mean_sq = None
    for step in range(NS_STEPS):
        rounded = gram.astype(BF16)
        mix = (cb * rounded.astype(F32) + cc * dot(rounded, rounded)).astype(BF16)
        mix32 = mix.astype(F32)
        turned = ca * gram + wide_left(gram, mix)
        if step < NS_STEPS - 1:
            gram = ca * turned + wide_right(mix, turned)
        else:
            diagonal = jnp.where(rows == cols, turned, 0.0)
            mean_sq = total_of(ca * diagonal + mix32 * turned) * (1.0 / width)
        if prod is None:
            prod = ratio * (jnp.where(rows == cols, ca, 0.0) + mix32)
        else:
            prod = ca * prod + wide_right(mix, prod)
    full[0:width, :] = prod[:, 0:a]
    full[width : 2 * width, :] = prod[:, a:b]
    group = width * tail // LANES
    for i in range(LANES // tail):
        full[2 * width : 2 * width + group, i * tail : (i + 1) * tail] = prod[i * group : (i + 1) * group, b:]
    full[2 * width + group :, :] = jnp.broadcast_to(mean_sq, (8, LANES))
    half = mine_ref.shape[0]
    mine_ref[...] = full[pl.ds(pl.multiple_of(core * half, 8), half), :]
    theirs_ref[...] = full[pl.ds(pl.multiple_of((1 - core) * half, 8), half), :]


def update_kernel(scale, width, rel, final, *refs):
    scal_ref, owner_ref, start_ref, mine_ref, other_ref = refs[:5]
    if rel == 0:
        out_ref, means_out, slot_ref, full = refs[5:]
    else:
        means_ref, _, out_ref, means_out, slot_ref, full = refs[5:]
    core = scal_ref[1]
    layer = scal_ref[0] ^ rel
    half = mine_ref.shape[0]
    full[pl.ds(pl.multiple_of(core * half, 8), half), :] = mine_ref[...]
    full[pl.ds(pl.multiple_of((1 - core) * half, 8), half), :] = other_ref[...]
    tail = width - 2 * LANES
    b = 2 * LANES
    group = width * tail // LANES
    main = jnp.concatenate([full[0:width, :], full[width : 2 * width, :]], axis=1)
    ends = full[2 * width : 2 * width + group, :]
    ends = jnp.concatenate([ends[:, i * tail : (i + 1) * tail] for i in range(LANES // tail)], axis=0)
    high, low = split(main)
    end_high, end_low = split(ends)
    start = start_ref[0]
    rest = jnp.concatenate([start[b:], start[b:]], axis=0)
    value = dot(high, start[:b]) + dot(low, start[:b])
    value = value + dot(jnp.concatenate([end_high, end_low], axis=1), rest)
    out_ref[0] = (value * scale).astype(BF16)
    lane = lax.broadcasted_iota(jnp.int32, means_out.shape, 1)
    means = jnp.where(lane == layer, full[2 * width + group :, :], 0.0)
    if rel:
        means = means + means_ref[...]
    means_out[...] = means
    if not final:
        for slot in range(MAXOWN):
            slot_ref[0, slot] = 0.0
        return
    layers = owner_ref.shape[1]
    me = scal_ref[3]
    for slot in range(MAXOWN):

        def visit(j, carry):
            seen, at = carry
            hit = owner_ref[0, j] == me
            at = jnp.where(hit & (seen == slot), j, at)
            return seen + jnp.where(hit, 1, 0), at

        _, at = lax.fori_loop(0, layers, visit, (jnp.int32(0), jnp.int32(-1)))
        slot_ref[0, slot] = jnp.sum(jnp.where(lane[0:1] == at, means[0:1], 0.0))


def step(momentum, gradient, assignment):
    _, layers, rows, width = momentum.shape
    owners = lax.axis_size("dp")
    sections = lax.axis_size("section")
    chips = owners // 2
    tail = width - 2 * LANES
    assert chips == layers and chips & (chips - 1) == 0 and LANES % tail == 0 and 3 * layers <= LANES
    everyone = sections * owners
    entries = everyone * layers * rows * width
    mom = jnp.swapaxes(momentum[0], 1, 2)
    grad = jnp.swapaxes(gradient[0], 1, 2)
    place = lax.axis_index("dp")
    scal = jnp.stack([place >> 1, place & 1, lax.axis_index("section"), place]).astype(jnp.int32)

    anywhere = pl.BlockSpec(memory_space=pl.ANY)
    near_by = pl.BlockSpec(memory_space=pltpu.VMEM)
    sums, grad_near, mom_near = pl.pallas_call(
        functools.partial(sums_kernel, layers),
        in_specs=[anywhere, anywhere],
        out_specs=[near_by] * 3,
        out_shape=[
            jax.ShapeDtypeStruct((everyone, LANES), F32),
            jax.ShapeDtypeStruct(grad.shape, BF16),
            jax.ShapeDtypeStruct(mom.shape, F32),
        ],
        scratch_shapes=[
            pltpu.VMEM((-(-3 * layers // 8) * 8, rows), F32),
            pltpu.SemaphoreType.DMA((layers, 2)),
        ],
        compiler_params=params(),
        name="sums",
    )(pltpu.with_memory_space_constraint(grad, pltpu.HBM), pltpu.with_memory_space_constraint(mom, pltpu.HBM))
    sums = lax.all_to_all(sums, ("section", "dp"), 0, 0, tiled=True)

    packed = 3 * LANES + 3 * tail
    half = packed // 2
    start, keep, send, factor = pl.pallas_call(
        functools.partial(start_kernel, layers, entries, owners),
        in_specs=[near_by] * 3,
        out_specs=[near_by] * 4,
        out_shape=[
            jax.ShapeDtypeStruct((layers, width, rows), BF16),
            jax.ShapeDtypeStruct((layers, half, LANES), F32),
            jax.ShapeDtypeStruct((layers, half, LANES), F32),
            jax.ShapeDtypeStruct((8, LANES), F32),
        ],
        scratch_shapes=[pltpu.VMEM((2, packed, LANES), F32)],
        compiler_params=params(),
        name="start",
    )(sums, grad_near, mom_near)

    def turn(value, by):
        return lax.ppermute(value, "dp", [(i, i ^ by) for i in range(owners)])

    chip_sums = keep + turn(send, 1)
    own = chip_sums[0]
    for rel in range(1, chips):
        own = own + turn(chip_sums[rel], 2 * rel)
    fresh = momentum_decay * mom_near + factor[0, 0] * grad_near.astype(F32)
    own, fresh = lax.optimization_barrier((own, fresh))
    other = turn(own, 1)

    full_rows = 2 * width + width * tail // LANES + 8
    piece = full_rows // 2
    mine, theirs = pl.pallas_call(
        functools.partial(newton_kernel, owners, width),
        grid_spec=pltpu.PrefetchScalarGridSpec(
            num_scalar_prefetch=1,
            grid=(1,),
            in_specs=[whole((half, LANES)), whole((half, LANES))],
            out_specs=[whole((piece, LANES)), whole((piece, LANES))],
            scratch_shapes=[pltpu.VMEM((packed, LANES), F32), pltpu.VMEM((full_rows, LANES), F32)],
        ),
        out_shape=[jax.ShapeDtypeStruct((piece, LANES), F32)] * 2,
        compiler_params=params(),
        name="newton",
    )(scal, own, other)

    update = means = slots = None
    flops = 4 * width * width * rows
    for rel in range(chips):
        if rel:
            near = arriving[rel]
            if rel < chips - 1:
                near, update = lax.optimization_barrier((near, update))
            far = turn(near, 1)
        else:
            arriving = {}
            for k in range(1, chips):
                arriving[k] = turn(mine, 2 * k)
            near, far = mine, theirs
        pick = pl.BlockSpec((1, width, rows), lambda k, s, _, rel=rel: (s[0] ^ rel, 0, 0))
        operands = [scal, assignment, start, near, far]
        in_specs = [pick, whole((piece, LANES)), whole((piece, LANES))]
        aliases = {}
        if rel:
            operands += [means, update]
            in_specs += [whole((8, LANES)), pl.BlockSpec(memory_space=pl.ANY)]
            aliases = {6: 0}
        call = pl.pallas_call(
            functools.partial(
                update_kernel, math.sqrt(owners * rows), width, rel, rel == chips - 1
            ),
            grid_spec=pltpu.PrefetchScalarGridSpec(
                num_scalar_prefetch=2,
                grid=(1,),
                in_specs=in_specs,
                out_specs=[
                    pick,
                    whole((8, LANES)),
                    pl.BlockSpec((1, MAXOWN), lambda *_: (0, 0), memory_space=pltpu.SMEM),
                ],
                scratch_shapes=[pltpu.VMEM((full_rows, LANES), F32)],
            ),
            out_shape=[
                jax.ShapeDtypeStruct((layers, width, rows), BF16),
                jax.ShapeDtypeStruct((8, LANES), F32),
                jax.ShapeDtypeStruct((1, MAXOWN), F32),
            ],
            input_output_aliases=aliases,
            compiler_params=params(),
            cost_estimate=cost(flops, 4 * width * rows + 8 * piece * LANES),
            name="update",
        )
        update, means, slots = call(*operands)
    return (jnp.swapaxes(fresh, 1, 2)[None], jnp.swapaxes(update, 1, 2)[None], slots)


def solution(mesh):
    in_specs = (P("section", None, "dp", None), P("section", None, "dp", None), P("section", None))
    out_specs = (P("section", None, "dp", None), P("section", None, "dp", None), P("section", "dp"))
    return jax.shard_map(step, mesh=mesh, in_specs=in_specs, out_specs=out_specs, check_vma=False)
```

time: 271 us -> 68.9 us (0.25)
  blocking collectives: 150 us -> 13.7 us
  local copies, waits for them, and re-layouts: 48.2 us -> 0.54 us
  matrix products: 31.5 us -> 0 us
  other arithmetic: 32.1 us -> 2.66 us
  waiting for transfers between devices: 0.01 us -> 18.9 us
  Pallas kernels: 0 us -> 17.3 us
  starting transfers between devices: 4.67 us -> 14.6 us
    psum x2 -> x0, blocking collectives: 91.3 us -> none  [the longest x1 50.5 us: body(): layer_vec = lax.psum(my_row * own_sum, 'dp')]
    all_to_all x1, blocking collectives: 58.3 us -> 13.7 us  [step(): sums = lax.all_to_all(sums, ('section', 'dp'), 0, 0, tiled=True)]
    dot_general x13 -> x0, matrix products: 31.5 us -> none  [the longest x5 18.5 us: newton(): jnp.einsum('kri,kij->krj', current, mixing, preferred_element_type=jnp.fl...]
    unnamed x1 -> x0, other arithmetic: 23.2 us -> none
    ppermute x0 -> x11, waiting for transfers between devices: none -> 18.9 us  [turn(): return lax.ppermute(value, 'dp', [(i, i ^ by) for i in range(owners)])]
    pallas_call x0 -> x7, Pallas kernels: none -> 17.3 us  [the longest x4 6.94 us: step(): update, means, slots = call(*operands)]
    unnamed x10 -> x2, local copies, waits for them, and re-layouts: 15 us -> 0.01 us
    ppermute x0 -> x11, starting transfers between devices: none -> 14.6 us  [turn(): return lax.ppermute(value, 'dp', [(i, i ^ by) for i in range(owners)])]
  transfers between devices with their start and end apart: 1 -> 11, of which waited for: 0 -> 6; matrix products, arithmetic and copies ran while one was open for 0% -> 4% of each run, Pallas kernels for 0% -> 7%
where the time goes in v2:
time: 68.9 us; the launch traced here: 68.4 us
  waiting for transfers between devices  18.9 us (27%)
  Pallas kernels  17.3 us (25%)
  starting transfers between devices  14.6 us (21%)
  blocking collectives  13.7 us (20%)
  other arithmetic  2.66 us (4%)
  between operations  0.7 us (1%)
    ppermute x11, waiting for transfers between devices, turn(): return lax.ppermute(value, 'dp', [(i, i ^ by) for i in range(owners)])  18.9 us
    ppermute x11, starting transfers between devices, turn(): return lax.ppermute(value, 'dp', [(i, i ^ by) for i in range(owners)])  14.6 us
    all_to_all x1, blocking collectives, step(): sums = lax.all_to_all(sums, ('section', 'dp'), 0, 0, tiled=True)  13.7 us
    pallas_call x4, Pallas kernels, step(): update, means, slots = call(*operands)  6.94 us
    pallas_call x1, Pallas kernels, step(): pl.pallas_call(functools.partial(newton_kernel, owners, width), grid_spec...  5.78 us
    add x1, other arithmetic, step(): fresh = momentum_decay * mom_near + factor[0, 0] * grad_near.astype(F32)  2.47 us
    pallas_call x1, Pallas kernels, step(): pl.pallas_call(functools.partial(sums_kernel, layers), in_specs=[anywhere...  2.31 us
    pallas_call x1, Pallas kernels, step(): pl.pallas_call(functools.partial(start_kernel, layers, entries, owners),...  2.29 us
  transfers between devices with their start and end apart: 11, of which 6 were waited for; matrix products, arithmetic and copies ran while one was open for 4% of the time, Pallas kernels for 7%

profile of v2, /device:TPU:1, one launch (start us, length us, event | category | flops | bytes accessed | tf_op | source)
XLA Modules:
  0.0 68.4 jit_solution(9565714620670491065)
XLA Ops:
  0.6 2.3 %sums.1 = (f32[32,128]{1,0:T(8,128)S(1)}, bf16[4,288,448]{2,1,0:T(8,128)(2,1)S(1)}, f32[4,288,448]{2,1,0:T(8,128)S(1)}) custom-call(bf16[4,288,448]{2,1,0:T(8,128)(2,1)} %bitcast.40, f32[4,288,448]{2,1,0:T(8,128)} %bitcast.39), custom_call_target="tpu_custom_call" | custom-call | tf_op jit(solution)/shard_map/sums/pallas_call | solution.py:279
  3.0 13.7 %all_to_all.11 = f32[32,1,128]{2,1,0:T(1,128)S(1)} all-to-all(f32[32,1,128]{2,1,0:T(1,128)S(1)} %bitcast.36), channel_id=1, replica_groups=mesh['section'=4,'dp'=8] {'section','dp'}, dimensions={0} | all-to-all | bytes 32768 | tf_op jit(solution)/shard_map/all_to_all | solution.py:295
  16.6 2.3 %start.1 = (bf16[4,288,448]{2,1,0:T(8,128)(2,1)S(1)}, f32[4,240,128]{2,1,0:T(8,128)S(1)}, f32[4,240,128]{2,1,0:T(8,128)S(1)}, f32[8,128]{1,0:T(8,128)S(1)}) custom-call(f32[32,128]{1,0:T(8,128)S(1)} %bitcast.35, bf16[4,288,448]{2,1,0:T(8,128)(2,1)S(1)} %get-tuple-element.27.grad_ref, f32[4,288,448]{2,1,0:T(8,128)S(1)} %get-tuple-element.28.mom_ref), custom_call_target="tpu_custom_call" | custom-call | tf_op jit(solution)/shard_map/start/pallas_call | solution.py:299
  18.9 0.7 %collective-permute-start = (f32[4,240,128]{2,1,0:T(8,128)S(1)}, f32[4,240,128]{2,1,0:T(8,128)S(1)}, u32[]{:S(2)}, u32[]{:S(2)}) collective-permute-start(f32[4,240,128]{2,1,0:T(8,128)S(1)} %get-tuple-element.30), channel_id=1, source_target_pairs={{0,1},{1,0},{2,3},{3,2},{4,5},{5,4},{6,7},{7,6},{8,9},{9,8},{10,11... | collective-permute-start | bytes 1474568 | tf_op jit(solution)/shard_map/ppermute | solution.py:315
  19.6 0.5 slice.19
  20.1 1.0 %collective-permute-done = f32[4,240,128]{2,1,0:T(8,128)S(1)} collective-permute-done((f32[4,240,128]{2,1,0:T(8,128)S(1)}, f32[4,240,128]{2,1,0:T(8,128)S(1)}, u32[]{:S(2)}, u32[]{:S(2)}) %collective-permute-start) | collective-permute-done | bytes 491552 | tf_op jit(solution)/shard_map/ppermute | solution.py:315
  21.1 0.1 add.15
  21.2 0.3 collective-permute-start.1
  21.5 0.3 collective-permute-start.2
  21.9 3.0 %collective-permute-start.3 = (f32[240,128]{1,0:T(8,128)S(1)}, f32[240,128]{1,0:T(8,128)S(1)}, u32[]{:S(2)}, u32[]{:S(2)}) collective-permute-start(f32[240,128]{1,0:T(8,128)S(1)} %get-tuple-element.50), channel_id=1, source_target_pairs={{0,6},{1,7},{2,4},{3,5},{4,2},{5,3},{6,0},{7,1},{8,14},{9,15},{10,... | collective-permute-start | bytes 368648 | tf_op jit(solution)/shard_map/ppermute | solution.py:315
  24.8 0.0 copy-start
  24.8 2.5 %multiply_add_fusion = f32[4,288,448]{2,1,0:T(8,128)} fusion(bf16[4,288,448]{2,1,0:T(8,128)(2,1)S(1)} %get-tuple-element.27.grad_ref, f32[4,288,448]{2,1,0:T(8,128)S(1)} %get-tuple-element.28.mom_ref, f32[]{:T(128)} %bitcast.11), kind=kLoop, calls=%fused_computation | loop fusion | flops 2064384 | bytes 5160964 | tf_op jit(solution)/shard_map/add | solution.py:321
  27.3 0.0 collective-permute-done.1
  27.3 4.7 %collective-permute-done.2 = f32[240,128]{1,0:T(8,128)S(1)} collective-permute-done((f32[240,128]{1,0:T(8,128)S(1)}, f32[240,128]{1,0:T(8,128)S(1)}, u32[]{:S(2)}, u32[]{:S(2)}) %collective-permute-start.2) | collective-permute-done | bytes 122912 | tf_op jit(solution)/shard_map/ppermute | solution.py:315
  32.0 0.0 collective-permute-done.3
  32.1 2.5 %collective-permute-start.4 = (f32[240,128]{1,0:T(8,128)S(1)}, f32[240,128]{1,0:T(8,128)S(1)}, u32[]{:S(2)}, u32[]{:S(2)}) collective-permute-start(f32[240,128]{1,0:T(8,128)S(1)} %fusion.2.own_ref), channel_id=1, source_target_pairs={{0,1},{1,0},{2,3},{3,2},{4,5},{5,4},{6,7},{7,6},{8,9},{9,8},{10,11... | collective-permute-start | bytes 368648 | tf_op jit(solution)/shard_map/ppermute | solution.py:315
  34.6 0.1 pad_add_fusion.scal_ref.refs_0_
  34.7 0.9 %collective-permute-done.4.other_ref = f32[240,128]{1,0:T(8,128)S(1)} collective-permute-done((f32[240,128]{1,0:T(8,128)S(1)}, f32[240,128]{1,0:T(8,128)S(1)}, u32[]{:S(2)}, u32[]{:S(2)}) %collective-permute-start.4) | collective-permute-done | bytes 122912 | tf_op jit(solution)/shard_map/ppermute | solution.py:315
  35.6 5.8 %newton.1 = (f32[328,128]{1,0:T(8,128)S(1)}, f32[328,128]{1,0:T(8,128)S(1)}) custom-call(s32[4]{0:T(128)S(1)} %pad_add_fusion.scal_ref.refs_0_, f32[240,128]{1,0:T(8,128)S(1)} %fusion.2.own_ref, f32[240,128]{1,0:T(8,128)S(1)} %collective-permute-done.4.other_ref), custom_call_target="tpu_custom_call" | custom-call | tf_op jit(solution)/shard_map/newton/pallas_call | solution.py:327
  41.3 2.0 %collective-permute-start.8 = (f32[328,128]{1,0:T(8,128)S(1)}, f32[328,128]{1,0:T(8,128)S(1)}, u32[]{:S(2)}, u32[]{:S(2)}) collective-permute-start(f32[328,128]{1,0:T(8,128)S(1)} %get-tuple-element.35.refs_3_), channel_id=1, source_target_pairs={{0,2},{1,3},{2,0},{3,1},{4,6},{5,7},{6,4},{7,5},{8,10},{9,11},{10,... | collective-permute-start | bytes 503816 | tf_op jit(solution)/shard_map/ppermute | solution.py:315
  43.3 0.0 copy-done
  43.3 1.7 %update.4 = (bf16[4,288,448]{2,1,0:T(8,128)(2,1)}, f32[8,128]{1,0:T(8,128)S(1)}, f32[1,2]{1,0:T(1,128)}) custom-call(s32[4]{0:T(128)S(1)} %pad_add_fusion.scal_ref.refs_0_, s32[1,4]{1,0:T(1,128)S(1)} %copy-done, bf16[4,288,448]{2,1,0:T(8,128)(2,1)S(1)} %get-tuple-element.33.refs_2_, f32[328,128]{1,0:T(8,128)S(1)} %get-tuple-element.35.refs_3_, ...), custom_call_target="tpu_custom_call" | custom-call | flops 148635648 | bytes 851968 | tf_op jit(solution)/shard_map/update/pallas_call | solution.py:387
  45.0 2.6 %collective-permute-done.8.refs_3_ = f32[328,128]{1,0:T(8,128)S(1)} collective-permute-done((f32[328,128]{1,0:T(8,128)S(1)}, f32[328,128]{1,0:T(8,128)S(1)}, u32[]{:S(2)}, u32[]{:S(2)}) %collective-permute-start.8) | collective-permute-done | bytes 167968 | tf_op jit(solution)/shard_map/ppermute | solution.py:315
  47.6 0.9 %collective-permute-start.9 = (f32[328,128]{1,0:T(8,128)S(1)}, f32[328,128]{1,0:T(8,128)S(1)}, u32[]{:S(2)}, u32[]{:S(2)}) collective-permute-start(f32[328,128]{1,0:T(8,128)S(1)} %collective-permute-done.8.refs_3_), channel_id=1, source_target_pairs={{0,1},{1,0},{2,3},{3,2},{4,5},{5,4},{6,7},{7,6},{8,9},{9,8},{10,11... | collective-permute-start | bytes 503816 | tf_op jit(solution)/shard_map/ppermute | solution.py:315
  48.5 1.5 %collective-permute-start.7 = (f32[328,128]{1,0:T(8,128)S(1)}, f32[328,128]{1,0:T(8,128)S(1)}, u32[]{:S(2)}, u32[]{:S(2)}) collective-permute-start(f32[328,128]{1,0:T(8,128)S(1)} %get-tuple-element.35.refs_3_), channel_id=1, source_target_pairs={{0,4},{1,5},{2,6},{3,7},{4,0},{5,1},{6,2},{7,3},{8,12},{9,13},{10,... | collective-permute-start | bytes 503816 | tf_op jit(solution)/shard_map/ppermute | solution.py:315
  50.0 2.1 %collective-permute-start.5 = (f32[328,128]{1,0:T(8,128)S(1)}, f32[328,128]{1,0:T(8,128)S(1)}, u32[]{:S(2)}, u32[]{:S(2)}) collective-permute-start(f32[328,128]{1,0:T(8,128)S(1)} %get-tuple-element.35.refs_3_), channel_id=1, source_target_pairs={{0,6},{1,7},{2,4},{3,5},{4,2},{5,3},{6,0},{7,1},{8,14},{9,15},{10,... | collective-permute-start | bytes 503816 | tf_op jit(solution)/shard_map/ppermute | solution.py:315
  52.1 0.0 collective-permute-done.9.refs_4_
  52.1 1.7 %update.5 = (bf16[4,288,448]{2,1,0:T(8,128)(2,1)}, f32[8,128]{1,0:T(8,128)S(1)}, f32[1,2]{1,0:T(1,128)}) custom-call(s32[4]{0:T(128)S(1)} %pad_add_fusion.scal_ref.refs_0_, s32[1,4]{1,0:T(1,128)S(1)} %copy-done, bf16[4,288,448]{2,1,0:T(8,128)(2,1)S(1)} %get-tuple-element.33.refs_2_, ...), custom_call_target="tpu_custom_call", output_to_operand_aliasing={{0}: (6, {})} | custom-call | flops 148635648 | bytes 851968 | tf_op jit(solution)/shard_map/update/pallas_call | solution.py:387
  53.8 8.7 %collective-permute-done.7.refs_3_ = f32[328,128]{1,0:T(8,128)S(1)} collective-permute-done((f32[328,128]{1,0:T(8,128)S(1)}, f32[328,128]{1,0:T(8,128)S(1)}, u32[]{:S(2)}, u32[]{:S(2)}) %collective-permute-start.7) | collective-permute-done | bytes 167968 | tf_op jit(solution)/shard_map/ppermute | solution.py:315
  62.5 1.3 %collective-permute-start.10 = (f32[328,128]{1,0:T(8,128)S(1)}, f32[328,128]{1,0:T(8,128)S(1)}, u32[]{:S(2)}, u32[]{:S(2)}) collective-permute-start(f32[328,128]{1,0:T(8,128)S(1)} %collective-permute-done.7.refs_3_), channel_id=1, source_target_pairs={{0,1},{1,0},{2,3},{3,2},{4,5},{5,4},{6,7},{7,6},{8,9},{9,8},{10,11... | collective-permute-start | bytes 503816 | tf_op jit(solution)/shard_map/ppermute | solution.py:315
  63.8 0.0 collective-permute-done.5.refs_3_
  63.8 0.0 collective-permute-start.6
  63.8 1.0 %collective-permute-done.10.refs_4_ = f32[328,128]{1,0:T(8,128)S(1)} collective-permute-done((f32[328,128]{1,0:T(8,128)S(1)}, f32[328,128]{1,0:T(8,128)S(1)}, u32[]{:S(2)}, u32[]{:S(2)}) %collective-permute-start.10) | collective-permute-done | bytes 167968 | tf_op jit(solution)/shard_map/ppermute | solution.py:315
  64.8 1.7 %update.6 = (bf16[4,288,448]{2,1,0:T(8,128)(2,1)}, f32[8,128]{1,0:T(8,128)S(1)}, f32[1,2]{1,0:T(1,128)}) custom-call(s32[4]{0:T(128)S(1)} %pad_add_fusion.scal_ref.refs_0_, s32[1,4]{1,0:T(1,128)S(1)} %copy-done, bf16[4,288,448]{2,1,0:T(8,128)(2,1)S(1)} %get-tuple-element.33.refs_2_, ...), custom_call_target="tpu_custom_call", output_to_operand_aliasing={{0}: (6, {})} | custom-call | flops 148635648 | bytes 851968 | tf_op jit(solution)/shard_map/update/pallas_call | solution.py:387
  66.5 0.0 collective-permute-done.6.refs_4_
  66.5 1.9 %update.7 = (bf16[4,288,448]{2,1,0:T(8,128)(2,1)}, f32[8,128]{1,0:T(8,128)}, f32[1,2]{1,0:T(1,128)}) custom-call(s32[4]{0:T(128)S(1)} %pad_add_fusion.scal_ref.refs_0_, s32[1,4]{1,0:T(1,128)S(1)} %copy-done, bf16[4,288,448]{2,1,0:T(8,128)(2,1)S(1)} %get-tuple-element.33.refs_2_, ...), custom_call_target="tpu_custom_call", output_to_operand_aliasing={{0}: (6, {})} | custom-call | flops 148635648 | bytes 851968 | tf_op jit(solution)/shard_map/update/pallas_call | solution.py:387
  (2 shorter events, 0.1 us)
Async XLA Ops:
  18.9 2.2 %collective-permute-start = (f32[4,240,128]{2,1,0:T(8,128)S(1)}, f32[4,240,128]{2,1,0:T(8,128)S(1)}, u32[]{:S(2)}, u32[]{:S(2)}) collective-permute-start(f32[4,240,128]{2,1,0:T(8,128)S(1)} %get-tuple-element.30), channel_id=1, source_target_pairs={{0,1},{1,0},{2,3},{3,2},{4,5},{5,4},{6,7},{7,6},{8,9},{9,8},{10,11... | collective-permute-start | bytes 1474568 | tf_op jit(solution)/shard_map/ppermute | solution.py:315
  21.2 6.1 %collective-permute-start.1 = (f32[240,128]{1,0:T(8,128)S(1)}, f32[240,128]{1,0:T(8,128)S(1)}, u32[]{:S(2)}, u32[]{:S(2)}) collective-permute-start(f32[240,128]{1,0:T(8,128)S(1)} %get-tuple-element.49), channel_id=1, source_target_pairs={{0,2},{1,3},{2,0},{3,1},{4,6},{5,7},{6,4},{7,5},{8,10},{9,11},{10,... | collective-permute-start | bytes 368648 | tf_op jit(solution)/shard_map/ppermute | solution.py:315
  21.5 10.5 %collective-permute-start.2 = (f32[240,128]{1,0:T(8,128)S(1)}, f32[240,128]{1,0:T(8,128)S(1)}, u32[]{:S(2)}, u32[]{:S(2)}) collective-permute-start(f32[240,128]{1,0:T(8,128)S(1)} %get-tuple-element.51), channel_id=1, source_target_pairs={{0,4},{1,5},{2,6},{3,7},{4,0},{5,1},{6,2},{7,3},{8,12},{9,13},{10,... | collective-permute-start | bytes 368648 | tf_op jit(solution)/shard_map/ppermute | solution.py:315
  21.9 10.2 %collective-permute-start.3 = (f32[240,128]{1,0:T(8,128)S(1)}, f32[240,128]{1,0:T(8,128)S(1)}, u32[]{:S(2)}, u32[]{:S(2)}) collective-permute-start(f32[240,128]{1,0:T(8,128)S(1)} %get-tuple-element.50), channel_id=1, source_target_pairs={{0,6},{1,7},{2,4},{3,5},{4,2},{5,3},{6,0},{7,1},{8,14},{9,15},{10,... | collective-permute-start | bytes 368648 | tf_op jit(solution)/shard_map/ppermute | solution.py:315
  24.8 18.5 %copy-start = (s32[1,4]{1,0:T(1,128)S(1)}, s32[1,4]{1,0:T(1,128)}, u32[]{:S(2)}) copy-start(s32[1,4]{1,0:T(1,128)} %refs_1_.7) | copy-start | bytes 52
  32.1 3.5 %collective-permute-start.4 = (f32[240,128]{1,0:T(8,128)S(1)}, f32[240,128]{1,0:T(8,128)S(1)}, u32[]{:S(2)}, u32[]{:S(2)}) collective-permute-start(f32[240,128]{1,0:T(8,128)S(1)} %fusion.2.own_ref), channel_id=1, source_target_pairs={{0,1},{1,0},{2,3},{3,2},{4,5},{5,4},{6,7},{7,6},{8,9},{9,8},{10,11... | collective-permute-start | bytes 368648 | tf_op jit(solution)/shard_map/ppermute | solution.py:315
  41.3 6.3 %collective-permute-start.8 = (f32[328,128]{1,0:T(8,128)S(1)}, f32[328,128]{1,0:T(8,128)S(1)}, u32[]{:S(2)}, u32[]{:S(2)}) collective-permute-start(f32[328,128]{1,0:T(8,128)S(1)} %get-tuple-element.35.refs_3_), channel_id=1, source_target_pairs={{0,2},{1,3},{2,0},{3,1},{4,6},{5,7},{6,4},{7,5},{8,10},{9,11},{10,... | collective-permute-start | bytes 503816 | tf_op jit(solution)/shard_map/ppermute | solution.py:315
  47.6 4.5 %collective-permute-start.9 = (f32[328,128]{1,0:T(8,128)S(1)}, f32[328,128]{1,0:T(8,128)S(1)}, u32[]{:S(2)}, u32[]{:S(2)}) collective-permute-start(f32[328,128]{1,0:T(8,128)S(1)} %collective-permute-done.8.refs_3_), channel_id=1, source_target_pairs={{0,1},{1,0},{2,3},{3,2},{4,5},{5,4},{6,7},{7,6},{8,9},{9,8},{10,11... | collective-permute-start | bytes 503816 | tf_op jit(solution)/shard_map/ppermute | solution.py:315
  48.5 13.9 %collective-permute-start.7 = (f32[328,128]{1,0:T(8,128)S(1)}, f32[328,128]{1,0:T(8,128)S(1)}, u32[]{:S(2)}, u32[]{:S(2)}) collective-permute-start(f32[328,128]{1,0:T(8,128)S(1)} %get-tuple-element.35.refs_3_), channel_id=1, source_target_pairs={{0,4},{1,5},{2,6},{3,7},{4,0},{5,1},{6,2},{7,3},{8,12},{9,13},{10,... | collective-permute-start | bytes 503816 | tf_op jit(solution)/shard_map/ppermute | solution.py:315
  50.0 13.8 %collective-permute-start.5 = (f32[328,128]{1,0:T(8,128)S(1)}, f32[328,128]{1,0:T(8,128)S(1)}, u32[]{:S(2)}, u32[]{:S(2)}) collective-permute-start(f32[328,128]{1,0:T(8,128)S(1)} %get-tuple-element.35.refs_3_), channel_id=1, source_target_pairs={{0,6},{1,7},{2,4},{3,5},{4,2},{5,3},{6,0},{7,1},{8,14},{9,15},{10,... | collective-permute-start | bytes 503816 | tf_op jit(solution)/shard_map/ppermute | solution.py:315
  62.5 2.4 %collective-permute-start.10 = (f32[328,128]{1,0:T(8,128)S(1)}, f32[328,128]{1,0:T(8,128)S(1)}, u32[]{:S(2)}, u32[]{:S(2)}) collective-permute-start(f32[328,128]{1,0:T(8,128)S(1)} %collective-permute-done.7.refs_3_), channel_id=1, source_target_pairs={{0,1},{1,0},{2,3},{3,2},{4,5},{5,4},{6,7},{7,6},{8,9},{9,8},{10,11... | collective-permute-start | bytes 503816 | tf_op jit(solution)/shard_map/ppermute | solution.py:315
  63.8 2.7 %collective-permute-start.6 = (f32[328,128]{1,0:T(8,128)S(1)}, f32[328,128]{1,0:T(8,128)S(1)}, u32[]{:S(2)}, u32[]{:S(2)}) collective-permute-start(f32[328,128]{1,0:T(8,128)S(1)} %collective-permute-done.5.refs_3_), channel_id=1, source_target_pairs={{0,1},{1,0},{2,3},{3,2},{4,5},{5,4},{6,7},{7,6},{8,9},{9,8},{10,11... | collective-permute-start | bytes 503816 | tf_op jit(solution)/shard_map/ppermute | solution.py:315

commit v3 on v2

--- a/solution.py
+++ b/solution.py
@@ -38,10 +38,6 @@
             visit(i)
     else:
         pl.loop(0, count)(visit)
-
-
-def whole(shape):
-    return pl.BlockSpec(shape, lambda *_: (0,) * len(shape))
 
 
 def total_of(values):
@@ -117,21 +113,51 @@
         gram = pair_nt(start[0:b], start[0:b])
         edge = pair_nt(start[b:], start)
         hold = pack.at[lax.rem(layer, 2)]
-        hold[0:a, :] = gram[0:a, 0:a]
+        down, across = grid_of(LANES)
+        t11 = gram[a:b, a:b]
+        hold[0:a, :] = jnp.where(down >= across, gram[0:a, 0:a], t11)
         hold[a:b, :] = gram[0:a, a:b]
-        hold[b : b + a, :] = gram[a:b, a:b]
-        at = b + a
-        hold[at : at + tail, :] = edge[:, 0:a]
-        hold[at + tail : at + 2 * tail, :] = edge[:, a:b]
-        spot = lax.broadcasted_iota(jnp.int32, (tail, LANES), 1)
-        extra = jnp.where(spot == 64, squares, 0.0) + jnp.where(spot == 65, guess, 0.0)
-        hold[at + 2 * tail :, :] = extra
-        hold[at + 2 * tail :, 0:tail] = edge[:, b:]
+        hold[b : b + tail, :] = edge[:, 0:a]
+        hold[b + tail : b + 2 * tail, :] = edge[:, a:b]
+        at = b + 2 * tail
+        small = tail * tail // LANES
+        lay_corner(hold, at, edge[:, b:])
+        diagonal = jnp.sum(jnp.where(down == across, t11, 0.0), axis=0, keepdims=True)
+        row, spot = lax.broadcasted_iota(jnp.int32, (8, LANES), 0), lax.broadcasted_iota(jnp.int32, (8, LANES), 1)
+        extra = jnp.where(spot == 0, squares, jnp.where(spot == 1, guess, 0.0))
+        hold[at + small :, :] = jnp.where(row == 0, diagonal, extra)
         half = pack.shape[1] // 2
         keep_ref[layer ^ chip] = hold[pl.ds(pl.multiple_of(core * half, 8), half), :]
         send_ref[layer ^ chip] = hold[pl.ds(pl.multiple_of((1 - core) * half, 8), half), :]
 
     over(layers, visit)
+
+
+def grid_of(size):
+    return lax.broadcasted_iota(jnp.int32, (size, size), 0), lax.broadcasted_iota(jnp.int32, (size, size), 1)
+
+
+def packed_rows(tail):
+    return 2 * LANES + 2 * tail + tail * tail // LANES + 8
+
+
+def lay_corner(hold, at, block):
+    tail = block.shape[1]
+    small = tail * tail // LANES
+    for i in range(LANES // tail):
+        hold[at : at + small, i * tail : (i + 1) * tail] = block[i * small : (i + 1) * small]
+
+
+def read_corner(block, tail):
+    return jnp.concatenate([block[:, i * tail : (i + 1) * tail] for i in range(LANES // tail)], axis=0)
+
+
+def half_of(ref, core, half, align=8):
+    return ref.at[pl.ds(pl.multiple_of(core * half, align), half)]
+
+
+def sent_rows(tail):
+    return -(-3 * packed_rows(tail) // 32) * 32
 
 
 def split(value):
@@ -159,20 +185,25 @@
     return dot(left[:, :b], high[:b]) + dot(left[:, :b], low[:b]) + dot(ends, rest)
 
 
-def newton_kernel(owners, width, scal_ref, own_ref, other_ref, mine_ref, theirs_ref, pack, full):
-    core = scal_ref[1]
+def newton_kernel(owners, width, own_ref, other_ref, mine_ref, theirs_ref, pack, skew, full):
+    core = lax.axis_index("dp") & 1
     half = own_ref.shape[0]
     pack[pl.ds(pl.multiple_of(core * half, 8), half), :] = own_ref[...]
     pack[pl.ds(pl.multiple_of((1 - core) * half, 8), half), :] = other_ref[...]
     tail = width - 2 * LANES
     a, b = LANES, 2 * LANES
-    at = b + a
-    t00, t01, t11 = pack[0:a, :], pack[a:b, :], pack[b:at, :]
-    t20, t21 = pack[at : at + tail, :], pack[at + tail : at + 2 * tail, :]
-    last = pack[at + 2 * tail :, :]
-    t22 = last[:, 0:tail]
-    squares = last[0:1, 64:65]
-    guess = last[0:1, 65:66] * (1.0 / owners)
+    merged, t01 = pack[0:a, :], pack[a:b, :]
+    t20, t21 = pack[b : b + tail, :], pack[b + tail : b + 2 * tail, :]
+    at = b + 2 * tail
+    small = tail * tail // LANES
+    t22 = read_corner(pack[at : at + small, :], tail)
+    extra = pack[at + small :, :]
+    down, across = grid_of(LANES)
+    flipped = merged.T
+    t00 = jnp.where(down >= across, merged, flipped)
+    t11 = jnp.where(down == across, extra[0:1, :], jnp.where(down < across, merged, flipped))
+    squares = extra[1:2, 0:1]
+    guess = extra[1:2, 1:2] * (1.0 / owners)
     ratio = (jnp.sqrt(guess) + 1e-07) / (jnp.sqrt(squares) + 1e-07)
     gram = jnp.concatenate(
         [
@@ -202,62 +233,113 @@
             prod = ratio * (jnp.where(rows == cols, ca, 0.0) + mix32)
         else:
             prod = ca * prod + wide_right(mix, prod)
-    full[0:width, :] = prod[:, 0:a]
-    full[width : 2 * width, :] = prod[:, a:b]
-    group = width * tail // LANES
-    for i in range(LANES // tail):
-        full[2 * width : 2 * width + group, i * tail : (i + 1) * tail] = prod[i * group : (i + 1) * group, b:]
-    full[2 * width + group :, :] = jnp.broadcast_to(mean_sq, (8, LANES))
+    p00, p11 = prod[0:a, 0:a], prod[a:b, a:b]
+    back00, back11 = p00.T, p11.T
+    p01, back10 = prod[0:a, a:b], prod[a:b, 0:a].T
+    p2, back2 = prod[b:, 0:b], prod[0:b, b:].T
+    p22 = prod[b:, b:]
+    lower = down >= across
+    for ref, sign in ((pack, 1.0), (skew, -1.0)):
+        ref[0:a, :] = 0.5 * jnp.where(lower, p00 + sign * back00, p11 + sign * back11)
+        ref[a:b, :] = 0.5 * (p01 + sign * back10)
+        edge = 0.5 * (p2 + sign * back2)
+        ref[b : b + tail, :] = edge[:, 0:a]
+        ref[b + tail : at, :] = edge[:, a:b]
+        lay_corner(ref, at, p22 if ref is pack else jnp.zeros_like(p22))
+    diagonal = jnp.sum(jnp.where(down == across, p11, 0.0), axis=0, keepdims=True)
+    first = lax.broadcasted_iota(jnp.int32, (8, LANES), 0) == 0
+    pack[at + small :, :] = jnp.where(first, diagonal, mean_sq)
+    skew[at + small :, :] = jnp.zeros((8, LANES), F32)
+    rows = pack.shape[0]
+    high, low = split(pack[...])
+    full[0:rows, :] = high
+    full[rows : 2 * rows, :] = low
+    full[2 * rows : 3 * rows, :] = skew[...].astype(BF16)
+    if full.shape[0] > 3 * rows:
+        full[3 * rows :, :] = jnp.zeros((full.shape[0] - 3 * rows, LANES), BF16)
     half = mine_ref.shape[0]
-    mine_ref[...] = full[pl.ds(pl.multiple_of(core * half, 8), half), :]
-    theirs_ref[...] = full[pl.ds(pl.multiple_of((1 - core) * half, 8), half), :]
-
-
-def update_kernel(scale, width, rel, final, *refs):
-    scal_ref, owner_ref, start_ref, mine_ref, other_ref = refs[:5]
-    if rel == 0:
-        out_ref, means_out, slot_ref, full = refs[5:]
-    else:
-        means_ref, _, out_ref, means_out, slot_ref, full = refs[5:]
-    core = scal_ref[1]
-    layer = scal_ref[0] ^ rel
-    half = mine_ref.shape[0]
-    full[pl.ds(pl.multiple_of(core * half, 8), half), :] = mine_ref[...]
-    full[pl.ds(pl.multiple_of((1 - core) * half, 8), half), :] = other_ref[...]
+    mine_ref[...] = half_of(full, core, half, 16)[...]
+    theirs_ref[...] = half_of(full, 1 - core, half, 16)[...]
+
+
+def update_kernel(scale, width, group, last, *refs):
+    owner_ref, start_ref = refs[:2]
+    products = refs[2 : 2 + 2 * len(group)]
+    refs = refs[2 + 2 * len(group) :]
+    means = None
+    if group[0]:
+        means = refs[0][...]
+        refs = refs[2:]
+    slot_ref = None
+    if last:
+        slot_ref, refs = refs[2], refs[:2] + refs[3:]
+    out_ref, means_out, fulls, values, sems = refs
+    place = lax.axis_index("dp")
+    chip, core = place >> 1, place & 1
     tail = width - 2 * LANES
     b = 2 * LANES
-    group = width * tail // LANES
-    main = jnp.concatenate([full[0:width, :], full[width : 2 * width, :]], axis=1)
-    ends = full[2 * width : 2 * width + group, :]
-    ends = jnp.concatenate([ends[:, i * tail : (i + 1) * tail] for i in range(LANES // tail)], axis=0)
-    high, low = split(main)
-    end_high, end_low = split(ends)
-    start = start_ref[0]
-    rest = jnp.concatenate([start[b:], start[b:]], axis=0)
-    value = dot(high, start[:b]) + dot(low, start[:b])
-    value = value + dot(jnp.concatenate([end_high, end_low], axis=1), rest)
-    out_ref[0] = (value * scale).astype(BF16)
+    down, across = grid_of(LANES)
     lane = lax.broadcasted_iota(jnp.int32, means_out.shape, 1)
-    means = jnp.where(lane == layer, full[2 * width + group :, :], 0.0)
-    if rel:
-        means = means + means_ref[...]
+    copies = []
+    for i, rel in enumerate(group):
+        layer = chip ^ rel
+        mine_ref, other_ref = products[2 * i : 2 * i + 2]
+        full = fulls.at[i]
+        half = mine_ref.shape[0]
+        half_of(full, core, half, 16)[...] = mine_ref[...]
+        half_of(full, 1 - core, half, 16)[...] = other_ref[...]
+        size = packed_rows(tail)
+        even = full[0:size, :].astype(F32) + full[size : 2 * size, :].astype(F32)
+        odd = full[2 * size : 3 * size, :].astype(F32)
+        plus, minus = even + odd, even - odd
+        at = b + 2 * tail
+        small = tail * tail // LANES
+        extra = even[at + small :]
+        turned = minus[0:LANES].T
+        p00 = jnp.where(down >= across, plus[0:LANES], turned)
+        p11 = jnp.where(
+            down == across, extra[0:1], jnp.where(down < across, plus[0:LANES], turned)
+        )
+        p10 = minus[LANES:b].T
+        main = jnp.concatenate(
+            [
+                jnp.concatenate([p00, plus[LANES:b]], axis=1),
+                jnp.concatenate([p10, p11], axis=1),
+                jnp.concatenate([plus[b : b + tail], plus[b + tail : at]], axis=1),
+            ],
+            axis=0,
+        )
+        ends = jnp.concatenate(
+            [minus[b : b + tail].T, minus[b + tail : at].T, read_corner(even[at : at + small], tail)],
+            axis=0,
+        )
+        high, low = split(main)
+        end_high, end_low = split(ends)
+        start = start_ref[layer]
+        rest = jnp.concatenate([start[b:], start[b:]], axis=0)
+        value = dot(high, start[:b]) + dot(low, start[:b])
+        value = value + dot(jnp.concatenate([end_high, end_low], axis=1), rest)
+        values[i] = (value * scale).astype(BF16)
+        copies.append(
+            pltpu.make_async_copy(values.at[i], out_ref.at[layer], sems.at[i])
+        )
+        copies[-1].start()
+        found = jnp.where(lane == layer, extra[1:2], 0.0)
+        means = found if means is None else means + found
     means_out[...] = means
-    if not final:
+    if last:
         for slot in range(MAXOWN):
-            slot_ref[0, slot] = 0.0
-        return
-    layers = owner_ref.shape[1]
-    me = scal_ref[3]
-    for slot in range(MAXOWN):
-
-        def visit(j, carry):
-            seen, at = carry
-            hit = owner_ref[0, j] == me
-            at = jnp.where(hit & (seen == slot), j, at)
-            return seen + jnp.where(hit, 1, 0), at
-
-        _, at = lax.fori_loop(0, layers, visit, (jnp.int32(0), jnp.int32(-1)))
-        slot_ref[0, slot] = jnp.sum(jnp.where(lane[0:1] == at, means[0:1], 0.0))
+
+            def visit(j, carry):
+                seen, at = carry
+                hit = owner_ref[0, j] == place
+                at = jnp.where(hit & (seen == slot), j, at)
+                return seen + jnp.where(hit, 1, 0), at
+
+            _, at = lax.fori_loop(0, owner_ref.shape[1], visit, (jnp.int32(0), jnp.int32(-1)))
+            slot_ref[0, slot] = jnp.sum(jnp.where(lane[0:1] == at, means[0:1], 0.0))
+    for copy in copies:
+        copy.wait()
 
 
 def step(momentum, gradient, assignment):
@@ -271,9 +353,6 @@
     entries = everyone * layers * rows * width
     mom = jnp.swapaxes(momentum[0], 1, 2)
     grad = jnp.swapaxes(gradient[0], 1, 2)
-    place = lax.axis_index("dp")
-    scal = jnp.stack([place >> 1, place & 1, lax.axis_index("section"), place]).astype(jnp.int32)
-
     anywhere = pl.BlockSpec(memory_space=pl.ANY)
     near_by = pl.BlockSpec(memory_space=pltpu.VMEM)
     sums, grad_near, mom_near = pl.pallas_call(
@@ -294,7 +373,7 @@
     )(pltpu.with_memory_space_constraint(grad, pltpu.HBM), pltpu.with_memory_space_constraint(mom, pltpu.HBM))
     sums = lax.all_to_all(sums, ("section", "dp"), 0, 0, tiled=True)
 
-    packed = 3 * LANES + 3 * tail
+    packed = packed_rows(tail)
     half = packed // 2
     start, keep, send, factor = pl.pallas_call(
         functools.partial(start_kernel, layers, entries, owners),
@@ -322,70 +401,67 @@
     own, fresh = lax.optimization_barrier((own, fresh))
     other = turn(own, 1)
 
-    full_rows = 2 * width + width * tail // LANES + 8
+    full_rows = sent_rows(tail)
     piece = full_rows // 2
     mine, theirs = pl.pallas_call(
         functools.partial(newton_kernel, owners, width),
-        grid_spec=pltpu.PrefetchScalarGridSpec(
-            num_scalar_prefetch=1,
-            grid=(1,),
-            in_specs=[whole((half, LANES)), whole((half, LANES))],
-            out_specs=[whole((piece, LANES)), whole((piece, LANES))],
-            scratch_shapes=[pltpu.VMEM((packed, LANES), F32), pltpu.VMEM((full_rows, LANES), F32)],
-        ),
-        out_shape=[jax.ShapeDtypeStruct((piece, LANES), F32)] * 2,
+        in_specs=[near_by] * 2,
+        out_specs=[near_by] * 2,
+        out_shape=[jax.ShapeDtypeStruct((piece, LANES), BF16)] * 2,
+        scratch_shapes=[
+            pltpu.VMEM((packed, LANES), F32),
+            pltpu.VMEM((packed, LANES), F32),
+            pltpu.VMEM((full_rows, LANES), BF16),
+        ],
         compiler_params=params(),
         name="newton",
-    )(scal, own, other)
-
+    )(own, other)
+
+    arriving = {}
+    for k in range(1, chips):
+        arriving[k] = turn(mine, 2 * k)
     update = means = slots = None
     flops = 4 * width * width * rows
-    for rel in range(chips):
-        if rel:
-            near = arriving[rel]
-            if rel < chips - 1:
-                near, update = lax.optimization_barrier((near, update))
-            far = turn(near, 1)
+    groups = [(0,), (1,)] + [tuple(range(k, min(k + 2, chips))) for k in range(2, chips, 2)]
+    for group in groups:
+        last = group[-1] == chips - 1
+        operands = [assignment, start]
+        if group[0]:
+            nears, update = lax.optimization_barrier(([arriving[rel] for rel in group], update))
+            for near in nears:
+                operands += [near, turn(near, 1)]
         else:
-            arriving = {}
-            for k in range(1, chips):
-                arriving[k] = turn(mine, 2 * k)
-            near, far = mine, theirs
-        pick = pl.BlockSpec((1, width, rows), lambda k, s, _, rel=rel: (s[0] ^ rel, 0, 0))
-        operands = [scal, assignment, start, near, far]
-        in_specs = [pick, whole((piece, LANES)), whole((piece, LANES))]
+            operands += [mine, theirs]
+        in_specs = [pl.BlockSpec(memory_space=pltpu.SMEM)] + [near_by] * (len(operands) - 1)
         aliases = {}
-        if rel:
+        if group[0]:
+            aliases = {len(operands) + 1: 0}
             operands += [means, update]
-            in_specs += [whole((8, LANES)), pl.BlockSpec(memory_space=pl.ANY)]
-            aliases = {6: 0}
+            in_specs += [near_by, pl.BlockSpec(memory_space=pl.ANY)]
         call = pl.pallas_call(
-            functools.partial(
-                update_kernel, math.sqrt(owners * rows), width, rel, rel == chips - 1
-            ),
-            grid_spec=pltpu.PrefetchScalarGridSpec(
-                num_scalar_prefetch=2,
-                grid=(1,),
-                in_specs=in_specs,
-                out_specs=[
-                    pick,
-                    whole((8, LANES)),
-                    pl.BlockSpec((1, MAXOWN), lambda *_: (0, 0), memory_space=pltpu.SMEM),
-                ],
-                scratch_shapes=[pltpu.VMEM((full_rows, LANES), F32)],
-            ),
+            functools.partial(update_kernel, math.sqrt(owners * rows), width, group, last),
+            in_specs=in_specs,
+            out_specs=[pl.BlockSpec(memory_space=pl.ANY), near_by]
+            + [pl.BlockSpec(memory_space=pltpu.SMEM)] * last,
             out_shape=[
                 jax.ShapeDtypeStruct((layers, width, rows), BF16),
                 jax.ShapeDtypeStruct((8, LANES), F32),
-                jax.ShapeDtypeStruct((1, MAXOWN), F32),
+            ]
+            + [jax.ShapeDtypeStruct((1, MAXOWN), F32)] * last,
+            scratch_shapes=[
+                pltpu.VMEM((len(group), full_rows, LANES), BF16),
+                pltpu.VMEM((len(group), width, rows), BF16),
+                pltpu.SemaphoreType.DMA((len(group),)),
             ],
             input_output_aliases=aliases,
             compiler_params=params(),
-            cost_estimate=cost(flops, 4 * width * rows + 8 * piece * LANES),
+            cost_estimate=cost(
+                len(group) * flops, len(group) * (4 * width * rows + 4 * piece * LANES)
+            ),
             name="update",
         )
-        update, means, slots = call(*operands)
-    return (jnp.swapaxes(fresh, 1, 2)[None], jnp.swapaxes(update, 1, 2)[None], slots)
+        update, means, *slots = call(*operands)
+    return (jnp.swapaxes(fresh, 1, 2)[None], jnp.swapaxes(update, 1, 2)[None], slots[0])
 
 
 def solution(mesh):

time: 68.9 us -> 61.2 us (0.89)
  waiting for transfers between devices: 18.9 us -> 12.5 us
  Pallas kernels: 17.3 us -> 15.7 us
    ppermute x11, waiting for transfers between devices: 18.9 us -> 12.5 us  [turn(): return lax.ppermute(value, 'dp', [(i, i ^ by) for i in range(owners)])]
    pallas_call x5 -> x4, Pallas kernels: 12.7 us -> 11.5 us  [the longest x3 6.21 us: step(): update, means, *slots = call(*operands)]
  transfers between devices with their start and end apart: 11 -> 11, of which waited for: 6 -> 7; matrix products, arithmetic and copies ran while one was open for 4% -> 5% of each run, Pallas kernels for 7% -> 6%
where the time goes in v3:
time: 61.2 us; the launch traced here: 60.6 us
  Pallas kernels  15.7 us (26%)
  starting transfers between devices  14.9 us (24%)
  blocking collectives  13.7 us (22%)
  waiting for transfers between devices  12.5 us (20%)
  other arithmetic  2.55 us (4%)
  between operations  0.68 us (1%)
    ppermute x11, starting transfers between devices, turn(): return lax.ppermute(value, 'dp', [(i, i ^ by) for i in range(owners)])  14.9 us
    all_to_all x1, blocking collectives, step(): sums = lax.all_to_all(sums, ('section', 'dp'), 0, 0, tiled=True)  13.7 us
    ppermute x11, waiting for transfers between devices, turn(): return lax.ppermute(value, 'dp', [(i, i ^ by) for i in range(owners)])  12.5 us
    pallas_call x3, Pallas kernels, step(): update, means, *slots = call(*operands)  6.21 us
    pallas_call x1, Pallas kernels, step(): pl.pallas_call(functools.partial(newton_kernel, owners, width), in_specs=...  5.28 us
    add x1, other arithmetic, step(): fresh = momentum_decay * mom_near + factor[0, 0] * grad_near.astype(F32)  2.47 us
    pallas_call x1, Pallas kernels, step(): pl.pallas_call(functools.partial(sums_kernel, layers), in_specs=[anywhere...  2.31 us
    pallas_call x1, Pallas kernels, step(): pl.pallas_call(functools.partial(start_kernel, layers, entries, owners),...  1.89 us
  transfers between devices with their start and end apart: 11, of which 7 were waited for; matrix products, arithmetic and copies ran while one was open for 5% of the time, Pallas kernels for 6%

profile of v3, /device:TPU:1, one launch (start us, length us, event | category | flops | bytes accessed | tf_op | source)
XLA Modules:
  0.0 60.6 jit_solution(17273992818876748395)
XLA Ops:
  0.6 2.3 %sums.1 = (f32[32,128]{1,0:T(8,128)S(1)}, bf16[4,288,448]{2,1,0:T(8,128)(2,1)S(1)}, f32[4,288,448]{2,1,0:T(8,128)S(1)}) custom-call(bf16[4,288,448]{2,1,0:T(8,128)(2,1)} %bitcast.36, f32[4,288,448]{2,1,0:T(8,128)} %bitcast.35), custom_call_target="tpu_custom_call" | custom-call | tf_op jit(solution)/shard_map/sums/pallas_call | solution.py:358
  3.0 13.7 %all_to_all.11 = f32[32,1,128]{2,1,0:T(1,128)S(1)} all-to-all(f32[32,1,128]{2,1,0:T(1,128)S(1)} %bitcast.32), channel_id=1, replica_groups=mesh['section'=4,'dp'=8] {'section','dp'}, dimensions={0} | all-to-all | bytes 32768 | tf_op jit(solution)/shard_map/all_to_all | solution.py:374
  16.6 1.9 %start.1 = (bf16[4,288,448]{2,1,0:T(8,128)(2,1)S(1)}, f32[4,168,128]{2,1,0:T(8,128)S(1)}, f32[4,168,128]{2,1,0:T(8,128)S(1)}, f32[8,128]{1,0:T(8,128)S(1)}) custom-call(f32[32,128]{1,0:T(8,128)S(1)} %bitcast.31, bf16[4,288,448]{2,1,0:T(8,128)(2,1)S(1)} %get-tuple-element.26.grad_ref, f32[4,288,448]{2,1,0:T(8,128)S(1)} %get-tuple-element.27.mom_ref), custom_call_target="tpu_custom_call" | custom-call | tf_op jit(solution)/shard_map/start/pallas_call | solution.py:378
  18.5 0.7 %collective-permute-start = (f32[4,168,128]{2,1,0:T(8,128)S(1)}, f32[4,168,128]{2,1,0:T(8,128)S(1)}, u32[]{:S(2)}, u32[]{:S(2)}) collective-permute-start(f32[4,168,128]{2,1,0:T(8,128)S(1)} %get-tuple-element.29), channel_id=1, source_target_pairs={{0,1},{1,0},{2,3},{3,2},{4,5},{5,4},{6,7},{7,6},{8,9},{9,8},{10,11... | collective-permute-start | bytes 1032200 | tf_op jit(solution)/shard_map/ppermute | solution.py:394
  19.2 0.5 slice.19
  19.7 0.8 %collective-permute-done = f32[4,168,128]{2,1,0:T(8,128)S(1)} collective-permute-done((f32[4,168,128]{2,1,0:T(8,128)S(1)}, f32[4,168,128]{2,1,0:T(8,128)S(1)}, u32[]{:S(2)}, u32[]{:S(2)}) %collective-permute-start) | collective-permute-done | bytes 344096 | tf_op jit(solution)/shard_map/ppermute | solution.py:394
  20.6 0.3 collective-permute-start.1
  20.9 0.3 collective-permute-start.2
  21.2 3.0 %collective-permute-start.3 = (f32[168,128]{1,0:T(8,128)S(1)}, f32[168,128]{1,0:T(8,128)S(1)}, u32[]{:S(2)}, u32[]{:S(2)}) collective-permute-start(f32[168,128]{1,0:T(8,128)S(1)} %get-tuple-element.48), channel_id=1, source_target_pairs={{0,6},{1,7},{2,4},{3,5},{4,2},{5,3},{6,0},{7,1},{8,14},{9,15},{10,... | collective-permute-start | bytes 258056 | tf_op jit(solution)/shard_map/ppermute | solution.py:394
  24.2 0.0 copy-start
  24.2 2.5 %multiply_add_fusion = f32[4,288,448]{2,1,0:T(8,128)} fusion(bf16[4,288,448]{2,1,0:T(8,128)(2,1)S(1)} %get-tuple-element.26.grad_ref, f32[4,288,448]{2,1,0:T(8,128)S(1)} %get-tuple-element.27.mom_ref, f32[]{:T(128)} %bitcast.11), kind=kLoop, calls=%fused_computation | loop fusion | flops 2064384 | bytes 5160964 | tf_op jit(solution)/shard_map/add | solution.py:400
  26.7 0.0 collective-permute-done.1
  26.7 0.0 collective-permute-done.2
  26.7 1.2 %collective-permute-done.3 = f32[168,128]{1,0:T(8,128)S(1)} collective-permute-done((f32[168,128]{1,0:T(8,128)S(1)}, f32[168,128]{1,0:T(8,128)S(1)}, u32[]{:S(2)}, u32[]{:S(2)}) %collective-permute-start.3) | collective-permute-done | bytes 86048 | tf_op jit(solution)/shard_map/ppermute | solution.py:394
  27.9 3.6 %collective-permute-start.4 = (f32[168,128]{1,0:T(8,128)S(1)}, f32[168,128]{1,0:T(8,128)S(1)}, u32[]{:S(2)}, u32[]{:S(2)}) collective-permute-start(f32[168,128]{1,0:T(8,128)S(1)} %fusion.2.own_ref), channel_id=1, source_target_pairs={{0,1},{1,0},{2,3},{3,2},{4,5},{5,4},{6,7},{7,6},{8,9},{9,8},{10,11... | collective-permute-start | bytes 258056 | tf_op jit(solution)/shard_map/ppermute | solution.py:394
  31.4 0.9 %collective-permute-done.4.other_ref = f32[168,128]{1,0:T(8,128)S(1)} collective-permute-done((f32[168,128]{1,0:T(8,128)S(1)}, f32[168,128]{1,0:T(8,128)S(1)}, u32[]{:S(2)}, u32[]{:S(2)}) %collective-permute-start.4) | collective-permute-done | bytes 86048 | tf_op jit(solution)/shard_map/ppermute | solution.py:394
  32.4 5.3 %newton.1 = (bf16[512,128]{1,0:T(8,128)(2,1)S(1)}, bf16[512,128]{1,0:T(8,128)(2,1)S(1)}) custom-call(f32[168,128]{1,0:T(8,128)S(1)} %fusion.2.own_ref, f32[168,128]{1,0:T(8,128)S(1)} %collective-permute-done.4.other_ref), custom_call_target="tpu_custom_call" | custom-call | tf_op jit(solution)/shard_map/newton/pallas_call | solution.py:406
  37.7 1.3 %collective-permute-start.7 = (bf16[512,128]{1,0:T(8,128)(2,1)S(1)}, bf16[512,128]{1,0:T(8,128)(2,1)S(1)}, u32[]{:S(2)}, u32[]{:S(2)}) collective-permute-start(bf16[512,128]{1,0:T(8,128)(2,1)S(1)} %get-tuple-element.34.refs_2_), channel_id=1, source_target_pairs={{0,2},{1,3},{2,0},{3,1},{4,6},{5,7},{6,4},{7,5},{8,10},{9,11},{10,... | collective-permute-start | bytes 393224 | tf_op jit(solution)/shard_map/ppermute | solution.py:394
  38.9 0.0 copy-done
  38.9 1.8 %update.3 = (bf16[4,288,448]{2,1,0:T(8,128)(2,1)}, f32[8,128]{1,0:T(8,128)S(1)}) custom-call(s32[1,4]{1,0:T(1,128)S(1)} %copy-done, bf16[4,288,448]{2,1,0:T(8,128)(2,1)S(1)} %get-tuple-element.32.refs_1_, bf16[512,128]{1,0:T(8,128)(2,1)S(1)} %get-tuple-element.34.refs_2_, bf16[512,128]{1,0:T(8,128)(2,1)S(1)} %get-tuple-element.35.refs_3_), custom_call_target="tpu_custom_call" | custom-call | flops 148635648 | bytes 778240 | tf_op jit(solution)/shard_map/update/pallas_call | solution.py:463
  40.7 1.7 %collective-permute-done.7.refs_2_ = bf16[512,128]{1,0:T(8,128)(2,1)S(1)} collective-permute-done((bf16[512,128]{1,0:T(8,128)(2,1)S(1)}, bf16[512,128]{1,0:T(8,128)(2,1)S(1)}, u32[]{:S(2)}, u32[]{:S(2)}) %collective-permute-start.7) | collective-permute-done | bytes 131104 | tf_op jit(solution)/shard_map/ppermute | solution.py:394
  42.4 1.2 %collective-permute-start.8 = (bf16[512,128]{1,0:T(8,128)(2,1)S(1)}, bf16[512,128]{1,0:T(8,128)(2,1)S(1)}, u32[]{:S(2)}, u32[]{:S(2)}) collective-permute-start(bf16[512,128]{1,0:T(8,128)(2,1)S(1)} %collective-permute-done.7.refs_2_), channel_id=1, source_target_pairs={{0,1},{1,0},{2,3},{3,2},{4,5},{5,4},{6,7},{7,6},{8,9},{9,8},{10,11... | collective-permute-start | bytes 393224 | tf_op jit(solution)/shard_map/ppermute | solution.py:394
  43.6 1.2 %collective-permute-start.5 = (bf16[512,128]{1,0:T(8,128)(2,1)S(1)}, bf16[512,128]{1,0:T(8,128)(2,1)S(1)}, u32[]{:S(2)}, u32[]{:S(2)}) collective-permute-start(bf16[512,128]{1,0:T(8,128)(2,1)S(1)} %get-tuple-element.34.refs_2_), channel_id=1, source_target_pairs={{0,4},{1,5},{2,6},{3,7},{4,0},{5,1},{6,2},{7,3},{8,12},{9,13},{10,... | collective-permute-start | bytes 393224 | tf_op jit(solution)/shard_map/ppermute | solution.py:394
  44.8 2.1 %collective-permute-start.6 = (bf16[512,128]{1,0:T(8,128)(2,1)S(1)}, bf16[512,128]{1,0:T(8,128)(2,1)S(1)}, u32[]{:S(2)}, u32[]{:S(2)}) collective-permute-start(bf16[512,128]{1,0:T(8,128)(2,1)S(1)} %get-tuple-element.34.refs_2_), channel_id=1, source_target_pairs={{0,6},{1,7},{2,4},{3,5},{4,2},{5,3},{6,0},{7,1},{8,14},{9,15},{10,... | collective-permute-start | bytes 393224 | tf_op jit(solution)/shard_map/ppermute | solution.py:394
  46.9 0.0 collective-permute-done.8.refs_3_
  46.9 1.8 %update.4 = (bf16[4,288,448]{2,1,0:T(8,128)(2,1)}, f32[8,128]{1,0:T(8,128)S(1)}) custom-call(s32[1,4]{1,0:T(1,128)S(1)} %copy-done, bf16[4,288,448]{2,1,0:T(8,128)(2,1)S(1)} %get-tuple-element.32.refs_1_, bf16[512,128]{1,0:T(8,128)(2,1)S(1)} %collective-permute-done.7.refs_2_, ...), custom_call_target="tpu_custom_call", output_to_operand_aliasing={{0}: (5, {})} | custom-call | flops 148635648 | bytes 778240 | tf_op jit(solution)/shard_map/update/pallas_call | solution.py:463
  48.7 6.5 %collective-permute-done.5.refs_2_ = bf16[512,128]{1,0:T(8,128)(2,1)S(1)} collective-permute-done((bf16[512,128]{1,0:T(8,128)(2,1)S(1)}, bf16[512,128]{1,0:T(8,128)(2,1)S(1)}, u32[]{:S(2)}, u32[]{:S(2)}) %collective-permute-start.5) | collective-permute-done | bytes 131104 | tf_op jit(solution)/shard_map/ppermute | solution.py:394
  55.2 0.0 collective-permute-done.6.refs_4_
  55.2 1.3 %collective-permute-start.10 = (bf16[512,128]{1,0:T(8,128)(2,1)S(1)}, bf16[512,128]{1,0:T(8,128)(2,1)S(1)}, u32[]{:S(2)}, u32[]{:S(2)}) collective-permute-start(bf16[512,128]{1,0:T(8,128)(2,1)S(1)} %collective-permute-done.6.refs_4_), channel_id=1, source_target_pairs={{0,1},{1,0},{2,3},{3,2},{4,5},{5,4},{6,7},{7,6},{8,9},{9,8},{10,11... | collective-permute-start | bytes 393224 | tf_op jit(solution)/shard_map/ppermute | solution.py:394
  56.5 0.0 collective-permute-start.9
  56.5 1.0 %collective-permute-done.10.refs_5_ = bf16[512,128]{1,0:T(8,128)(2,1)S(1)} collective-permute-done((bf16[512,128]{1,0:T(8,128)(2,1)S(1)}, bf16[512,128]{1,0:T(8,128)(2,1)S(1)}, u32[]{:S(2)}, u32[]{:S(2)}) %collective-permute-start.10) | collective-permute-done | bytes 131104 | tf_op jit(solution)/shard_map/ppermute | solution.py:394
  57.5 0.4 collective-permute-done.9.refs_3_
  57.9 2.7 %update.5 = (bf16[4,288,448]{2,1,0:T(8,128)(2,1)}, f32[8,128]{1,0:T(8,128)}, f32[1,2]{1,0:T(1,128)}) custom-call(s32[1,4]{1,0:T(1,128)S(1)} %copy-done, bf16[4,288,448]{2,1,0:T(8,128)(2,1)S(1)} %get-tuple-element.32.refs_1_, bf16[512,128]{1,0:T(8,128)(2,1)S(1)} %collective-permute-done.5.refs_2_, ...), custom_call_target="tpu_custom_call", output_to_operand_aliasing={{0}: (7, {})} | custom-call | flops 297271296 | bytes 1556480 | tf_op jit(solution)/shard_map/update/pallas_call | solution.py:463
  (3 shorter events, 0.1 us)
Async XLA Ops:
  18.5 2.0 %collective-permute-start = (f32[4,168,128]{2,1,0:T(8,128)S(1)}, f32[4,168,128]{2,1,0:T(8,128)S(1)}, u32[]{:S(2)}, u32[]{:S(2)}) collective-permute-start(f32[4,168,128]{2,1,0:T(8,128)S(1)} %get-tuple-element.29), channel_id=1, source_target_pairs={{0,1},{1,0},{2,3},{3,2},{4,5},{5,4},{6,7},{7,6},{8,9},{9,8},{10,11... | collective-permute-start | bytes 1032200 | tf_op jit(solution)/shard_map/ppermute | solution.py:394
  20.6 6.1 %collective-permute-start.1 = (f32[168,128]{1,0:T(8,128)S(1)}, f32[168,128]{1,0:T(8,128)S(1)}, u32[]{:S(2)}, u32[]{:S(2)}) collective-permute-start(f32[168,128]{1,0:T(8,128)S(1)} %get-tuple-element.47), channel_id=1, source_target_pairs={{0,2},{1,3},{2,0},{3,1},{4,6},{5,7},{6,4},{7,5},{8,10},{9,11},{10,... | collective-permute-start | bytes 258056 | tf_op jit(solution)/shard_map/ppermute | solution.py:394
  20.9 5.8 %collective-permute-start.2 = (f32[168,128]{1,0:T(8,128)S(1)}, f32[168,128]{1,0:T(8,128)S(1)}, u32[]{:S(2)}, u32[]{:S(2)}) collective-permute-start(f32[168,128]{1,0:T(8,128)S(1)} %get-tuple-element.49), channel_id=1, source_target_pairs={{0,4},{1,5},{2,6},{3,7},{4,0},{5,1},{6,2},{7,3},{8,12},{9,13},{10,... | collective-permute-start | bytes 258056 | tf_op jit(solution)/shard_map/ppermute | solution.py:394
  21.2 6.6 %collective-permute-start.3 = (f32[168,128]{1,0:T(8,128)S(1)}, f32[168,128]{1,0:T(8,128)S(1)}, u32[]{:S(2)}, u32[]{:S(2)}) collective-permute-start(f32[168,128]{1,0:T(8,128)S(1)} %get-tuple-element.48), channel_id=1, source_target_pairs={{0,6},{1,7},{2,4},{3,5},{4,2},{5,3},{6,0},{7,1},{8,14},{9,15},{10,... | collective-permute-start | bytes 258056 | tf_op jit(solution)/shard_map/ppermute | solution.py:394
  24.2 14.7 %copy-start = (s32[1,4]{1,0:T(1,128)S(1)}, s32[1,4]{1,0:T(1,128)}, u32[]{:S(2)}) copy-start(s32[1,4]{1,0:T(1,128)} %refs_0_.5) | copy-start | bytes 52
  27.9 4.5 %collective-permute-start.4 = (f32[168,128]{1,0:T(8,128)S(1)}, f32[168,128]{1,0:T(8,128)S(1)}, u32[]{:S(2)}, u32[]{:S(2)}) collective-permute-start(f32[168,128]{1,0:T(8,128)S(1)} %fusion.2.own_ref), channel_id=1, source_target_pairs={{0,1},{1,0},{2,3},{3,2},{4,5},{5,4},{6,7},{7,6},{8,9},{9,8},{10,11... | collective-permute-start | bytes 258056 | tf_op jit(solution)/shard_map/ppermute | solution.py:394
  37.7 4.8 %collective-permute-start.7 = (bf16[512,128]{1,0:T(8,128)(2,1)S(1)}, bf16[512,128]{1,0:T(8,128)(2,1)S(1)}, u32[]{:S(2)}, u32[]{:S(2)}) collective-permute-start(bf16[512,128]{1,0:T(8,128)(2,1)S(1)} %get-tuple-element.34.refs_2_), channel_id=1, source_target_pairs={{0,2},{1,3},{2,0},{3,1},{4,6},{5,7},{6,4},{7,5},{8,10},{9,11},{10,... | collective-permute-start | bytes 393224 | tf_op jit(solution)/shard_map/ppermute | solution.py:394
  42.4 4.5 %collective-permute-start.8 = (bf16[512,128]{1,0:T(8,128)(2,1)S(1)}, bf16[512,128]{1,0:T(8,128)(2,1)S(1)}, u32[]{:S(2)}, u32[]{:S(2)}) collective-permute-start(bf16[512,128]{1,0:T(8,128)(2,1)S(1)} %collective-permute-done.7.refs_2_), channel_id=1, source_target_pairs={{0,1},{1,0},{2,3},{3,2},{4,5},{5,4},{6,7},{7,6},{8,9},{9,8},{10,11... | collective-permute-start | bytes 393224 | tf_op jit(solution)/shard_map/ppermute | solution.py:394
  43.6 11.6 %collective-permute-start.5 = (bf16[512,128]{1,0:T(8,128)(2,1)S(1)}, bf16[512,128]{1,0:T(8,128)(2,1)S(1)}, u32[]{:S(2)}, u32[]{:S(2)}) collective-permute-start(bf16[512,128]{1,0:T(8,128)(2,1)S(1)} %get-tuple-element.34.refs_2_), channel_id=1, source_target_pairs={{0,4},{1,5},{2,6},{3,7},{4,0},{5,1},{6,2},{7,3},{8,12},{9,13},{10,... | collective-permute-start | bytes 393224 | tf_op jit(solution)/shard_map/ppermute | solution.py:394
  44.8 10.4 %collective-permute-start.6 = (bf16[512,128]{1,0:T(8,128)(2,1)S(1)}, bf16[512,128]{1,0:T(8,128)(2,1)S(1)}, u32[]{:S(2)}, u32[]{:S(2)}) collective-permute-start(bf16[512,128]{1,0:T(8,128)(2,1)S(1)} %get-tuple-element.34.refs_2_), channel_id=1, source_target_pairs={{0,6},{1,7},{2,4},{3,5},{4,2},{5,3},{6,0},{7,1},{8,14},{9,15},{10,... | collective-permute-start | bytes 393224 | tf_op jit(solution)/shard_map/ppermute | solution.py:394
  55.2 2.3 %collective-permute-start.10 = (bf16[512,128]{1,0:T(8,128)(2,1)S(1)}, bf16[512,128]{1,0:T(8,128)(2,1)S(1)}, u32[]{:S(2)}, u32[]{:S(2)}) collective-permute-start(bf16[512,128]{1,0:T(8,128)(2,1)S(1)} %collective-permute-done.6.refs_4_), channel_id=1, source_target_pairs={{0,1},{1,0},{2,3},{3,2},{4,5},{5,4},{6,7},{7,6},{8,9},{9,8},{10,11... | collective-permute-start | bytes 393224 | tf_op jit(solution)/shard_map/ppermute | solution.py:394
  56.5 1.3 %collective-permute-start.9 = (bf16[512,128]{1,0:T(8,128)(2,1)S(1)}, bf16[512,128]{1,0:T(8,128)(2,1)S(1)}, u32[]{:S(2)}, u32[]{:S(2)}) collective-permute-start(bf16[512,128]{1,0:T(8,128)(2,1)S(1)} %collective-permute-done.5.refs_2_), channel_id=1, source_target_pairs={{0,1},{1,0},{2,3},{3,2},{4,5},{5,4},{6,7},{7,6},{8,9},{9,8},{10,11... | collective-permute-start | bytes 393224 | tf_op jit(solution)/shard_map/ppermute | solution.py:394

commit v4 on v3

--- a/solution.py
+++ b/solution.py
@@ -270,16 +270,16 @@
     if group[0]:
         means = refs[0][...]
         refs = refs[2:]
-    slot_ref = None
     if last:
-        slot_ref, refs = refs[2], refs[:2] + refs[3:]
-    out_ref, means_out, fulls, values, sems = refs
+        out_ref, slot_out, fulls, values, sems, slot_ref, slot_sem = refs
+    else:
+        out_ref, means_out, fulls, values, sems = refs
     place = lax.axis_index("dp")
     chip, core = place >> 1, place & 1
     tail = width - 2 * LANES
     b = 2 * LANES
     down, across = grid_of(LANES)
-    lane = lax.broadcasted_iota(jnp.int32, means_out.shape, 1)
+    lane = lax.broadcasted_iota(jnp.int32, (8, LANES), 1)
     copies = []
     for i, rel in enumerate(group):
         layer = chip ^ rel
@@ -326,8 +326,8 @@
         copies[-1].start()
         found = jnp.where(lane == layer, extra[1:2], 0.0)
         means = found if means is None else means + found
-    means_out[...] = means
     if last:
+        line = jnp.zeros((1, LANES), F32)
         for slot in range(MAXOWN):
 
             def visit(j, carry):
@@ -336,8 +336,16 @@
                 at = jnp.where(hit & (seen == slot), j, at)
                 return seen + jnp.where(hit, 1, 0), at
 
-            _, at = lax.fori_loop(0, owner_ref.shape[1], visit, (jnp.int32(0), jnp.int32(-1)))
-            slot_ref[0, slot] = jnp.sum(jnp.where(lane[0:1] == at, means[0:1], 0.0))
+            _, at = lax.fori_loop(
+                0, owner_ref.shape[1], visit, (jnp.int32(0), jnp.int32(-1)), unroll=owner_ref.shape[1] <= 8
+            )
+            value = jnp.sum(jnp.where(lane[0:1] == at, means[0:1], 0.0), axis=1, keepdims=True)
+            line = jnp.where(lane[0:1] == slot, value, line)
+        slot_ref[...] = line[:, 0:MAXOWN]
+        copies.append(pltpu.make_async_copy(slot_ref, slot_out, slot_sem))
+        copies[-1].start()
+    else:
+        means_out[...] = means
     for copy in copies:
         copy.wait()
 
@@ -420,16 +428,15 @@
     arriving = {}
     for k in range(1, chips):
         arriving[k] = turn(mine, 2 * k)
-    update = means = slots = None
+    update = means = None
     flops = 4 * width * width * rows
-    groups = [(0,), (1,)] + [tuple(range(k, min(k + 2, chips))) for k in range(2, chips, 2)]
-    for group in groups:
-        last = group[-1] == chips - 1
+    for rel in range(chips):
+        group = (rel,)
+        last = rel == chips - 1
         operands = [assignment, start]
         if group[0]:
-            nears, update = lax.optimization_barrier(([arriving[rel] for rel in group], update))
-            for near in nears:
-                operands += [near, turn(near, 1)]
+            near = arriving[rel]
+            operands += [near, turn(near, 1)]
         else:
             operands += [mine, theirs]
         in_specs = [pl.BlockSpec(memory_space=pltpu.SMEM)] + [near_by] * (len(operands) - 1)
@@ -441,18 +448,20 @@
         call = pl.pallas_call(
             functools.partial(update_kernel, math.sqrt(owners * rows), width, group, last),
             in_specs=in_specs,
-            out_specs=[pl.BlockSpec(memory_space=pl.ANY), near_by]
-            + [pl.BlockSpec(memory_space=pltpu.SMEM)] * last,
+            out_specs=[
+                pl.BlockSpec(memory_space=pl.ANY),
+                pl.BlockSpec(memory_space=pl.ANY) if last else near_by,
+            ],
             out_shape=[
                 jax.ShapeDtypeStruct((layers, width, rows), BF16),
-                jax.ShapeDtypeStruct((8, LANES), F32),
-            ]
-            + [jax.ShapeDtypeStruct((1, MAXOWN), F32)] * last,
+                jax.ShapeDtypeStruct((1, MAXOWN) if last else (8, LANES), F32),
+            ],
             scratch_shapes=[
                 pltpu.VMEM((len(group), full_rows, LANES), BF16),
                 pltpu.VMEM((len(group), width, rows), BF16),
                 pltpu.SemaphoreType.DMA((len(group),)),
-            ],
+            ]
+            + [pltpu.VMEM((1, MAXOWN), F32), pltpu.SemaphoreType.DMA] * last,
             input_output_aliases=aliases,
             compiler_params=params(),
             cost_estimate=cost(
@@ -460,8 +469,8 @@
             ),
             name="update",
         )
-        update, means, *slots = call(*operands)
-    return (jnp.swapaxes(fresh, 1, 2)[None], jnp.swapaxes(update, 1, 2)[None], slots[0])
+        update, means = call(*operands)
+    return (jnp.swapaxes(fresh, 1, 2)[None], jnp.swapaxes(update, 1, 2)[None], means)
 
 
 def solution(mesh):

time: 61.2 us -> 60.1 us (0.982)
  waiting for transfers between devices: 12.5 us -> 8.94 us
  starting transfers between devices: 14.9 us -> 16.4 us
  Pallas kernels: 15.7 us -> 16.6 us
    ppermute x11, waiting for transfers between devices: 12.5 us -> 8.94 us  [turn(): return lax.ppermute(value, 'dp', [(i, i ^ by) for i in range(owners)])]
    ppermute x11, starting transfers between devices: 14.9 us -> 16.4 us  [turn(): return lax.ppermute(value, 'dp', [(i, i ^ by) for i in range(owners)])]
    pallas_call x3 -> x4, Pallas kernels: 6.21 us -> 7.09 us  [step(): update, means = call(*operands)]
  transfers between devices with their start and end apart: 11 -> 11, of which waited for: 7 -> 5; matrix products, arithmetic and copies ran while one was open for 5% -> 5% of each run, Pallas kernels for 6% -> 9%
where the time goes in v4:
time: 60.1 us; the launch traced here: 59.5 us
  Pallas kernels  16.6 us (28%)
  starting transfers between devices  16.4 us (27%)
  blocking collectives  13.7 us (23%)
  waiting for transfers between devices  8.94 us (15%)
  other arithmetic  2.55 us (4%)
  between operations  0.71 us (1%)
    ppermute x11, starting transfers between devices, turn(): return lax.ppermute(value, 'dp', [(i, i ^ by) for i in range(owners)])  16.4 us
    all_to_all x1, blocking collectives, step(): sums = lax.all_to_all(sums, ('section', 'dp'), 0, 0, tiled=True)  13.7 us
    ppermute x11, waiting for transfers between devices, turn(): return lax.ppermute(value, 'dp', [(i, i ^ by) for i in range(owners)])  8.94 us
    pallas_call x4, Pallas kernels, step(): update, means = call(*operands)  7.09 us
    pallas_call x1, Pallas kernels, step(): pl.pallas_call(functools.partial(newton_kernel, owners, width), in_specs=...  5.28 us
    add x1, other arithmetic, step(): fresh = momentum_decay * mom_near + factor[0, 0] * grad_near.astype(F32)  2.47 us
    pallas_call x1, Pallas kernels, step(): pl.pallas_call(functools.partial(sums_kernel, layers), in_specs=[anywhere...  2.31 us
    pallas_call x1, Pallas kernels, step(): pl.pallas_call(functools.partial(start_kernel, layers, entries, owners),...  1.89 us
  transfers between devices with their start and end apart: 11, of which 5 were waited for; matrix products, arithmetic and copies ran while one was open for 5% of the time, Pallas kernels for 9%

profile of v4, /device:TPU:1, one launch (start us, length us, event | category | flops | bytes accessed | tf_op | source)
XLA Modules:
  0.0 59.5 jit_solution(15367754813434892457)
XLA Ops:
  0.6 2.3 %sums.1 = (f32[32,128]{1,0:T(8,128)S(1)}, bf16[4,288,448]{2,1,0:T(8,128)(2,1)S(1)}, f32[4,288,448]{2,1,0:T(8,128)S(1)}) custom-call(bf16[4,288,448]{2,1,0:T(8,128)(2,1)} %bitcast.36, f32[4,288,448]{2,1,0:T(8,128)} %bitcast.35), custom_call_target="tpu_custom_call" | custom-call | tf_op jit(solution)/shard_map/sums/pallas_call | solution.py:366
  3.0 13.7 %all_to_all.11 = f32[32,1,128]{2,1,0:T(1,128)S(1)} all-to-all(f32[32,1,128]{2,1,0:T(1,128)S(1)} %bitcast.32), channel_id=1, replica_groups=mesh['section'=4,'dp'=8] {'section','dp'}, dimensions={0} | all-to-all | bytes 32768 | tf_op jit(solution)/shard_map/all_to_all | solution.py:382
  16.6 1.9 %start.1 = (bf16[4,288,448]{2,1,0:T(8,128)(2,1)S(1)}, f32[4,168,128]{2,1,0:T(8,128)S(1)}, f32[4,168,128]{2,1,0:T(8,128)S(1)}, f32[8,128]{1,0:T(8,128)S(1)}) custom-call(f32[32,128]{1,0:T(8,128)S(1)} %bitcast.31, bf16[4,288,448]{2,1,0:T(8,128)(2,1)S(1)} %get-tuple-element.23.grad_ref, f32[4,288,448]{2,1,0:T(8,128)S(1)} %get-tuple-element.24.mom_ref), custom_call_target="tpu_custom_call" | custom-call | tf_op jit(solution)/shard_map/start/pallas_call | solution.py:386
  18.5 0.7 %collective-permute-start = (f32[4,168,128]{2,1,0:T(8,128)S(1)}, f32[4,168,128]{2,1,0:T(8,128)S(1)}, u32[]{:S(2)}, u32[]{:S(2)}) collective-permute-start(f32[4,168,128]{2,1,0:T(8,128)S(1)} %get-tuple-element.26), channel_id=1, source_target_pairs={{0,1},{1,0},{2,3},{3,2},{4,5},{5,4},{6,7},{7,6},{8,9},{9,8},{10,11... | collective-permute-start | bytes 1032200 | tf_op jit(solution)/shard_map/ppermute | solution.py:402
  19.2 0.5 slice.19
  19.7 0.8 %collective-permute-done = f32[4,168,128]{2,1,0:T(8,128)S(1)} collective-permute-done((f32[4,168,128]{2,1,0:T(8,128)S(1)}, f32[4,168,128]{2,1,0:T(8,128)S(1)}, u32[]{:S(2)}, u32[]{:S(2)}) %collective-permute-start) | collective-permute-done | bytes 344096 | tf_op jit(solution)/shard_map/ppermute | solution.py:402
  20.6 0.3 collective-permute-start.1
  20.9 0.3 collective-permute-start.2
  21.2 3.0 %collective-permute-start.3 = (f32[168,128]{1,0:T(8,128)S(1)}, f32[168,128]{1,0:T(8,128)S(1)}, u32[]{:S(2)}, u32[]{:S(2)}) collective-permute-start(f32[168,128]{1,0:T(8,128)S(1)} %get-tuple-element.42), channel_id=1, source_target_pairs={{0,6},{1,7},{2,4},{3,5},{4,2},{5,3},{6,0},{7,1},{8,14},{9,15},{10,... | collective-permute-start | bytes 258056 | tf_op jit(solution)/shard_map/ppermute | solution.py:402
  24.2 0.0 copy-start
  24.2 2.5 %multiply_add_fusion = f32[4,288,448]{2,1,0:T(8,128)} fusion(bf16[4,288,448]{2,1,0:T(8,128)(2,1)S(1)} %get-tuple-element.23.grad_ref, f32[4,288,448]{2,1,0:T(8,128)S(1)} %get-tuple-element.24.mom_ref, f32[]{:T(128)} %bitcast.11), kind=kLoop, calls=%fused_computation | loop fusion | flops 2064384 | bytes 5160964 | tf_op jit(solution)/shard_map/add | solution.py:408
  26.7 0.0 collective-permute-done.1
  26.7 0.0 collective-permute-done.2
  26.7 1.2 %collective-permute-done.3 = f32[168,128]{1,0:T(8,128)S(1)} collective-permute-done((f32[168,128]{1,0:T(8,128)S(1)}, f32[168,128]{1,0:T(8,128)S(1)}, u32[]{:S(2)}, u32[]{:S(2)}) %collective-permute-start.3) | collective-permute-done | bytes 86048 | tf_op jit(solution)/shard_map/ppermute | solution.py:402
  27.9 3.6 %collective-permute-start.4 = (f32[168,128]{1,0:T(8,128)S(1)}, f32[168,128]{1,0:T(8,128)S(1)}, u32[]{:S(2)}, u32[]{:S(2)}) collective-permute-start(f32[168,128]{1,0:T(8,128)S(1)} %fusion.2.own_ref), channel_id=1, source_target_pairs={{0,1},{1,0},{2,3},{3,2},{4,5},{5,4},{6,7},{7,6},{8,9},{9,8},{10,11... | collective-permute-start | bytes 258056 | tf_op jit(solution)/shard_map/ppermute | solution.py:402
  31.4 0.9 %collective-permute-done.4.other_ref = f32[168,128]{1,0:T(8,128)S(1)} collective-permute-done((f32[168,128]{1,0:T(8,128)S(1)}, f32[168,128]{1,0:T(8,128)S(1)}, u32[]{:S(2)}, u32[]{:S(2)}) %collective-permute-start.4) | collective-permute-done | bytes 86048 | tf_op jit(solution)/shard_map/ppermute | solution.py:402
  32.4 5.3 %newton.1 = (bf16[512,128]{1,0:T(8,128)(2,1)S(1)}, bf16[512,128]{1,0:T(8,128)(2,1)S(1)}) custom-call(f32[168,128]{1,0:T(8,128)S(1)} %fusion.2.own_ref, f32[168,128]{1,0:T(8,128)S(1)} %collective-permute-done.4.other_ref), custom_call_target="tpu_custom_call" | custom-call | tf_op jit(solution)/shard_map/newton/pallas_call | solution.py:414
  37.7 1.3 %collective-permute-start.9 = (bf16[512,128]{1,0:T(8,128)(2,1)S(1)}, bf16[512,128]{1,0:T(8,128)(2,1)S(1)}, u32[]{:S(2)}, u32[]{:S(2)}) collective-permute-start(bf16[512,128]{1,0:T(8,128)(2,1)S(1)} %get-tuple-element.31.refs_2_), channel_id=1, source_target_pairs={{0,2},{1,3},{2,0},{3,1},{4,6},{5,7},{6,4},{7,5},{8,10},{9,11},{10,... | collective-permute-start | bytes 393224 | tf_op jit(solution)/shard_map/ppermute | solution.py:402
  38.9 0.2 collective-permute-start.7
  39.1 2.1 %collective-permute-start.5 = (bf16[512,128]{1,0:T(8,128)(2,1)S(1)}, bf16[512,128]{1,0:T(8,128)(2,1)S(1)}, u32[]{:S(2)}, u32[]{:S(2)}) collective-permute-start(bf16[512,128]{1,0:T(8,128)(2,1)S(1)} %get-tuple-element.31.refs_2_), channel_id=1, source_target_pairs={{0,6},{1,7},{2,4},{3,5},{4,2},{5,3},{6,0},{7,1},{8,14},{9,15},{10,... | collective-permute-start | bytes 393224 | tf_op jit(solution)/shard_map/ppermute | solution.py:402
  41.3 1.2 %collective-permute-done.9.refs_2_ = bf16[512,128]{1,0:T(8,128)(2,1)S(1)} collective-permute-done((bf16[512,128]{1,0:T(8,128)(2,1)S(1)}, bf16[512,128]{1,0:T(8,128)(2,1)S(1)}, u32[]{:S(2)}, u32[]{:S(2)}) %collective-permute-start.9) | collective-permute-done | bytes 131104 | tf_op jit(solution)/shard_map/ppermute | solution.py:402
  42.4 2.7 %collective-permute-start.10 = (bf16[512,128]{1,0:T(8,128)(2,1)S(1)}, bf16[512,128]{1,0:T(8,128)(2,1)S(1)}, u32[]{:S(2)}, u32[]{:S(2)}) collective-permute-start(bf16[512,128]{1,0:T(8,128)(2,1)S(1)} %collective-permute-done.9.refs_2_), channel_id=1, source_target_pairs={{0,1},{1,0},{2,3},{3,2},{4,5},{5,4},{6,7},{7,6},{8,9},{9,8},{10,11... | collective-permute-start | bytes 393224 | tf_op jit(solution)/shard_map/ppermute | solution.py:402
  45.1 4.9 %collective-permute-done.7.refs_2_ = bf16[512,128]{1,0:T(8,128)(2,1)S(1)} collective-permute-done((bf16[512,128]{1,0:T(8,128)(2,1)S(1)}, bf16[512,128]{1,0:T(8,128)(2,1)S(1)}, u32[]{:S(2)}, u32[]{:S(2)}) %collective-permute-start.7) | collective-permute-done | bytes 131104 | tf_op jit(solution)/shard_map/ppermute | solution.py:402
  50.0 2.3 %collective-permute-start.8 = (bf16[512,128]{1,0:T(8,128)(2,1)S(1)}, bf16[512,128]{1,0:T(8,128)(2,1)S(1)}, u32[]{:S(2)}, u32[]{:S(2)}) collective-permute-start(bf16[512,128]{1,0:T(8,128)(2,1)S(1)} %collective-permute-done.7.refs_2_), channel_id=1, source_target_pairs={{0,1},{1,0},{2,3},{3,2},{4,5},{5,4},{6,7},{7,6},{8,9},{9,8},{10,11... | collective-permute-start | bytes 393224 | tf_op jit(solution)/shard_map/ppermute | solution.py:402
  52.3 0.0 collective-permute-done.5.refs_2_
  52.3 0.0 collective-permute-start.6
  52.3 0.0 copy-done
  52.3 1.8 %update.4 = (bf16[4,288,448]{2,1,0:T(8,128)(2,1)}, f32[8,128]{1,0:T(8,128)S(1)}) custom-call(s32[1,4]{1,0:T(1,128)S(1)} %copy-done, bf16[4,288,448]{2,1,0:T(8,128)(2,1)S(1)} %get-tuple-element.29.refs_1_, bf16[512,128]{1,0:T(8,128)(2,1)S(1)} %get-tuple-element.31.refs_2_, bf16[512,128]{1,0:T(8,128)(2,1)S(1)} %get-tuple-element.32.refs_3_), custom_call_target="tpu_custom_call" | custom-call | flops 148635648 | bytes 778240 | tf_op jit(solution)/shard_map/update/pallas_call | solution.py:472
  54.1 0.0 collective-permute-done.10.refs_3_
  54.1 1.8 %update.5 = (bf16[4,288,448]{2,1,0:T(8,128)(2,1)}, f32[8,128]{1,0:T(8,128)S(1)}) custom-call(s32[1,4]{1,0:T(1,128)S(1)} %copy-done, bf16[4,288,448]{2,1,0:T(8,128)(2,1)S(1)} %get-tuple-element.29.refs_1_, bf16[512,128]{1,0:T(8,128)(2,1)S(1)} %collective-permute-done.9.refs_2_, ...), custom_call_target="tpu_custom_call", output_to_operand_aliasing={{0}: (5, {})} | custom-call | flops 148635648 | bytes 778240 | tf_op jit(solution)/shard_map/update/pallas_call | solution.py:472
  55.9 0.0 collective-permute-done.8.refs_3_
  55.9 1.8 %update.6 = (bf16[4,288,448]{2,1,0:T(8,128)(2,1)}, f32[8,128]{1,0:T(8,128)S(1)}) custom-call(s32[1,4]{1,0:T(1,128)S(1)} %copy-done, bf16[4,288,448]{2,1,0:T(8,128)(2,1)S(1)} %get-tuple-element.29.refs_1_, bf16[512,128]{1,0:T(8,128)(2,1)S(1)} %collective-permute-done.7.refs_2_, ...), custom_call_target="tpu_custom_call", output_to_operand_aliasing={{0}: (5, {})} | custom-call | flops 148635648 | bytes 778240 | tf_op jit(solution)/shard_map/update/pallas_call | solution.py:472
  57.7 0.0 collective-permute-done.6.refs_3_
  57.7 1.8 %update.7 = (bf16[4,288,448]{2,1,0:T(8,128)(2,1)}, f32[1,2]{1,0:T(1,128)}) custom-call(s32[1,4]{1,0:T(1,128)S(1)} %copy-done, bf16[4,288,448]{2,1,0:T(8,128)(2,1)S(1)} %get-tuple-element.29.refs_1_, bf16[512,128]{1,0:T(8,128)(2,1)S(1)} %collective-permute-done.5.refs_2_, ...), custom_call_target="tpu_custom_call", output_to_operand_aliasing={{0}: (5, {})} | custom-call | flops 148635648 | bytes 778240 | tf_op jit(solution)/shard_map/update/pallas_call | solution.py:472
  (3 shorter events, 0.1 us)
Async XLA Ops:
  18.5 2.0 %collective-permute-start = (f32[4,168,128]{2,1,0:T(8,128)S(1)}, f32[4,168,128]{2,1,0:T(8,128)S(1)}, u32[]{:S(2)}, u32[]{:S(2)}) collective-permute-start(f32[4,168,128]{2,1,0:T(8,128)S(1)} %get-tuple-element.26), channel_id=1, source_target_pairs={{0,1},{1,0},{2,3},{3,2},{4,5},{5,4},{6,7},{7,6},{8,9},{9,8},{10,11... | collective-permute-start | bytes 1032200 | tf_op jit(solution)/shard_map/ppermute | solution.py:402
  20.6 6.1 %collective-permute-start.1 = (f32[168,128]{1,0:T(8,128)S(1)}, f32[168,128]{1,0:T(8,128)S(1)}, u32[]{:S(2)}, u32[]{:S(2)}) collective-permute-start(f32[168,128]{1,0:T(8,128)S(1)} %get-tuple-element.41), channel_id=1, source_target_pairs={{0,2},{1,3},{2,0},{3,1},{4,6},{5,7},{6,4},{7,5},{8,10},{9,11},{10,... | collective-permute-start | bytes 258056 | tf_op jit(solution)/shard_map/ppermute | solution.py:402
  20.9 5.8 %collective-permute-start.2 = (f32[168,128]{1,0:T(8,128)S(1)}, f32[168,128]{1,0:T(8,128)S(1)}, u32[]{:S(2)}, u32[]{:S(2)}) collective-permute-start(f32[168,128]{1,0:T(8,128)S(1)} %get-tuple-element.43), channel_id=1, source_target_pairs={{0,4},{1,5},{2,6},{3,7},{4,0},{5,1},{6,2},{7,3},{8,12},{9,13},{10,... | collective-permute-start | bytes 258056 | tf_op jit(solution)/shard_map/ppermute | solution.py:402
  21.2 6.6 %collective-permute-start.3 = (f32[168,128]{1,0:T(8,128)S(1)}, f32[168,128]{1,0:T(8,128)S(1)}, u32[]{:S(2)}, u32[]{:S(2)}) collective-permute-start(f32[168,128]{1,0:T(8,128)S(1)} %get-tuple-element.42), channel_id=1, source_target_pairs={{0,6},{1,7},{2,4},{3,5},{4,2},{5,3},{6,0},{7,1},{8,14},{9,15},{10,... | collective-permute-start | bytes 258056 | tf_op jit(solution)/shard_map/ppermute | solution.py:402
  24.2 28.1 %copy-start = (s32[1,4]{1,0:T(1,128)S(1)}, s32[1,4]{1,0:T(1,128)}, u32[]{:S(2)}) copy-start(s32[1,4]{1,0:T(1,128)} %refs_0_.7) | copy-start | bytes 52
  27.9 4.5 %collective-permute-start.4 = (f32[168,128]{1,0:T(8,128)S(1)}, f32[168,128]{1,0:T(8,128)S(1)}, u32[]{:S(2)}, u32[]{:S(2)}) collective-permute-start(f32[168,128]{1,0:T(8,128)S(1)} %fusion.2.own_ref), channel_id=1, source_target_pairs={{0,1},{1,0},{2,3},{3,2},{4,5},{5,4},{6,7},{7,6},{8,9},{9,8},{10,11... | collective-permute-start | bytes 258056 | tf_op jit(solution)/shard_map/ppermute | solution.py:402
  37.7 4.8 %collective-permute-start.9 = (bf16[512,128]{1,0:T(8,128)(2,1)S(1)}, bf16[512,128]{1,0:T(8,128)(2,1)S(1)}, u32[]{:S(2)}, u32[]{:S(2)}) collective-permute-start(bf16[512,128]{1,0:T(8,128)(2,1)S(1)} %get-tuple-element.31.refs_2_), channel_id=1, source_target_pairs={{0,2},{1,3},{2,0},{3,1},{4,6},{5,7},{6,4},{7,5},{8,10},{9,11},{10,... | collective-permute-start | bytes 393224 | tf_op jit(solution)/shard_map/ppermute | solution.py:402
  38.9 11.1 %collective-permute-start.7 = (bf16[512,128]{1,0:T(8,128)(2,1)S(1)}, bf16[512,128]{1,0:T(8,128)(2,1)S(1)}, u32[]{:S(2)}, u32[]{:S(2)}) collective-permute-start(bf16[512,128]{1,0:T(8,128)(2,1)S(1)} %get-tuple-element.31.refs_2_), channel_id=1, source_target_pairs={{0,4},{1,5},{2,6},{3,7},{4,0},{5,1},{6,2},{7,3},{8,12},{9,13},{10,... | collective-permute-start | bytes 393224 | tf_op jit(solution)/shard_map/ppermute | solution.py:402
  39.1 13.2 %collective-permute-start.5 = (bf16[512,128]{1,0:T(8,128)(2,1)S(1)}, bf16[512,128]{1,0:T(8,128)(2,1)S(1)}, u32[]{:S(2)}, u32[]{:S(2)}) collective-permute-start(bf16[512,128]{1,0:T(8,128)(2,1)S(1)} %get-tuple-element.31.refs_2_), channel_id=1, source_target_pairs={{0,6},{1,7},{2,4},{3,5},{4,2},{5,3},{6,0},{7,1},{8,14},{9,15},{10,... | collective-permute-start | bytes 393224 | tf_op jit(solution)/shard_map/ppermute | solution.py:402
  42.4 11.7 %collective-permute-start.10 = (bf16[512,128]{1,0:T(8,128)(2,1)S(1)}, bf16[512,128]{1,0:T(8,128)(2,1)S(1)}, u32[]{:S(2)}, u32[]{:S(2)}) collective-permute-start(bf16[512,128]{1,0:T(8,128)(2,1)S(1)} %collective-permute-done.9.refs_2_), channel_id=1, source_target_pairs={{0,1},{1,0},{2,3},{3,2},{4,5},{5,4},{6,7},{7,6},{8,9},{9,8},{10,11... | collective-permute-start | bytes 393224 | tf_op jit(solution)/shard_map/ppermute | solution.py:402
  50.0 5.9 %collective-permute-start.8 = (bf16[512,128]{1,0:T(8,128)(2,1)S(1)}, bf16[512,128]{1,0:T(8,128)(2,1)S(1)}, u32[]{:S(2)}, u32[]{:S(2)}) collective-permute-start(bf16[512,128]{1,0:T(8,128)(2,1)S(1)} %collective-permute-done.7.refs_2_), channel_id=1, source_target_pairs={{0,1},{1,0},{2,3},{3,2},{4,5},{5,4},{6,7},{7,6},{8,9},{9,8},{10,11... | collective-permute-start | bytes 393224 | tf_op jit(solution)/shard_map/ppermute | solution.py:402
  52.3 5.4 %collective-permute-start.6 = (bf16[512,128]{1,0:T(8,128)(2,1)S(1)}, bf16[512,128]{1,0:T(8,128)(2,1)S(1)}, u32[]{:S(2)}, u32[]{:S(2)}) collective-permute-start(bf16[512,128]{1,0:T(8,128)(2,1)S(1)} %collective-permute-done.5.refs_2_), channel_id=1, source_target_pairs={{0,1},{1,0},{2,3},{3,2},{4,5},{5,4},{6,7},{7,6},{8,9},{9,8},{10,11... | collective-permute-start | bytes 393224 | tf_op jit(solution)/shard_map/ppermute | solution.py:402

commit v5 on v4

--- a/solution.py
+++ b/solution.py
@@ -217,22 +217,26 @@
     ca, cb, cc = newton_coeffs
     rows = lax.broadcasted_iota(jnp.int32, (width, width), 0)
     cols = lax.broadcasted_iota(jnp.int32, (width, width), 1)
+    eye = rows == cols
     prod = None
     mean_sq = None
     for step in range(NS_STEPS):
         rounded = gram.astype(BF16)
         mix = (cb * rounded.astype(F32) + cc * dot(rounded, rounded)).astype(BF16)
-        mix32 = mix.astype(F32)
-        turned = ca * gram + wide_left(gram, mix)
         if step < NS_STEPS - 1:
-            gram = ca * turned + wide_right(mix, turned)
+            turned = ca * gram + wide_right(mix, gram)
+            gram = ca * turned + wide_left(turned, mix)
         else:
-            diagonal = jnp.where(rows == cols, turned, 0.0)
-            mean_sq = total_of(ca * diagonal + mix32 * turned) * (1.0 / width)
-        if prod is None:
-            prod = ratio * (jnp.where(rows == cols, ca, 0.0) + mix32)
+            inner = dot(mix, mix) + (2.0 * ca) * mix.astype(F32) + jnp.where(eye, ca * ca, 0.0)
+            mean_sq = total_of(gram * inner) * (1.0 / width)
+        if step == 0:
+            before = mix
+        elif step == 1:
+            both = ca * (before.astype(F32) + mix.astype(F32)) + dot(mix, before)
+            prod = both + jnp.where(eye, ca * ca, 0.0)
         else:
             prod = ca * prod + wide_right(mix, prod)
+    prod = ratio * prod
     p00, p11 = prod[0:a, 0:a], prod[a:b, a:b]
     back00, back11 = p00.T, p11.T
     p01, back10 = prod[0:a, a:b], prod[a:b, 0:a].T
@@ -262,72 +266,59 @@
     theirs_ref[...] = half_of(full, 1 - core, half, 16)[...]
 
 
-def update_kernel(scale, width, group, last, *refs):
-    owner_ref, start_ref = refs[:2]
-    products = refs[2 : 2 + 2 * len(group)]
-    refs = refs[2 + 2 * len(group) :]
-    means = None
-    if group[0]:
-        means = refs[0][...]
-        refs = refs[2:]
-    if last:
-        out_ref, slot_out, fulls, values, sems, slot_ref, slot_sem = refs
+def update_kernel(scale, width, rel, last, *refs):
+    if rel == 0:
+        start_ref, mine_ref, other_ref, owner_ref, out_ref, means_out, full, values, sems = refs
+    elif last:
+        start_ref, mine_ref, other_ref, means_ref, _, out_ref, slot_out, full, values, sems, slot_ref = refs
     else:
-        out_ref, means_out, fulls, values, sems = refs
+        start_ref, mine_ref, other_ref, means_ref, _, out_ref, means_out, full, values, sems = refs
     place = lax.axis_index("dp")
     chip, core = place >> 1, place & 1
+    layer = chip ^ rel
     tail = width - 2 * LANES
     b = 2 * LANES
+    half = mine_ref.shape[0]
+    half_of(full, core, half, 16)[...] = mine_ref[...]
+    half_of(full, 1 - core, half, 16)[...] = other_ref[...]
+    size = packed_rows(tail)
+    even = full[0:size, :].astype(F32) + full[size : 2 * size, :].astype(F32)
+    odd = full[2 * size : 3 * size, :].astype(F32)
+    plus, minus = even + odd, even - odd
+    at = b + 2 * tail
+    small = tail * tail // LANES
+    extra = even[at + small :]
+    start = start_ref[layer]
+    rest = jnp.concatenate([start[b:], start[b:]], axis=0)
     down, across = grid_of(LANES)
-    lane = lax.broadcasted_iota(jnp.int32, (8, LANES), 1)
+    turned = minus[0:LANES].T
+    p00 = jnp.where(down >= across, plus[0:LANES], turned)
+    p11 = jnp.where(down == across, extra[0:1], jnp.where(down < across, plus[0:LANES], turned))
+    p10 = minus[LANES:b].T
+    strips = (
+        (p00, plus[LANES:b], minus[b : b + tail].T),
+        (p10, p11, minus[b + tail : at].T),
+        (plus[b : b + tail], plus[b + tail : at], read_corner(even[at : at + small], tail)),
+    )
     copies = []
-    for i, rel in enumerate(group):
-        layer = chip ^ rel
-        mine_ref, other_ref = products[2 * i : 2 * i + 2]
-        full = fulls.at[i]
-        half = mine_ref.shape[0]
-        half_of(full, core, half, 16)[...] = mine_ref[...]
-        half_of(full, 1 - core, half, 16)[...] = other_ref[...]
-        size = packed_rows(tail)
-        even = full[0:size, :].astype(F32) + full[size : 2 * size, :].astype(F32)
-        odd = full[2 * size : 3 * size, :].astype(F32)
-        plus, minus = even + odd, even - odd
-        at = b + 2 * tail
-        small = tail * tail // LANES
-        extra = even[at + small :]
-        turned = minus[0:LANES].T
-        p00 = jnp.where(down >= across, plus[0:LANES], turned)
-        p11 = jnp.where(
-            down == across, extra[0:1], jnp.where(down < across, plus[0:LANES], turned)
-        )
-        p10 = minus[LANES:b].T
-        main = jnp.concatenate(
-            [
-                jnp.concatenate([p00, plus[LANES:b]], axis=1),
-                jnp.concatenate([p10, p11], axis=1),
-                jnp.concatenate([plus[b : b + tail], plus[b + tail : at]], axis=1),
-            ],
-            axis=0,
-        )
-        ends = jnp.concatenate(
-            [minus[b : b + tail].T, minus[b + tail : at].T, read_corner(even[at : at + small], tail)],
-            axis=0,
-        )
-        high, low = split(main)
-        end_high, end_low = split(ends)
-        start = start_ref[layer]
-        rest = jnp.concatenate([start[b:], start[b:]], axis=0)
-        value = dot(high, start[:b]) + dot(low, start[:b])
-        value = value + dot(jnp.concatenate([end_high, end_low], axis=1), rest)
-        values[i] = (value * scale).astype(BF16)
+    first = 0
+    for i, strip in enumerate(strips):
+        high, low = split(jnp.concatenate(strip[:2], axis=1))
+        ends = jnp.concatenate(split(strip[2]), axis=1)
+        value = dot(high, start[:b]) + dot(low, start[:b]) + dot(ends, rest)
+        strip_rows = pl.ds(first, value.shape[0])
+        values[strip_rows, :] = (value * scale).astype(BF16)
         copies.append(
-            pltpu.make_async_copy(values.at[i], out_ref.at[layer], sems.at[i])
+            pltpu.make_async_copy(values.at[strip_rows], out_ref.at[layer, strip_rows], sems.at[i])
         )
         copies[-1].start()
-        found = jnp.where(lane == layer, extra[1:2], 0.0)
-        means = found if means is None else means + found
-    if last:
-        line = jnp.zeros((1, LANES), F32)
+        first += value.shape[0]
+    row = lax.broadcasted_iota(jnp.int32, (8, LANES), 0)
+    lane = lax.broadcasted_iota(jnp.int32, (8, LANES), 1)
+    means = jnp.where((row == 0) & (lane == layer), extra[1:2], 0.0)
+    if rel:
+        means = means + means_ref[...]
+    else:
         for slot in range(MAXOWN):
 
             def visit(j, carry):
@@ -336,13 +327,17 @@
                 at = jnp.where(hit & (seen == slot), j, at)
                 return seen + jnp.where(hit, 1, 0), at
 
-            _, at = lax.fori_loop(
-                0, owner_ref.shape[1], visit, (jnp.int32(0), jnp.int32(-1)), unroll=owner_ref.shape[1] <= 8
-            )
-            value = jnp.sum(jnp.where(lane[0:1] == at, means[0:1], 0.0), axis=1, keepdims=True)
-            line = jnp.where(lane[0:1] == slot, value, line)
-        slot_ref[...] = line[:, 0:MAXOWN]
-        copies.append(pltpu.make_async_copy(slot_ref, slot_out, slot_sem))
+            _, at = lax.fori_loop(0, owner_ref.shape[1], visit, (jnp.int32(0), jnp.int32(-1)))
+            means = jnp.where((row == 1 + slot) & (lane == at), 1.0, means)
+    if last:
+        chosen = jnp.where(means > 0.0, means[0:1], 0.0)
+        spots = lax.broadcasted_iota(jnp.int32, slot_ref.shape, 1)
+        line = jnp.zeros(slot_ref.shape, F32)
+        for slot in range(MAXOWN):
+            value = jnp.sum(chosen[1 + slot : 2 + slot], axis=1, keepdims=True)
+            line = jnp.where(spots == slot, value, line)
+        slot_ref[...] = line
+        copies.append(pltpu.make_async_copy(slot_ref, slot_out, sems.at[len(strips)]))
         copies[-1].start()
     else:
         means_out[...] = means
@@ -431,22 +426,20 @@
     update = means = None
     flops = 4 * width * width * rows
     for rel in range(chips):
-        group = (rel,)
         last = rel == chips - 1
-        operands = [assignment, start]
-        if group[0]:
+        operands, in_specs = [start], [near_by] * 3
+        aliases = {}
+        if rel:
             near = arriving[rel]
             operands += [near, turn(near, 1)]
-        else:
-            operands += [mine, theirs]
-        in_specs = [pl.BlockSpec(memory_space=pltpu.SMEM)] + [near_by] * (len(operands) - 1)
-        aliases = {}
-        if group[0]:
-            aliases = {len(operands) + 1: 0}
             operands += [means, update]
             in_specs += [near_by, pl.BlockSpec(memory_space=pl.ANY)]
+            aliases = {4: 0}
+        else:
+            operands += [mine, theirs, assignment]
+            in_specs.append(pl.BlockSpec(memory_space=pltpu.SMEM))
         call = pl.pallas_call(
-            functools.partial(update_kernel, math.sqrt(owners * rows), width, group, last),
+            functools.partial(update_kernel, math.sqrt(owners * rows), width, rel, last),
             in_specs=in_specs,
             out_specs=[
                 pl.BlockSpec(memory_space=pl.ANY),
@@ -457,16 +450,14 @@
                 jax.ShapeDtypeStruct((1, MAXOWN) if last else (8, LANES), F32),
             ],
             scratch_shapes=[
-                pltpu.VMEM((len(group), full_rows, LANES), BF16),
-                pltpu.VMEM((len(group), width, rows), BF16),
-                pltpu.SemaphoreType.DMA((len(group),)),
+                pltpu.VMEM((full_rows, LANES), BF16),
+                pltpu.VMEM((width, rows), BF16),
+                pltpu.SemaphoreType.DMA((4,)),
             ]
-            + [pltpu.VMEM((1, MAXOWN), F32), pltpu.SemaphoreType.DMA] * last,
+            + [pltpu.VMEM((1, MAXOWN), F32)] * last,
             input_output_aliases=aliases,
             compiler_params=params(),
-            cost_estimate=cost(
-                len(group) * flops, len(group) * (4 * width * rows + 4 * piece * LANES)
-            ),
+            cost_estimate=cost(flops, 4 * width * rows + 4 * piece * LANES),
             name="update",
         )
         update, means = call(*operands)

time: 60.1 us -> 58.1 us (0.967)
  Pallas kernels: 16.6 us -> 14.5 us
    pallas_call x4, Pallas kernels: 7.09 us -> 5.39 us  [step(): update, means = call(*operands)]
  transfers between devices with their start and end apart: 11 -> 11, of which waited for: 5 -> 5; matrix products, arithmetic and copies ran while one was open for 5% -> 5% of each run, Pallas kernels for 9% -> 7%
where the time goes in v5:
time: 58.1 us; the launch traced here: 57.4 us
  starting transfers between devices  16.5 us (28%)
  Pallas kernels  14.5 us (25%)
  blocking collectives  13.7 us (24%)
  waiting for transfers between devices  8.95 us (15%)
  other arithmetic  2.55 us (4%)
  between operations  0.71 us (1%)
    ppermute x11, starting transfers between devices, turn(): return lax.ppermute(value, 'dp', [(i, i ^ by) for i in range(owners)])  16.5 us
    all_to_all x1, blocking collectives, step(): sums = lax.all_to_all(sums, ('section', 'dp'), 0, 0, tiled=True)  13.7 us
    ppermute x11, waiting for transfers between devices, turn(): return lax.ppermute(value, 'dp', [(i, i ^ by) for i in range(owners)])  8.95 us
    pallas_call x4, Pallas kernels, step(): update, means = call(*operands)  5.39 us
    pallas_call x1, Pallas kernels, step(): pl.pallas_call(functools.partial(newton_kernel, owners, width), in_specs=...  4.88 us
    add x1, other arithmetic, step(): fresh = momentum_decay * mom_near + factor[0, 0] * grad_near.astype(F32)  2.47 us
    pallas_call x1, Pallas kernels, step(): pl.pallas_call(functools.partial(sums_kernel, layers), in_specs=[anywhere...  2.31 us
    pallas_call x1, Pallas kernels, step(): pl.pallas_call(functools.partial(start_kernel, layers, entries, owners),...  1.89 us
  transfers between devices with their start and end apart: 11, of which 5 were waited for; matrix products, arithmetic and copies ran while one was open for 5% of the time, Pallas kernels for 7%

profile of v5, /device:TPU:1, one launch (start us, length us, event | category | flops | bytes accessed | tf_op | source)
XLA Modules:
  0.0 57.4 jit_solution(12724699117279852583)
XLA Ops:
  0.6 2.3 %sums.1 = (f32[32,128]{1,0:T(8,128)S(1)}, bf16[4,288,448]{2,1,0:T(8,128)(2,1)S(1)}, f32[4,288,448]{2,1,0:T(8,128)S(1)}) custom-call(bf16[4,288,448]{2,1,0:T(8,128)(2,1)} %bitcast.36, f32[4,288,448]{2,1,0:T(8,128)} %bitcast.35), custom_call_target="tpu_custom_call" | custom-call | tf_op jit(solution)/shard_map/sums/pallas_call | solution.py:361
  3.0 13.7 %all_to_all.11 = f32[32,1,128]{2,1,0:T(1,128)S(1)} all-to-all(f32[32,1,128]{2,1,0:T(1,128)S(1)} %bitcast.32), channel_id=1, replica_groups=mesh['section'=4,'dp'=8] {'section','dp'}, dimensions={0} | all-to-all | bytes 32768 | tf_op jit(solution)/shard_map/all_to_all | solution.py:377
  16.6 1.9 %start.1 = (bf16[4,288,448]{2,1,0:T(8,128)(2,1)S(1)}, f32[4,168,128]{2,1,0:T(8,128)S(1)}, f32[4,168,128]{2,1,0:T(8,128)S(1)}, f32[8,128]{1,0:T(8,128)S(1)}) custom-call(f32[32,128]{1,0:T(8,128)S(1)} %bitcast.31, bf16[4,288,448]{2,1,0:T(8,128)(2,1)S(1)} %get-tuple-element.23.grad_ref, f32[4,288,448]{2,1,0:T(8,128)S(1)} %get-tuple-element.24.mom_ref), custom_call_target="tpu_custom_call" | custom-call | tf_op jit(solution)/shard_map/start/pallas_call | solution.py:381
  18.5 0.7 %collective-permute-start = (f32[4,168,128]{2,1,0:T(8,128)S(1)}, f32[4,168,128]{2,1,0:T(8,128)S(1)}, u32[]{:S(2)}, u32[]{:S(2)}) collective-permute-start(f32[4,168,128]{2,1,0:T(8,128)S(1)} %get-tuple-element.26), channel_id=1, source_target_pairs={{0,1},{1,0},{2,3},{3,2},{4,5},{5,4},{6,7},{7,6},{8,9},{9,8},{10,11... | collective-permute-start | bytes 1032200 | tf_op jit(solution)/shard_map/ppermute | solution.py:397
  19.2 0.5 slice.19
  19.7 0.8 %collective-permute-done = f32[4,168,128]{2,1,0:T(8,128)S(1)} collective-permute-done((f32[4,168,128]{2,1,0:T(8,128)S(1)}, f32[4,168,128]{2,1,0:T(8,128)S(1)}, u32[]{:S(2)}, u32[]{:S(2)}) %collective-permute-start) | collective-permute-done | bytes 344096 | tf_op jit(solution)/shard_map/ppermute | solution.py:397
  20.6 0.3 collective-permute-start.1
  20.9 0.3 collective-permute-start.2
  21.2 3.0 %collective-permute-start.3 = (f32[168,128]{1,0:T(8,128)S(1)}, f32[168,128]{1,0:T(8,128)S(1)}, u32[]{:S(2)}, u32[]{:S(2)}) collective-permute-start(f32[168,128]{1,0:T(8,128)S(1)} %get-tuple-element.42), channel_id=1, source_target_pairs={{0,6},{1,7},{2,4},{3,5},{4,2},{5,3},{6,0},{7,1},{8,14},{9,15},{10,... | collective-permute-start | bytes 258056 | tf_op jit(solution)/shard_map/ppermute | solution.py:397
  24.2 0.0 copy-start
  24.2 2.5 %multiply_add_fusion = f32[4,288,448]{2,1,0:T(8,128)} fusion(bf16[4,288,448]{2,1,0:T(8,128)(2,1)S(1)} %get-tuple-element.23.grad_ref, f32[4,288,448]{2,1,0:T(8,128)S(1)} %get-tuple-element.24.mom_ref, f32[]{:T(128)} %bitcast.11), kind=kLoop, calls=%fused_computation | loop fusion | flops 2064384 | bytes 5160964 | tf_op jit(solution)/shard_map/add | solution.py:403
  26.7 0.0 collective-permute-done.1
  26.7 0.0 collective-permute-done.2
  26.7 1.2 %collective-permute-done.3 = f32[168,128]{1,0:T(8,128)S(1)} collective-permute-done((f32[168,128]{1,0:T(8,128)S(1)}, f32[168,128]{1,0:T(8,128)S(1)}, u32[]{:S(2)}, u32[]{:S(2)}) %collective-permute-start.3) | collective-permute-done | bytes 86048 | tf_op jit(solution)/shard_map/ppermute | solution.py:397
  27.9 3.6 %collective-permute-start.4 = (f32[168,128]{1,0:T(8,128)S(1)}, f32[168,128]{1,0:T(8,128)S(1)}, u32[]{:S(2)}, u32[]{:S(2)}) collective-permute-start(f32[168,128]{1,0:T(8,128)S(1)} %fusion.2.own_ref), channel_id=1, source_target_pairs={{0,1},{1,0},{2,3},{3,2},{4,5},{5,4},{6,7},{7,6},{8,9},{9,8},{10,11... | collective-permute-start | bytes 258056 | tf_op jit(solution)/shard_map/ppermute | solution.py:397
  31.4 0.9 %collective-permute-done.4.other_ref = f32[168,128]{1,0:T(8,128)S(1)} collective-permute-done((f32[168,128]{1,0:T(8,128)S(1)}, f32[168,128]{1,0:T(8,128)S(1)}, u32[]{:S(2)}, u32[]{:S(2)}) %collective-permute-start.4) | collective-permute-done | bytes 86048 | tf_op jit(solution)/shard_map/ppermute | solution.py:397
  32.4 4.9 %newton.1 = (bf16[512,128]{1,0:T(8,128)(2,1)S(1)}, bf16[512,128]{1,0:T(8,128)(2,1)S(1)}) custom-call(f32[168,128]{1,0:T(8,128)S(1)} %fusion.2.own_ref, f32[168,128]{1,0:T(8,128)S(1)} %collective-permute-done.4.other_ref), custom_call_target="tpu_custom_call" | custom-call | tf_op jit(solution)/shard_map/newton/pallas_call | solution.py:409
  37.3 1.3 %collective-permute-start.9 = (bf16[512,128]{1,0:T(8,128)(2,1)S(1)}, bf16[512,128]{1,0:T(8,128)(2,1)S(1)}, u32[]{:S(2)}, u32[]{:S(2)}) collective-permute-start(bf16[512,128]{1,0:T(8,128)(2,1)S(1)} %get-tuple-element.31.refs_1_), channel_id=1, source_target_pairs={{0,2},{1,3},{2,0},{3,1},{4,6},{5,7},{6,4},{7,5},{8,10},{9,11},{10,... | collective-permute-start | bytes 393224 | tf_op jit(solution)/shard_map/ppermute | solution.py:397
  38.5 0.2 collective-permute-start.7
  38.7 2.1 %collective-permute-start.5 = (bf16[512,128]{1,0:T(8,128)(2,1)S(1)}, bf16[512,128]{1,0:T(8,128)(2,1)S(1)}, u32[]{:S(2)}, u32[]{:S(2)}) collective-permute-start(bf16[512,128]{1,0:T(8,128)(2,1)S(1)} %get-tuple-element.31.refs_1_), channel_id=1, source_target_pairs={{0,6},{1,7},{2,4},{3,5},{4,2},{5,3},{6,0},{7,1},{8,14},{9,15},{10,... | collective-permute-start | bytes 393224 | tf_op jit(solution)/shard_map/ppermute | solution.py:397
  40.9 1.2 %collective-permute-done.9.refs_1_ = bf16[512,128]{1,0:T(8,128)(2,1)S(1)} collective-permute-done((bf16[512,128]{1,0:T(8,128)(2,1)S(1)}, bf16[512,128]{1,0:T(8,128)(2,1)S(1)}, u32[]{:S(2)}, u32[]{:S(2)}) %collective-permute-start.9) | collective-permute-done | bytes 131104 | tf_op jit(solution)/shard_map/ppermute | solution.py:397
  42.0 2.7 %collective-permute-start.10 = (bf16[512,128]{1,0:T(8,128)(2,1)S(1)}, bf16[512,128]{1,0:T(8,128)(2,1)S(1)}, u32[]{:S(2)}, u32[]{:S(2)}) collective-permute-start(bf16[512,128]{1,0:T(8,128)(2,1)S(1)} %collective-permute-done.9.refs_1_), channel_id=1, source_target_pairs={{0,1},{1,0},{2,3},{3,2},{4,5},{5,4},{6,7},{7,6},{8,9},{9,8},{10,11... | collective-permute-start | bytes 393224 | tf_op jit(solution)/shard_map/ppermute | solution.py:397
  44.7 4.9 %collective-permute-done.7.refs_1_ = bf16[512,128]{1,0:T(8,128)(2,1)S(1)} collective-permute-done((bf16[512,128]{1,0:T(8,128)(2,1)S(1)}, bf16[512,128]{1,0:T(8,128)(2,1)S(1)}, u32[]{:S(2)}, u32[]{:S(2)}) %collective-permute-start.7) | collective-permute-done | bytes 131104 | tf_op jit(solution)/shard_map/ppermute | solution.py:397
  49.6 2.3 %collective-permute-start.8 = (bf16[512,128]{1,0:T(8,128)(2,1)S(1)}, bf16[512,128]{1,0:T(8,128)(2,1)S(1)}, u32[]{:S(2)}, u32[]{:S(2)}) collective-permute-start(bf16[512,128]{1,0:T(8,128)(2,1)S(1)} %collective-permute-done.7.refs_1_), channel_id=1, source_target_pairs={{0,1},{1,0},{2,3},{3,2},{4,5},{5,4},{6,7},{7,6},{8,9},{9,8},{10,11... | collective-permute-start | bytes 393224 | tf_op jit(solution)/shard_map/ppermute | solution.py:397
  51.9 0.0 collective-permute-done.5.refs_1_
  51.9 0.0 collective-permute-start.6
  51.9 0.0 copy-done
  51.9 1.7 %update.4 = (bf16[4,288,448]{2,1,0:T(8,128)(2,1)}, f32[8,128]{1,0:T(8,128)S(1)}) custom-call(bf16[4,288,448]{2,1,0:T(8,128)(2,1)S(1)} %get-tuple-element.29.refs_0_, bf16[512,128]{1,0:T(8,128)(2,1)S(1)} %get-tuple-element.31.refs_1_, bf16[512,128]{1,0:T(8,128)(2,1)S(1)} %get-tuple-element.32.refs_2_, s32[1,4]{1,0:T(1,128)S(1)} %copy-done), custom_call_target="tpu_custom_call" | custom-call | flops 148635648 | bytes 778240 | tf_op jit(solution)/shard_map/update/pallas_call | solution.py:463
  53.7 0.0 collective-permute-done.10.refs_2_
  53.7 1.2 %update.5 = (bf16[4,288,448]{2,1,0:T(8,128)(2,1)}, f32[8,128]{1,0:T(8,128)S(1)}) custom-call(bf16[4,288,448]{2,1,0:T(8,128)(2,1)S(1)} %get-tuple-element.29.refs_0_, bf16[512,128]{1,0:T(8,128)(2,1)S(1)} %collective-permute-done.9.refs_1_, bf16[512,128]{1,0:T(8,128)(2,1)S(1)} %collective-permute-done.10.refs_2_, ...), custom_call_target="tpu_custom_call", output_to_operand_aliasing={{0}: (4, {})} | custom-call | flops 148635648 | bytes 778240 | tf_op jit(solution)/shard_map/update/pallas_call | solution.py:463
  54.9 0.0 collective-permute-done.8.refs_2_
  54.9 1.2 %update.6 = (bf16[4,288,448]{2,1,0:T(8,128)(2,1)}, f32[8,128]{1,0:T(8,128)S(1)}) custom-call(bf16[4,288,448]{2,1,0:T(8,128)(2,1)S(1)} %get-tuple-element.29.refs_0_, bf16[512,128]{1,0:T(8,128)(2,1)S(1)} %collective-permute-done.7.refs_1_, bf16[512,128]{1,0:T(8,128)(2,1)S(1)} %collective-permute-done.8.refs_2_, ...), custom_call_target="tpu_custom_call", output_to_operand_aliasing={{0}: (4, {})} | custom-call | flops 148635648 | bytes 778240 | tf_op jit(solution)/shard_map/update/pallas_call | solution.py:463
  56.1 0.0 collective-permute-done.6.refs_2_
  56.1 1.2 %update.7 = (bf16[4,288,448]{2,1,0:T(8,128)(2,1)}, f32[1,2]{1,0:T(1,128)}) custom-call(bf16[4,288,448]{2,1,0:T(8,128)(2,1)S(1)} %get-tuple-element.29.refs_0_, bf16[512,128]{1,0:T(8,128)(2,1)S(1)} %collective-permute-done.5.refs_1_, bf16[512,128]{1,0:T(8,128)(2,1)S(1)} %collective-permute-done.6.refs_2_, ...), custom_call_target="tpu_custom_call", output_to_operand_aliasing={{0}: (4, {})} | custom-call | flops 148635648 | bytes 778240 | tf_op jit(solution)/shard_map/update/pallas_call | solution.py:463
  (3 shorter events, 0.1 us)
Async XLA Ops:
  18.5 2.0 %collective-permute-start = (f32[4,168,128]{2,1,0:T(8,128)S(1)}, f32[4,168,128]{2,1,0:T(8,128)S(1)}, u32[]{:S(2)}, u32[]{:S(2)}) collective-permute-start(f32[4,168,128]{2,1,0:T(8,128)S(1)} %get-tuple-element.26), channel_id=1, source_target_pairs={{0,1},{1,0},{2,3},{3,2},{4,5},{5,4},{6,7},{7,6},{8,9},{9,8},{10,11... | collective-permute-start | bytes 1032200 | tf_op jit(solution)/shard_map/ppermute | solution.py:397
  20.6 6.1 %collective-permute-start.1 = (f32[168,128]{1,0:T(8,128)S(1)}, f32[168,128]{1,0:T(8,128)S(1)}, u32[]{:S(2)}, u32[]{:S(2)}) collective-permute-start(f32[168,128]{1,0:T(8,128)S(1)} %get-tuple-element.41), channel_id=1, source_target_pairs={{0,2},{1,3},{2,0},{3,1},{4,6},{5,7},{6,4},{7,5},{8,10},{9,11},{10,... | collective-permute-start | bytes 258056 | tf_op jit(solution)/shard_map/ppermute | solution.py:397
  20.9 5.8 %collective-permute-start.2 = (f32[168,128]{1,0:T(8,128)S(1)}, f32[168,128]{1,0:T(8,128)S(1)}, u32[]{:S(2)}, u32[]{:S(2)}) collective-permute-start(f32[168,128]{1,0:T(8,128)S(1)} %get-tuple-element.43), channel_id=1, source_target_pairs={{0,4},{1,5},{2,6},{3,7},{4,0},{5,1},{6,2},{7,3},{8,12},{9,13},{10,... | collective-permute-start | bytes 258056 | tf_op jit(solution)/shard_map/ppermute | solution.py:397
  21.2 6.6 %collective-permute-start.3 = (f32[168,128]{1,0:T(8,128)S(1)}, f32[168,128]{1,0:T(8,128)S(1)}, u32[]{:S(2)}, u32[]{:S(2)}) collective-permute-start(f32[168,128]{1,0:T(8,128)S(1)} %get-tuple-element.42), channel_id=1, source_target_pairs={{0,6},{1,7},{2,4},{3,5},{4,2},{5,3},{6,0},{7,1},{8,14},{9,15},{10,... | collective-permute-start | bytes 258056 | tf_op jit(solution)/shard_map/ppermute | solution.py:397
  24.2 27.7 %copy-start = (s32[1,4]{1,0:T(1,128)S(1)}, s32[1,4]{1,0:T(1,128)}, u32[]{:S(2)}) copy-start(s32[1,4]{1,0:T(1,128)} %refs_3_.1) | copy-start | bytes 52
  27.9 4.5 %collective-permute-start.4 = (f32[168,128]{1,0:T(8,128)S(1)}, f32[168,128]{1,0:T(8,128)S(1)}, u32[]{:S(2)}, u32[]{:S(2)}) collective-permute-start(f32[168,128]{1,0:T(8,128)S(1)} %fusion.2.own_ref), channel_id=1, source_target_pairs={{0,1},{1,0},{2,3},{3,2},{4,5},{5,4},{6,7},{7,6},{8,9},{9,8},{10,11... | collective-permute-start | bytes 258056 | tf_op jit(solution)/shard_map/ppermute | solution.py:397
  37.3 4.8 %collective-permute-start.9 = (bf16[512,128]{1,0:T(8,128)(2,1)S(1)}, bf16[512,128]{1,0:T(8,128)(2,1)S(1)}, u32[]{:S(2)}, u32[]{:S(2)}) collective-permute-start(bf16[512,128]{1,0:T(8,128)(2,1)S(1)} %get-tuple-element.31.refs_1_), channel_id=1, source_target_pairs={{0,2},{1,3},{2,0},{3,1},{4,6},{5,7},{6,4},{7,5},{8,10},{9,11},{10,... | collective-permute-start | bytes 393224 | tf_op jit(solution)/shard_map/ppermute | solution.py:397
  38.5 11.1 %collective-permute-start.7 = (bf16[512,128]{1,0:T(8,128)(2,1)S(1)}, bf16[512,128]{1,0:T(8,128)(2,1)S(1)}, u32[]{:S(2)}, u32[]{:S(2)}) collective-permute-start(bf16[512,128]{1,0:T(8,128)(2,1)S(1)} %get-tuple-element.31.refs_1_), channel_id=1, source_target_pairs={{0,4},{1,5},{2,6},{3,7},{4,0},{5,1},{6,2},{7,3},{8,12},{9,13},{10,... | collective-permute-start | bytes 393224 | tf_op jit(solution)/shard_map/ppermute | solution.py:397
  38.7 13.2 %collective-permute-start.5 = (bf16[512,128]{1,0:T(8,128)(2,1)S(1)}, bf16[512,128]{1,0:T(8,128)(2,1)S(1)}, u32[]{:S(2)}, u32[]{:S(2)}) collective-permute-start(bf16[512,128]{1,0:T(8,128)(2,1)S(1)} %get-tuple-element.31.refs_1_), channel_id=1, source_target_pairs={{0,6},{1,7},{2,4},{3,5},{4,2},{5,3},{6,0},{7,1},{8,14},{9,15},{10,... | collective-permute-start | bytes 393224 | tf_op jit(solution)/shard_map/ppermute | solution.py:397
  42.0 11.7 %collective-permute-start.10 = (bf16[512,128]{1,0:T(8,128)(2,1)S(1)}, bf16[512,128]{1,0:T(8,128)(2,1)S(1)}, u32[]{:S(2)}, u32[]{:S(2)}) collective-permute-start(bf16[512,128]{1,0:T(8,128)(2,1)S(1)} %collective-permute-done.9.refs_1_), channel_id=1, source_target_pairs={{0,1},{1,0},{2,3},{3,2},{4,5},{5,4},{6,7},{7,6},{8,9},{9,8},{10,11... | collective-permute-start | bytes 393224 | tf_op jit(solution)/shard_map/ppermute | solution.py:397
  49.6 5.3 %collective-permute-start.8 = (bf16[512,128]{1,0:T(8,128)(2,1)S(1)}, bf16[512,128]{1,0:T(8,128)(2,1)S(1)}, u32[]{:S(2)}, u32[]{:S(2)}) collective-permute-start(bf16[512,128]{1,0:T(8,128)(2,1)S(1)} %collective-permute-done.7.refs_1_), channel_id=1, source_target_pairs={{0,1},{1,0},{2,3},{3,2},{4,5},{5,4},{6,7},{7,6},{8,9},{9,8},{10,11... | collective-permute-start | bytes 393224 | tf_op jit(solution)/shard_map/ppermute | solution.py:397
  51.9 4.2 %collective-permute-start.6 = (bf16[512,128]{1,0:T(8,128)(2,1)S(1)}, bf16[512,128]{1,0:T(8,128)(2,1)S(1)}, u32[]{:S(2)}, u32[]{:S(2)}) collective-permute-start(bf16[512,128]{1,0:T(8,128)(2,1)S(1)} %collective-permute-done.5.refs_1_), channel_id=1, source_target_pairs={{0,1},{1,0},{2,3},{3,2},{4,5},{5,4},{6,7},{7,6},{8,9},{9,8},{10,11... | collective-permute-start | bytes 393224 | tf_op jit(solution)/shard_map/ppermute | solution.py:397

commit v6 on v5

--- a/solution.py
+++ b/solution.py
@@ -10,6 +10,7 @@
 
 
 MAXOWN = 2
+STRIP = 32
 NS_STEPS = 5
 LANES = 128
 
@@ -58,10 +59,14 @@
     def visit(layer):
         for copy in copies(layer):
             copy.wait()
-        grads = grad_ref[layer].astype(F32)
-        moms = mom_ref[layer]
-        for i, prod in enumerate((grads * grads, grads * moms, moms * moms)):
-            acc[pl.ds(3 * layer + i, 1), :] = jnp.sum(prod, axis=0, keepdims=True)
+        kept = [0.0, 0.0, 0.0]
+        for first in range(0, grad_ref.shape[1], STRIP):
+            grads = grad_ref[layer, first : first + STRIP].astype(F32)
+            moms = mom_ref[layer, first : first + STRIP]
+            for i, prod in enumerate((grads * grads, grads * moms, moms * moms)):
+                kept[i] = kept[i] + (prod[: STRIP // 2] + prod[STRIP // 2 :])
+        for i in range(3):
+            acc[pl.ds(3 * layer + i, 1), :] = jnp.sum(kept[i], axis=0, keepdims=True)
 
     acc[...] = jnp.zeros_like(acc)
     over(layers, begin)
@@ -101,13 +106,17 @@
         here = (lane >= 3 * layer) & (lane < 3 * layer + 3)
         guess = jnp.maximum(jnp.sum(jnp.where(here, known, 0.0), axis=1, keepdims=True), 0.0)
         scale = 1.0 / (jnp.sqrt(guess) + 1e-07)
-        scaled = factor * grad_ref[layer].astype(F32)
-        fresh = momentum_decay * mom_ref[layer] + scaled
-        nesterov = (scaled + momentum_decay * fresh).astype(BF16).astype(F32)
-        squares = total_of(nesterov * nesterov)
-        start = (nesterov * scale).astype(BF16)
-        start_ref[layer] = start
-        width = start.shape[0]
+        width = grad_ref.shape[1]
+        kept = 0.0
+        for first in range(0, width, STRIP):
+            scaled = factor * grad_ref[layer, first : first + STRIP].astype(F32)
+            fresh = momentum_decay * mom_ref[layer, first : first + STRIP] + scaled
+            nesterov = (scaled + momentum_decay * fresh).astype(BF16).astype(F32)
+            start_ref[layer, first : first + STRIP, :] = (nesterov * scale).astype(BF16)
+            square = nesterov * nesterov
+            kept = kept + (square[: STRIP // 2] + square[STRIP // 2 :])
+        squares = total_of(kept)
+        start = start_ref[layer]
         tail = width - 2 * LANES
         a, b = LANES, 2 * LANES
         gram = pair_nt(start[0:b], start[0:b])

time: 58.1 us -> 57.7 us (level)
  no operation moved by 1% of the time
where the time goes in v6:
time: 57.7 us; the launch traced here: 57 us
  starting transfers between devices  16.4 us (28%)
  Pallas kernels  14.1 us (24%)
  blocking collectives  13.7 us (24%)
  waiting for transfers between devices  8.95 us (16%)
  other arithmetic  2.55 us (4%)
  between operations  0.71 us (1%)
    ppermute x11, starting transfers between devices, turn(): return lax.ppermute(value, 'dp', [(i, i ^ by) for i in range(owners)])  16.4 us
    all_to_all x1, blocking collectives, step(): sums = lax.all_to_all(sums, ('section', 'dp'), 0, 0, tiled=True)  13.7 us
    ppermute x11, waiting for transfers between devices, turn(): return lax.ppermute(value, 'dp', [(i, i ^ by) for i in range(owners)])  8.95 us
    pallas_call x4, Pallas kernels, step(): update, means = call(*operands)  5.39 us
    pallas_call x1, Pallas kernels, step(): pl.pallas_call(functools.partial(newton_kernel, owners, width), in_specs=...  4.88 us
    add x1, other arithmetic, step(): fresh = momentum_decay * mom_near + factor[0, 0] * grad_near.astype(F32)  2.47 us
    pallas_call x1, Pallas kernels, step(): pl.pallas_call(functools.partial(sums_kernel, layers), in_specs=[anywhere...  2.3 us
    pallas_call x1, Pallas kernels, step(): pl.pallas_call(functools.partial(start_kernel, layers, entries, owners),...  1.53 us
  transfers between devices with their start and end apart: 11, of which 5 were waited for; matrix products, arithmetic and copies ran while one was open for 5% of the time, Pallas kernels for 7%

profile of v6, /device:TPU:1, one launch (start us, length us, event | category | flops | bytes accessed | tf_op | source)
XLA Modules:
  0.0 57.0 jit_solution(7123100094138443380)
XLA Ops:
  0.6 2.3 %sums.1 = (f32[32,128]{1,0:T(8,128)S(1)}, bf16[4,288,448]{2,1,0:T(8,128)(2,1)S(1)}, f32[4,288,448]{2,1,0:T(8,128)S(1)}) custom-call(bf16[4,288,448]{2,1,0:T(8,128)(2,1)} %bitcast.36, f32[4,288,448]{2,1,0:T(8,128)} %bitcast.35), custom_call_target="tpu_custom_call" | custom-call | tf_op jit(solution)/shard_map/sums/pallas_call | solution.py:370
  2.9 13.7 %all_to_all.11 = f32[32,1,128]{2,1,0:T(1,128)S(1)} all-to-all(f32[32,1,128]{2,1,0:T(1,128)S(1)} %bitcast.32), channel_id=1, replica_groups=mesh['section'=4,'dp'=8] {'section','dp'}, dimensions={0} | all-to-all | bytes 32768 | tf_op jit(solution)/shard_map/all_to_all | solution.py:386
  16.6 1.5 %start.1 = (bf16[4,288,448]{2,1,0:T(8,128)(2,1)S(1)}, f32[4,168,128]{2,1,0:T(8,128)S(1)}, f32[4,168,128]{2,1,0:T(8,128)S(1)}, f32[8,128]{1,0:T(8,128)S(1)}) custom-call(f32[32,128]{1,0:T(8,128)S(1)} %bitcast.31, bf16[4,288,448]{2,1,0:T(8,128)(2,1)S(1)} %get-tuple-element.23.grad_ref, f32[4,288,448]{2,1,0:T(8,128)S(1)} %get-tuple-element.24.mom_ref), custom_call_target="tpu_custom_call" | custom-call | tf_op jit(solution)/shard_map/start/pallas_call | solution.py:390
  18.2 0.7 %collective-permute-start = (f32[4,168,128]{2,1,0:T(8,128)S(1)}, f32[4,168,128]{2,1,0:T(8,128)S(1)}, u32[]{:S(2)}, u32[]{:S(2)}) collective-permute-start(f32[4,168,128]{2,1,0:T(8,128)S(1)} %get-tuple-element.26), channel_id=1, source_target_pairs={{0,1},{1,0},{2,3},{3,2},{4,5},{5,4},{6,7},{7,6},{8,9},{9,8},{10,11... | collective-permute-start | bytes 1032200 | tf_op jit(solution)/shard_map/ppermute | solution.py:406
  18.8 0.5 slice.19
  19.3 0.8 %collective-permute-done = f32[4,168,128]{2,1,0:T(8,128)S(1)} collective-permute-done((f32[4,168,128]{2,1,0:T(8,128)S(1)}, f32[4,168,128]{2,1,0:T(8,128)S(1)}, u32[]{:S(2)}, u32[]{:S(2)}) %collective-permute-start) | collective-permute-done | bytes 344096 | tf_op jit(solution)/shard_map/ppermute | solution.py:406
  20.2 0.3 collective-permute-start.1
  20.5 0.3 collective-permute-start.2
  20.8 3.0 %collective-permute-start.3 = (f32[168,128]{1,0:T(8,128)S(1)}, f32[168,128]{1,0:T(8,128)S(1)}, u32[]{:S(2)}, u32[]{:S(2)}) collective-permute-start(f32[168,128]{1,0:T(8,128)S(1)} %get-tuple-element.42), channel_id=1, source_target_pairs={{0,6},{1,7},{2,4},{3,5},{4,2},{5,3},{6,0},{7,1},{8,14},{9,15},{10,... | collective-permute-start | bytes 258056 | tf_op jit(solution)/shard_map/ppermute | solution.py:406
  23.8 0.0 copy-start
  23.8 2.5 %multiply_add_fusion = f32[4,288,448]{2,1,0:T(8,128)} fusion(bf16[4,288,448]{2,1,0:T(8,128)(2,1)S(1)} %get-tuple-element.23.grad_ref, f32[4,288,448]{2,1,0:T(8,128)S(1)} %get-tuple-element.24.mom_ref, f32[]{:T(128)} %bitcast.11), kind=kLoop, calls=%fused_computation | loop fusion | flops 2064384 | bytes 5160964 | tf_op jit(solution)/shard_map/add | solution.py:412
  26.3 0.0 collective-permute-done.1
  26.3 0.0 collective-permute-done.2
  26.3 1.2 %collective-permute-done.3 = f32[168,128]{1,0:T(8,128)S(1)} collective-permute-done((f32[168,128]{1,0:T(8,128)S(1)}, f32[168,128]{1,0:T(8,128)S(1)}, u32[]{:S(2)}, u32[]{:S(2)}) %collective-permute-start.3) | collective-permute-done | bytes 86048 | tf_op jit(solution)/shard_map/ppermute | solution.py:406
  27.5 3.6 %collective-permute-start.4 = (f32[168,128]{1,0:T(8,128)S(1)}, f32[168,128]{1,0:T(8,128)S(1)}, u32[]{:S(2)}, u32[]{:S(2)}) collective-permute-start(f32[168,128]{1,0:T(8,128)S(1)} %fusion.2.own_ref), channel_id=1, source_target_pairs={{0,1},{1,0},{2,3},{3,2},{4,5},{5,4},{6,7},{7,6},{8,9},{9,8},{10,11... | collective-permute-start | bytes 258056 | tf_op jit(solution)/shard_map/ppermute | solution.py:406
  31.1 0.9 %collective-permute-done.4.other_ref = f32[168,128]{1,0:T(8,128)S(1)} collective-permute-done((f32[168,128]{1,0:T(8,128)S(1)}, f32[168,128]{1,0:T(8,128)S(1)}, u32[]{:S(2)}, u32[]{:S(2)}) %collective-permute-start.4) | collective-permute-done | bytes 86048 | tf_op jit(solution)/shard_map/ppermute | solution.py:406
  32.0 4.9 %newton.1 = (bf16[512,128]{1,0:T(8,128)(2,1)S(1)}, bf16[512,128]{1,0:T(8,128)(2,1)S(1)}) custom-call(f32[168,128]{1,0:T(8,128)S(1)} %fusion.2.own_ref, f32[168,128]{1,0:T(8,128)S(1)} %collective-permute-done.4.other_ref), custom_call_target="tpu_custom_call" | custom-call | tf_op jit(solution)/shard_map/newton/pallas_call | solution.py:418
  36.9 1.3 %collective-permute-start.9 = (bf16[512,128]{1,0:T(8,128)(2,1)S(1)}, bf16[512,128]{1,0:T(8,128)(2,1)S(1)}, u32[]{:S(2)}, u32[]{:S(2)}) collective-permute-start(bf16[512,128]{1,0:T(8,128)(2,1)S(1)} %get-tuple-element.31.refs_1_), channel_id=1, source_target_pairs={{0,2},{1,3},{2,0},{3,1},{4,6},{5,7},{6,4},{7,5},{8,10},{9,11},{10,... | collective-permute-start | bytes 393224 | tf_op jit(solution)/shard_map/ppermute | solution.py:406
  38.1 0.2 collective-permute-start.7
  38.3 2.1 %collective-permute-start.5 = (bf16[512,128]{1,0:T(8,128)(2,1)S(1)}, bf16[512,128]{1,0:T(8,128)(2,1)S(1)}, u32[]{:S(2)}, u32[]{:S(2)}) collective-permute-start(bf16[512,128]{1,0:T(8,128)(2,1)S(1)} %get-tuple-element.31.refs_1_), channel_id=1, source_target_pairs={{0,6},{1,7},{2,4},{3,5},{4,2},{5,3},{6,0},{7,1},{8,14},{9,15},{10,... | collective-permute-start | bytes 393224 | tf_op jit(solution)/shard_map/ppermute | solution.py:406
  40.5 1.2 %collective-permute-done.9.refs_1_ = bf16[512,128]{1,0:T(8,128)(2,1)S(1)} collective-permute-done((bf16[512,128]{1,0:T(8,128)(2,1)S(1)}, bf16[512,128]{1,0:T(8,128)(2,1)S(1)}, u32[]{:S(2)}, u32[]{:S(2)}) %collective-permute-start.9) | collective-permute-done | bytes 131104 | tf_op jit(solution)/shard_map/ppermute | solution.py:406
  41.6 2.7 %collective-permute-start.10 = (bf16[512,128]{1,0:T(8,128)(2,1)S(1)}, bf16[512,128]{1,0:T(8,128)(2,1)S(1)}, u32[]{:S(2)}, u32[]{:S(2)}) collective-permute-start(bf16[512,128]{1,0:T(8,128)(2,1)S(1)} %collective-permute-done.9.refs_1_), channel_id=1, source_target_pairs={{0,1},{1,0},{2,3},{3,2},{4,5},{5,4},{6,7},{7,6},{8,9},{9,8},{10,11... | collective-permute-start | bytes 393224 | tf_op jit(solution)/shard_map/ppermute | solution.py:406
  44.3 4.9 %collective-permute-done.7.refs_1_ = bf16[512,128]{1,0:T(8,128)(2,1)S(1)} collective-permute-done((bf16[512,128]{1,0:T(8,128)(2,1)S(1)}, bf16[512,128]{1,0:T(8,128)(2,1)S(1)}, u32[]{:S(2)}, u32[]{:S(2)}) %collective-permute-start.7) | collective-permute-done | bytes 131104 | tf_op jit(solution)/shard_map/ppermute | solution.py:406
  49.2 2.3 %collective-permute-start.8 = (bf16[512,128]{1,0:T(8,128)(2,1)S(1)}, bf16[512,128]{1,0:T(8,128)(2,1)S(1)}, u32[]{:S(2)}, u32[]{:S(2)}) collective-permute-start(bf16[512,128]{1,0:T(8,128)(2,1)S(1)} %collective-permute-done.7.refs_1_), channel_id=1, source_target_pairs={{0,1},{1,0},{2,3},{3,2},{4,5},{5,4},{6,7},{7,6},{8,9},{9,8},{10,11... | collective-permute-start | bytes 393224 | tf_op jit(solution)/shard_map/ppermute | solution.py:406
  51.5 0.0 collective-permute-done.5.refs_1_
  51.5 0.0 collective-permute-start.6
  51.5 0.0 copy-done
  51.5 1.7 %update.4 = (bf16[4,288,448]{2,1,0:T(8,128)(2,1)}, f32[8,128]{1,0:T(8,128)S(1)}) custom-call(bf16[4,288,448]{2,1,0:T(8,128)(2,1)S(1)} %get-tuple-element.29.refs_0_, bf16[512,128]{1,0:T(8,128)(2,1)S(1)} %get-tuple-element.31.refs_1_, bf16[512,128]{1,0:T(8,128)(2,1)S(1)} %get-tuple-element.32.refs_2_, s32[1,4]{1,0:T(1,128)S(1)} %copy-done), custom_call_target="tpu_custom_call" | custom-call | flops 148635648 | bytes 778240 | tf_op jit(solution)/shard_map/update/pallas_call | solution.py:472
  53.3 0.0 collective-permute-done.10.refs_2_
  53.3 1.2 %update.5 = (bf16[4,288,448]{2,1,0:T(8,128)(2,1)}, f32[8,128]{1,0:T(8,128)S(1)}) custom-call(bf16[4,288,448]{2,1,0:T(8,128)(2,1)S(1)} %get-tuple-element.29.refs_0_, bf16[512,128]{1,0:T(8,128)(2,1)S(1)} %collective-permute-done.9.refs_1_, bf16[512,128]{1,0:T(8,128)(2,1)S(1)} %collective-permute-done.10.refs_2_, ...), custom_call_target="tpu_custom_call", output_to_operand_aliasing={{0}: (4, {})} | custom-call | flops 148635648 | bytes 778240 | tf_op jit(solution)/shard_map/update/pallas_call | solution.py:472
  54.5 0.0 collective-permute-done.8.refs_2_
  54.5 1.2 %update.6 = (bf16[4,288,448]{2,1,0:T(8,128)(2,1)}, f32[8,128]{1,0:T(8,128)S(1)}) custom-call(bf16[4,288,448]{2,1,0:T(8,128)(2,1)S(1)} %get-tuple-element.29.refs_0_, bf16[512,128]{1,0:T(8,128)(2,1)S(1)} %collective-permute-done.7.refs_1_, bf16[512,128]{1,0:T(8,128)(2,1)S(1)} %collective-permute-done.8.refs_2_, ...), custom_call_target="tpu_custom_call", output_to_operand_aliasing={{0}: (4, {})} | custom-call | flops 148635648 | bytes 778240 | tf_op jit(solution)/shard_map/update/pallas_call | solution.py:472
  55.7 0.0 collective-permute-done.6.refs_2_
  55.8 1.2 %update.7 = (bf16[4,288,448]{2,1,0:T(8,128)(2,1)}, f32[1,2]{1,0:T(1,128)}) custom-call(bf16[4,288,448]{2,1,0:T(8,128)(2,1)S(1)} %get-tuple-element.29.refs_0_, bf16[512,128]{1,0:T(8,128)(2,1)S(1)} %collective-permute-done.5.refs_1_, bf16[512,128]{1,0:T(8,128)(2,1)S(1)} %collective-permute-done.6.refs_2_, ...), custom_call_target="tpu_custom_call", output_to_operand_aliasing={{0}: (4, {})} | custom-call | flops 148635648 | bytes 778240 | tf_op jit(solution)/shard_map/update/pallas_call | solution.py:472
  (3 shorter events, 0.1 us)
Async XLA Ops:
  18.2 1.9 %collective-permute-start = (f32[4,168,128]{2,1,0:T(8,128)S(1)}, f32[4,168,128]{2,1,0:T(8,128)S(1)}, u32[]{:S(2)}, u32[]{:S(2)}) collective-permute-start(f32[4,168,128]{2,1,0:T(8,128)S(1)} %get-tuple-element.26), channel_id=1, source_target_pairs={{0,1},{1,0},{2,3},{3,2},{4,5},{5,4},{6,7},{7,6},{8,9},{9,8},{10,11... | collective-permute-start | bytes 1032200 | tf_op jit(solution)/shard_map/ppermute | solution.py:406
  20.2 6.1 %collective-permute-start.1 = (f32[168,128]{1,0:T(8,128)S(1)}, f32[168,128]{1,0:T(8,128)S(1)}, u32[]{:S(2)}, u32[]{:S(2)}) collective-permute-start(f32[168,128]{1,0:T(8,128)S(1)} %get-tuple-element.41), channel_id=1, source_target_pairs={{0,2},{1,3},{2,0},{3,1},{4,6},{5,7},{6,4},{7,5},{8,10},{9,11},{10,... | collective-permute-start | bytes 258056 | tf_op jit(solution)/shard_map/ppermute | solution.py:406
  20.5 5.8 %collective-permute-start.2 = (f32[168,128]{1,0:T(8,128)S(1)}, f32[168,128]{1,0:T(8,128)S(1)}, u32[]{:S(2)}, u32[]{:S(2)}) collective-permute-start(f32[168,128]{1,0:T(8,128)S(1)} %get-tuple-element.43), channel_id=1, source_target_pairs={{0,4},{1,5},{2,6},{3,7},{4,0},{5,1},{6,2},{7,3},{8,12},{9,13},{10,... | collective-permute-start | bytes 258056 | tf_op jit(solution)/shard_map/ppermute | solution.py:406
  20.8 6.6 %collective-permute-start.3 = (f32[168,128]{1,0:T(8,128)S(1)}, f32[168,128]{1,0:T(8,128)S(1)}, u32[]{:S(2)}, u32[]{:S(2)}) collective-permute-start(f32[168,128]{1,0:T(8,128)S(1)} %get-tuple-element.42), channel_id=1, source_target_pairs={{0,6},{1,7},{2,4},{3,5},{4,2},{5,3},{6,0},{7,1},{8,14},{9,15},{10,... | collective-permute-start | bytes 258056 | tf_op jit(solution)/shard_map/ppermute | solution.py:406
  23.8 27.7 %copy-start = (s32[1,4]{1,0:T(1,128)S(1)}, s32[1,4]{1,0:T(1,128)}, u32[]{:S(2)}) copy-start(s32[1,4]{1,0:T(1,128)} %refs_3_.1) | copy-start | bytes 52
  27.5 4.5 %collective-permute-start.4 = (f32[168,128]{1,0:T(8,128)S(1)}, f32[168,128]{1,0:T(8,128)S(1)}, u32[]{:S(2)}, u32[]{:S(2)}) collective-permute-start(f32[168,128]{1,0:T(8,128)S(1)} %fusion.2.own_ref), channel_id=1, source_target_pairs={{0,1},{1,0},{2,3},{3,2},{4,5},{5,4},{6,7},{7,6},{8,9},{9,8},{10,11... | collective-permute-start | bytes 258056 | tf_op jit(solution)/shard_map/ppermute | solution.py:406
  36.9 4.8 %collective-permute-start.9 = (bf16[512,128]{1,0:T(8,128)(2,1)S(1)}, bf16[512,128]{1,0:T(8,128)(2,1)S(1)}, u32[]{:S(2)}, u32[]{:S(2)}) collective-permute-start(bf16[512,128]{1,0:T(8,128)(2,1)S(1)} %get-tuple-element.31.refs_1_), channel_id=1, source_target_pairs={{0,2},{1,3},{2,0},{3,1},{4,6},{5,7},{6,4},{7,5},{8,10},{9,11},{10,... | collective-permute-start | bytes 393224 | tf_op jit(solution)/shard_map/ppermute | solution.py:406
  38.1 11.1 %collective-permute-start.7 = (bf16[512,128]{1,0:T(8,128)(2,1)S(1)}, bf16[512,128]{1,0:T(8,128)(2,1)S(1)}, u32[]{:S(2)}, u32[]{:S(2)}) collective-permute-start(bf16[512,128]{1,0:T(8,128)(2,1)S(1)} %get-tuple-element.31.refs_1_), channel_id=1, source_target_pairs={{0,4},{1,5},{2,6},{3,7},{4,0},{5,1},{6,2},{7,3},{8,12},{9,13},{10,... | collective-permute-start | bytes 393224 | tf_op jit(solution)/shard_map/ppermute | solution.py:406
  38.3 13.2 %collective-permute-start.5 = (bf16[512,128]{1,0:T(8,128)(2,1)S(1)}, bf16[512,128]{1,0:T(8,128)(2,1)S(1)}, u32[]{:S(2)}, u32[]{:S(2)}) collective-permute-start(bf16[512,128]{1,0:T(8,128)(2,1)S(1)} %get-tuple-element.31.refs_1_), channel_id=1, source_target_pairs={{0,6},{1,7},{2,4},{3,5},{4,2},{5,3},{6,0},{7,1},{8,14},{9,15},{10,... | collective-permute-start | bytes 393224 | tf_op jit(solution)/shard_map/ppermute | solution.py:406
  41.6 11.7 %collective-permute-start.10 = (bf16[512,128]{1,0:T(8,128)(2,1)S(1)}, bf16[512,128]{1,0:T(8,128)(2,1)S(1)}, u32[]{:S(2)}, u32[]{:S(2)}) collective-permute-start(bf16[512,128]{1,0:T(8,128)(2,1)S(1)} %collective-permute-done.9.refs_1_), channel_id=1, source_target_pairs={{0,1},{1,0},{2,3},{3,2},{4,5},{5,4},{6,7},{7,6},{8,9},{9,8},{10,11... | collective-permute-start | bytes 393224 | tf_op jit(solution)/shard_map/ppermute | solution.py:406
  49.2 5.3 %collective-permute-start.8 = (bf16[512,128]{1,0:T(8,128)(2,1)S(1)}, bf16[512,128]{1,0:T(8,128)(2,1)S(1)}, u32[]{:S(2)}, u32[]{:S(2)}) collective-permute-start(bf16[512,128]{1,0:T(8,128)(2,1)S(1)} %collective-permute-done.7.refs_1_), channel_id=1, source_target_pairs={{0,1},{1,0},{2,3},{3,2},{4,5},{5,4},{6,7},{7,6},{8,9},{9,8},{10,11... | collective-permute-start | bytes 393224 | tf_op jit(solution)/shard_map/ppermute | solution.py:406
  51.5 4.2 %collective-permute-start.6 = (bf16[512,128]{1,0:T(8,128)(2,1)S(1)}, bf16[512,128]{1,0:T(8,128)(2,1)S(1)}, u32[]{:S(2)}, u32[]{:S(2)}) collective-permute-start(bf16[512,128]{1,0:T(8,128)(2,1)S(1)} %collective-permute-done.5.refs_1_), channel_id=1, source_target_pairs={{0,1},{1,0},{2,3},{3,2},{4,5},{5,4},{6,7},{7,6},{8,9},{9,8},{10,11... | collective-permute-start | bytes 393224 | tf_op jit(solution)/shard_map/ppermute | solution.py:406
